TPU v7x, 32 devices: a whole 2x2x4 slice. The times are simulated.
32 devices in a mesh: dp: 8 (over y, x, core), sp: 4 (over z).
Axes of the slice: x: 2, y: 2, z: 4, core: 2. Of those that a mesh axis runs over, the one named last changes fastest.
Arguments:
- tokens: bfloat16 [8192, 2048], P(('dp', 'sp')), may hold values from -6 to 6
- lengths: int32 [8], P('dp'), may hold values from 64 to 1024, as said below
- cotangent: bfloat16 [8192, 2048], P(('dp', 'sp')), may hold values from -6 to 6
- ln_gains: bfloat16 [2, 2048], replicated, may hold values from 0.099609375 to 1.8984375
- ln_shifts: bfloat16 [2, 2048], replicated, may hold values from -1.5 to 1.5
- qkv_weight: bfloat16 [2048, 6144], P(('dp', 'sp')), may hold values from -0.125 to 0.125
- qkv_bias: bfloat16 [3, 2048], replicated, may hold values from -0.25 to 0.25
- out_weight: bfloat16 [2048, 2048], P(('dp', 'sp')), may hold values from -1 to 1
- up_weight: bfloat16 [8192, 2048], P(('dp', 'sp')), may hold values from -0.125 to 0.125
- up_bias: bfloat16 [8192], replicated, may hold values from -1.5 to 1.5
- down_weight: bfloat16 [8192, 2048], P(('dp', 'sp')), may hold values from -0.0625 to 0.0625
- out_bias: bfloat16 [2048], replicated, may hold values from -1.5 to 1.5
Outputs:
- output: bfloat16 [8192, 2048], P(('dp', 'sp'))
- input_grad: bfloat16 [8192, 2048], P(('dp', 'sp'))
- ln_gains_grad: float32 [2, 2048], replicated
- ln_shifts_grad: float32 [2, 2048], replicated
- qkv_weight_grad: float32 [2048, 6144], P(('dp', 'sp'))
- qkv_bias_grad: float32 [3, 2048], replicated
- out_weight_grad: float32 [2048, 2048], P(('dp', 'sp'))
- up_weight_grad: float32 [8192, 2048], P(('dp', 'sp'))
- up_bias_grad: float32 [8192], replicated
- down_weight_grad: float32 [8192, 2048], P(('dp', 'sp'))
- out_bias_grad: float32 [2048], replicated
Inputs may be any that keep to these rules, and one draw needn't show every extreme that they name: `lengths`: a sequence's valid tokens fill the front of its 1024 rows; the first sequence is always full.
All inputs are finite; a program needn't handle non-finite values.
Results may differ from a plain program's by a relative error of at most 0.011.
Values may be sent and summed in bfloat16 or wider, within the bound.
A program may use at most 768 MiB of HBM per device.

v0:
```python
import functools

import jax
import jax.numpy as jnp
from jax import lax
from jax.experimental import pallas as pl
from jax.experimental.pallas import tpu as pltpu
from jax.sharding import PartitionSpec as P

D = 2048
HEADS = 8
HEAD = 256
ROT = 64


eps = 1e-05
base_freq = 10000.0
root_half = 0.7071067811865476
inv_root_two_pi = 0.3989422804014327


def contract_rows(left, right):
    return lax.dot_general(
        left, right, (((0,), (0,)), ((), ())), preferred_element_type=jnp.float32
    )


def contract_cols(left, right):
    return lax.dot_general(
        left, right, (((1,), (1,)), ((), ())), preferred_element_type=jnp.float32
    )


def gelu_value(pre_act):
    return 0.5 * pre_act * (1.0 + lax.erf(pre_act * root_half))


def gelu_slope(pre_act):
    return 0.5 * (1.0 + lax.erf(pre_act * root_half)) + pre_act * inv_root_two_pi * jnp.exp(
        -0.5 * pre_act * pre_act
    )


BAND=256
def turn(x, cos_t, sin_t):
    first = x[:, :128]
    lane = lax.broadcasted_iota(jnp.int32, first.shape, 1)
    partner = jnp.where(lane < ROT // 2, pltpu.roll(first, 128 - ROT // 2, 1), pltpu.roll(first, ROT // 2, 1))
    return jnp.concatenate([first * cos_t + partner * sin_t, x[:, 128:]], axis=1)

def weights_of(q, k, start, length, scale):
    rows, cols = q.shape[0], k.shape[0]
    s = lax.dot_general(q, k, (((1,), (1,)), ((), ())), preferred_element_type=jnp.float32) * scale
    key = lax.broadcasted_iota(jnp.int32, (rows, cols), 1)
    query = start + lax.broadcasted_iota(jnp.int32, (rows, cols), 0)
    s = jnp.where((key <= query) & (key < length), s, -1e30)
    e = jnp.exp(s - jnp.max(s, axis=-1, keepdims=True))
    return e / jnp.sum(e, axis=-1, keepdims=True)

def fwd_kernel(scale, len_ref, pq, pk, pv, bq, bk, bv, cos_ref, sin_ref, q_ref, k_ref, v_ref, ctx_ref):
    length = len_ref[0]
    seq = pq.shape[0]
    cos_t, sin_t = cos_ref[...], sin_ref[...]
    q_ref[...] = turn(pq[...] + bq[...], cos_t, sin_t).astype(jnp.bfloat16)
    k_ref[...] = turn(pk[...] + bk[...], cos_t, sin_t).astype(jnp.bfloat16)
    v_ref[...] = (pv[...] + bv[...]).astype(jnp.bfloat16)
    for start in range(0, seq, BAND):
        end = start + BAND
        p = weights_of(q_ref[start:end, :], k_ref[:end, :], start, length, scale)
        ctx_ref[start:end, :] = jnp.dot(p.astype(jnp.bfloat16), v_ref[:end, :], preferred_element_type=jnp.float32).astype(jnp.bfloat16)

def attend_fwd(projected, bias, cos_t, sin_t, lengths):
    seq, width = projected.shape
    heads = width // 3 // HEAD
    col = lambda g: pl.BlockSpec((seq, HEAD), lambda h, *_, g=g: (0, g * heads + h))
    bcol = lambda g: pl.BlockSpec((1, HEAD), lambda h, *_, g=g: (0, g * heads + h))
    tab = pl.BlockSpec((seq, 128), lambda h, *_: (0, 0))
    out = pl.BlockSpec((seq, HEAD), lambda h, *_: (0, h))
    return pl.pallas_call(
        functools.partial(fwd_kernel, HEAD ** -0.5),
        grid_spec=pltpu.PrefetchScalarGridSpec(num_scalar_prefetch=1, grid=(heads,),
            in_specs=[col(0), col(1), col(2), bcol(0), bcol(1), bcol(2), tab, tab], out_specs=[out] * 4),
        out_shape=[jax.ShapeDtypeStruct((seq, heads * HEAD), jnp.bfloat16)] * 4,
        name="attend_fwd",
        cost_estimate=pl.CostEstimate(flops=heads * seq * seq * HEAD * 4, bytes_accessed=seq * width * 8, transcendentals=heads * seq * seq),
    )(lengths, projected, projected, projected, bias, bias, bias, cos_t, sin_t)

def bwd_kernel(scale, heads, len_ref, q_ref, k_ref, v_ref, g_ref, cos_ref, sin_ref, gp_ref, sum_ref, dk, dv, dq):
    length = len_ref[0]
    h = pl.program_id(0)
    seq = q_ref.shape[0]
    dk[...] = jnp.zeros_like(dk)
    dv[...] = jnp.zeros_like(dv)
    for start in range(0, seq, BAND):
        end = start + BAND
        q, g = q_ref[start:end, :], g_ref[start:end, :]
        k, v = k_ref[:end, :], v_ref[:end, :]
        p = weights_of(q, k, start, length, scale)
        gp = lax.dot_general(g, v, (((1,), (1,)), ((), ())), preferred_element_type=jnp.float32)
        ds = (p * (gp - jnp.sum(p * gp, axis=-1, keepdims=True))).astype(jnp.bfloat16)
        dq[start:end, :] = jnp.dot(ds, k, preferred_element_type=jnp.float32) * scale
        dk[:end, :] += lax.dot_general(ds, q, (((0,), (0,)), ((), ())), preferred_element_type=jnp.float32)
        dv[:end, :] += lax.dot_general(p.astype(jnp.bfloat16), g, (((0,), (0,)), ((), ())), preferred_element_type=jnp.float32)
    cos_t, sin_t = cos_ref[...], sin_ref[...]
    def back(x):
        return turn(x.astype(jnp.bfloat16).astype(jnp.float32), cos_t, -sin_t).astype(jnp.bfloat16)
    for g, piece in enumerate((back(dq[...]), back(dk[...] * scale), dv[...].astype(jnp.bfloat16))):
        at = pl.ds(pl.multiple_of((g * heads + h) * HEAD, HEAD), HEAD)
        gp_ref[:, at] = piece
        sum_ref[:, at] = jnp.sum(piece.astype(jnp.float32), axis=0, keepdims=True)

def attend_bwd(q, k, v, gctx, cos_t, sin_t, lengths):
    seq, width = q.shape
    heads = width // HEAD
    col = pl.BlockSpec((seq, HEAD), lambda h, *_: (0, h))
    tab = pl.BlockSpec((seq, 128), lambda h, *_: (0, 0))
    return pl.pallas_call(
        functools.partial(bwd_kernel, HEAD ** -0.5, heads),
        grid_spec=pltpu.PrefetchScalarGridSpec(num_scalar_prefetch=1, grid=(heads,),
            in_specs=[col] * 4 + [tab, tab],
            out_specs=[pl.BlockSpec((seq, 3 * width), lambda h, *_: (0, 0)), pl.BlockSpec((1, 3 * width), lambda h, *_: (0, 0))],
            scratch_shapes=[pltpu.VMEM((seq, HEAD), jnp.float32)] * 3),
        out_shape=[jax.ShapeDtypeStruct((seq, 3 * width), jnp.bfloat16), jax.ShapeDtypeStruct((1, 3 * width), jnp.float32)],
        name="attend_bwd",
        cost_estimate=pl.CostEstimate(flops=heads * seq * seq * HEAD * 10, bytes_accessed=seq * width * 20, transcendentals=heads * seq * seq),
    )(lengths, q, k, v, gctx, cos_t, sin_t)

def rotary_rows(seq):
    half = ROT // 2
    freq = 10000.0 ** (-jnp.arange(half, dtype=jnp.float32) * (2.0 / ROT))
    ang = jnp.arange(seq, dtype=jnp.int32).astype(jnp.float32)[:, None] * freq[None, :]
    c, s = jnp.cos(ang), jnp.sin(ang)
    rest = 128 - ROT
    return (jnp.concatenate([c, c, jnp.ones((seq, rest), jnp.float32)], 1), jnp.concatenate([-s, s, jnp.zeros((seq, rest), jnp.float32)], 1))

MESH = pl.DeviceIdType.MESH

def square_partners(dp):
    core, x, y = dp % 2, (dp // 2) % 2, dp // 4
    across_x, across_y = dp + 2 - 4 * x, dp + 4 - 8 * y
    first = across_x * (1 - core) + across_y * core
    second = across_y * (1 - core) + across_x * core
    return first, second, across_x + across_y - dp, 1 - 2 * core

class Hops:
    def __init__(self, count, dp, sp, source, result, send, recv):
        self.count, self.dp, self.sp, self.source, self.result = count, dp, sp, source, result
        self.send, self.recv, self.rows = send, recv, source.shape[0]

    def place(self, owner):
        return pl.ds(pl.multiple_of(owner * self.rows, self.rows), self.rows)

    def copy(self, way, step, owner, own):
        to = lax.rem(self.sp + (1 if way == 0 else self.count - 1), self.count)
        at = self.result.at[self.place(owner)]
        return pltpu.make_async_remote_copy(
            src_ref=self.source if own else at, dst_ref=at, send_sem=self.send.at[way, step],
            recv_sem=self.recv.at[way, step], device_id=(self.dp, to), device_id_type=MESH)

    def sends(self, way, step):
        if way == 0:
            return (self.sp >= step) & (self.sp < self.count - 1)
        return (self.sp < self.count - step) & (self.sp > 0)

    def receives(self, way, step):
        return self.sp >= step + 1 if way == 0 else self.sp < self.count - step - 1

    def owner(self, way, step):
        return self.sp - step if way == 0 else self.sp + step

    def start(self, way, step):
        @pl.when(self.sends(way, step))
        def _():
            self.copy(way, step, self.owner(way, step), step == 0).start()

    def begin(self):
        for way in (0, 1):
            self.start(way, 0)

    def forward(self, step):
        for way in (0, 1):
            @pl.when(self.receives(way, step - 1))
            def _():
                self.copy(way, step - 1, self.owner(way, step), False).wait_recv()
            if step < self.count - 1:
                self.start(way, step)

    def finish(self):
        for step in range(self.count - 1):
            for way in (0, 1):
                @pl.when(self.sends(way, step))
                def _():
                    self.copy(way, step, self.owner(way, step), step == 0).wait_send()


def gather_kernel(sp_size, qkv_ref, out_ref, up_ref, tok_ref, freq_ref, qkv_all, out_all, up_all, tok_all,
                  cos_ref, sin_ref,
                  send_sem, recv_sem, slab_send, slab_recv, local_sem, turn_send, turn_recv, hop_send, hop_recv):
    dp, sp = lax.axis_index("dp"), lax.axis_index("sp")
    first, second, diagonal, flip = square_partners(dp)
    sibling = dp + flip
    per = 2
    pair, lane = dp // per, dp % per
    rows = qkv_ref.shape[0]
    wide = up_ref.shape[1]
    head_width = wide // sp_size
    turn_dp = sp * per + lane

    barrier = pltpu.get_barrier_semaphore()
    for other in (first, second, sibling):
        pl.semaphore_signal(barrier, inc=1, device_id=(other, sp), device_id_type=MESH)
    for step in range(1, sp_size):
        pl.semaphore_signal(barrier, inc=1, device_id=(dp, lax.rem(sp + step, sp_size)), device_id_type=MESH)
    @pl.when(pair != sp)
    def _():
        pl.semaphore_signal(barrier, inc=1, device_id=(turn_dp, pair), device_id_type=MESH)

    pl.semaphore_wait(barrier, 2 + sp_size + jnp.where(pair != sp, 1, 0))

    def slab_at(owner_sp):
        return pl.ds(pl.multiple_of((dp * sp_size + owner_sp) * rows, rows), rows)

    def slab_copy(step, part):
        there = lax.rem(sp + step, sp_size)
        return pltpu.make_async_remote_copy(
            src_ref=qkv_ref.at[:, pl.ds(pl.multiple_of(part * wide + there * head_width, head_width), head_width)],
            dst_ref=qkv_all.at[slab_at(sp), pl.ds(part * head_width, head_width)],
            send_sem=slab_send.at[step - 1, part], recv_sem=slab_recv.at[step - 1, part],
            device_id=(dp, there), device_id_type=MESH)

    def slab_arrival(step, part):
        origin = lax.rem(sp + sp_size - step, sp_size)
        return pltpu.make_async_remote_copy(
            src_ref=qkv_ref.at[:, pl.ds(part * head_width, head_width)],
            dst_ref=qkv_all.at[slab_at(origin), pl.ds(part * head_width, head_width)],
            send_sem=slab_send.at[step - 1, part], recv_sem=slab_recv.at[step - 1, part],
            device_id=(dp, origin), device_id_type=MESH)

    units = up_ref.shape[0]
    slab = rows * sp_size

    def plain(height):
        return lambda owner: pl.ds(pl.multiple_of(owner * height, height), height)

    def turned(owner):
        return pl.ds(pl.multiple_of((owner % per) * slab + (owner // per) * rows, rows), rows)

    arrays = ((up_ref, up_all, plain(units)), (None, qkv_all, plain(slab)), (None, out_all, turned))
    hops = Hops(sp_size, dp, sp, tok_ref, tok_all, hop_send, hop_recv)

    def copy(index, message, block, target):
        source, result, place = arrays[index]
        at = result.at[place(block)]
        src = at
        if source is not None and message < 3:
            src = source
        return pltpu.make_async_remote_copy(
            src_ref=src, dst_ref=at, send_sem=send_sem.at[index, message], recv_sem=recv_sem.at[index, message],
            device_id=(target, sp), device_id_type=MESH)

    sends = ((dp, first), (dp, second), (dp, sibling), (first, second), (first, sibling), (second, sibling), (diagonal, sibling))
    arrivals = (first, second, sibling, diagonal, second + flip, first + flip, diagonal + flip)

    def start(index, message):
        copy(index, message, *sends[message]).start()

    def arrived(index, message):
        copy(index, message, arrivals[message], dp).wait_recv()

    def own(index):
        for message in (0, 1, 2):
            start(index, message)

    def keep(source, target, which):
        return pltpu.make_async_copy(source, target, local_sem.at[which])

    hops.begin()
    own(0)
    for step in range(1, sp_size):
        for part in range(3):
            slab_copy(step, part).start()

    out_place = out_all.at[turned(turn_dp)]
    my_out_place = out_all.at[turned(dp)]
    turn = pltpu.make_async_remote_copy(
        src_ref=out_ref, dst_ref=out_place, send_sem=turn_send, recv_sem=turn_recv,
        device_id=(turn_dp, pair), device_id_type=MESH)
    turn_arrival = pltpu.make_async_remote_copy(
        src_ref=out_ref, dst_ref=my_out_place, send_sem=turn_send, recv_sem=turn_recv,
        device_id=(turn_dp, pair), device_id_type=MESH)

    @pl.when(pair != sp)
    def _():
        turn.start()

    local = [keep(tok_ref, tok_all.at[hops.place(sp)], 0), keep(up_ref, up_all.at[plain(units)(dp)], 1)]
    for part in range(3):
        local.append(keep(
            qkv_ref.at[:, pl.ds(pl.multiple_of(part * wide + sp * head_width, head_width), head_width)],
            qkv_all.at[slab_at(sp), pl.ds(part * head_width, head_width)], 2 + part))
    for c in local:
        c.start()

    def onward(index):
        arrived(index, 0)
        start(index, 3)
        start(index, 4)
        arrived(index, 1)
        start(index, 5)

    def table(i, carry):
        at = pl.ds(pl.multiple_of(i * 64, 64), 64)
        lane = lax.broadcasted_iota(jnp.int32, (64, 128), 1)
        position = i * 64 + lax.broadcasted_iota(jnp.int32, (64, 128), 0)
        angle = position.astype(jnp.float32) * freq_ref[...]
        turned_lane = lane < ROT
        cos_ref[at, :] = jnp.where(turned_lane, jnp.cos(angle), 1.0)
        sine = jnp.sin(angle)
        sin_ref[at, :] = jnp.where(turned_lane, jnp.where(lane < ROT // 2, -sine, sine), 0.0)
        return carry

    onward(0)
    hops.forward(1)
    lax.fori_loop(0, cos_ref.shape[0] // 64, table, 0)

    @pl.when(pair == sp)
    def _():
        c = keep(out_ref, my_out_place, 5)
        c.start()
        c.wait()

    @pl.when(pair != sp)
    def _():
        turn_arrival.wait_recv()

    own(2)
    for step in range(1, sp_size):
        for part in range(3):
            slab_arrival(step, part).wait_recv()
    for c in local:
        c.wait()
    own(1)
    arrived(0, 3)
    start(0, 6)
    onward(2)
    hops.forward(2)
    onward(1)
    for index in (2, 1):
        arrived(index, 3)
        start(index, 6)
    hops.forward(3)
    for index in range(3):
        for message in (2, 4, 5, 6):
            arrived(index, message)
    for index in range(3):
        for message in range(7):
            copy(index, message, *sends[message]).wait_send()
    for step in range(1, sp_size):
        for part in range(3):
            slab_copy(step, part).wait_send()

    @pl.when(pair != sp)
    def _():
        turn.wait_send()

    hops.finish()

def gather_weights(dp_size, sp_size, qkv_weight, out_weight, up_weight, tokens):
    rows, wide = out_weight.shape
    units = up_weight.shape[0]
    seq = tokens.shape[0] * sp_size
    low = jnp.bfloat16
    half = ROT // 2
    freq = base_freq ** (-jnp.arange(half, dtype=jnp.float32) * (2.0 / ROT))
    freq = jnp.concatenate([freq, freq, jnp.zeros((128 - ROT,), jnp.float32)])[None]
    hbm = pl.BlockSpec(memory_space=pltpu.HBM)
    vmem = pl.BlockSpec(memory_space=pltpu.VMEM)
    dma = pltpu.SemaphoreType.DMA
    shape = jax.ShapeDtypeStruct
    return pl.pallas_call(
        functools.partial(gather_kernel, sp_size),
        out_shape=[shape((rows * sp_size * dp_size, 3 * wide // sp_size), low),
                   shape((rows * dp_size, wide), low),
                   shape((units * dp_size, wide), low),
                   shape((seq, wide), low),
                   shape((seq, 128), jnp.float32), shape((seq, 128), jnp.float32)],
        in_specs=[vmem] * 5, out_specs=[hbm] * 4 + [vmem] * 2,
        scratch_shapes=[dma((3, 7)), dma((3, 7)), dma((sp_size - 1, 3)), dma((sp_size - 1, 3)), dma((6,)), dma, dma,
                        dma((2, sp_size)), dma((2, sp_size))],
        compiler_params=pltpu.CompilerParams(collective_id=0, has_side_effects=True),
        cost_estimate=pl.CostEstimate(flops=0, bytes_accessed=250 * 1000 * 1000, transcendentals=0),
        name="gather_weights",
    )(qkv_weight, out_weight, up_weight, tokens, freq)

def front_kernel(sp_size, len_ref, tok_hbm, qkv_hbm, up_hbm, out_hbm, down_ref, cot_ref, gain_ref, shift_ref, qkv_bias_ref, unit_bias_ref,
                 cos_ref, sin_ref,
                 down_all, cot_all, attn_out, mlp_out, hidden_out, pre_out, part_out, q_ref, k_ref, v_ref, ctx_ref,
                 tok, attn, mlp, qkv_w, up_w, hidden, pre,
                 send_sem, recv_sem, load_sem, store_sem, pre_sem, keep_sem, part_sem, hop_send, hop_recv):
    full, low = jnp.float32, jnp.bfloat16
    dp, sp = lax.axis_index("dp"), lax.axis_index("sp")
    first, second, diagonal, flip = square_partners(dp)
    sibling = dp + flip
    seq, wide = tok.shape
    units = down_ref.shape[0]
    width = q_ref.shape[1]
    scale = HEAD ** -0.5
    band = 256

    def load(source, target, which):
        return pltpu.make_async_copy(source, target, load_sem.at[which])

    token_loads = [load(tok_hbm.at[pl.ds(r, band)], tok.at[pl.ds(r, band)], r // band) for r in range(0, seq, band)]
    loads = token_loads + [load(qkv_hbm, qkv_w, seq // band), load(up_hbm, up_w, seq // band + 1)]
    for c in loads:
        c.start()

    barrier = pltpu.get_barrier_semaphore()
    for other in (first, second, sibling):
        pl.semaphore_signal(barrier, inc=1, device_id=(other, sp), device_id_type=MESH)
    for step in range(1, sp_size):
        pl.semaphore_signal(barrier, inc=1, device_id=(dp, lax.rem(sp + step, sp_size)), device_id_type=MESH)
    pl.semaphore_wait(barrier, 2 + sp_size)

    sends = ((dp, first), (dp, second), (dp, sibling), (first, second), (first, sibling), (second, sibling), (diagonal, sibling))
    arrivals = (first, second, sibling, diagonal, second + flip, first + flip, diagonal + flip)

    def copy(message, block, target):
        at = down_all.at[pl.ds(pl.multiple_of(block * units, units), units)]
        return pltpu.make_async_remote_copy(
            src_ref=down_ref if message < 3 else at, dst_ref=at,
            send_sem=send_sem.at[message], recv_sem=recv_sem.at[message],
            device_id=(target, sp), device_id_type=MESH)

    def start(message):
        copy(message, *sends[message]).start()

    def arrived(message):
        copy(message, arrivals[message], sibling).wait_recv()

    hops = Hops(sp_size, dp, sp, cot_ref, cot_all, hop_send, hop_recv)
    hops.begin()
    for message in (0, 1, 2):
        start(message)
    keeps = [pltpu.make_async_copy(down_ref, down_all.at[pl.ds(pl.multiple_of(dp * units, units), units)], keep_sem.at[0]),
             pltpu.make_async_copy(cot_ref, cot_all.at[hops.place(sp)], keep_sem.at[1])]
    for c in keeps:
        c.start()

    def normalize(i, carry):
        at = pl.ds(pl.multiple_of(i * 32, 32), 32)
        rows = tok[at, :].astype(full)
        centered = rows - jnp.mean(rows, axis=-1, keepdims=True)
        normed = centered * lax.rsqrt(jnp.mean(centered * centered, axis=-1, keepdims=True) + eps)
        attn[at, :] = (normed * gain_ref[0:1, :] + shift_ref[0:1, :]).astype(low)
        mlp[at, :] = (normed * gain_ref[1:2, :] + shift_ref[1:2, :]).astype(low)
        return carry

    for part, c in enumerate(token_loads):
        c.wait()
        lax.fori_loop(part * band // 32, (part + 1) * band // 32, normalize, 0)
    stores = [pltpu.make_async_copy(attn, attn_out, store_sem.at[0]), pltpu.make_async_copy(mlp, mlp_out, store_sem.at[1])]
    for c in stores:
        c.start()
    loads[-2].wait()

    def head(h, carry):
        lanes = pl.ds(pl.multiple_of(h * HEAD, HEAD), HEAD)

        def project(r, carry):
            at = pl.ds(pl.multiple_of(r * band, band), band)
            cos_t, sin_t = cos_ref[at, :], sin_ref[at, :]
            for part, target in enumerate((q_ref, k_ref, v_ref)):
                cols = pl.ds(pl.multiple_of(part * width + h * HEAD, HEAD), HEAD)
                value = jnp.dot(attn[at, :], qkv_w[:, cols], preferred_element_type=full) + qkv_bias_ref[:, cols]
                if part < 2:
                    value = turn(value, cos_t, sin_t)
                target[at, lanes] = value.astype(low)
            return carry
        lax.fori_loop(0, seq // band, project, 0)
        for begin in range(0, seq, band):
            end = begin + band
            p = weights_of(q_ref[begin:end, lanes], k_ref[:end, lanes], begin, len_ref[0], scale)
            ctx_ref[begin:end, lanes] = jnp.dot(p.astype(low), v_ref[:end, lanes], preferred_element_type=full).astype(low)
        return carry

    lax.fori_loop(0, width // HEAD, head, 0)
    arrived(0)
    start(3)
    start(4)
    arrived(1)
    start(5)
    hops.forward(1)
    loads[-1].wait()

    def pre_store(block, slot):
        return pltpu.make_async_copy(pre.at[slot], pre_out.at[:, pl.ds(pl.multiple_of(block * units, units), units)],
                                     pre_sem.at[slot])

    def unit_block(block, carry):
        slot = lax.rem(block, 2)

        @pl.when(block >= 2)
        def _():
            pre_store(block - 2, slot).wait()

        of = pl.ds(pl.multiple_of(block * units, units), units)

        def row_band(r, carry):
            at = pl.ds(pl.multiple_of(r * band, band), band)
            value = lax.dot_general(mlp[at, :], up_w[of, :], (((1,), (1,)), ((), ())), preferred_element_type=full)
            value = value + unit_bias_ref[:, of]
            pre[slot, at, :] = value
            hidden[at, of] = gelu_value(value).astype(low)
            return carry
        lax.fori_loop(0, seq // band, row_band, 0)
        pre_store(block, slot).start()
        return carry

    blocks = up_w.shape[0] // units
    lax.fori_loop(0, blocks // 2, unit_block, 0)
    arrived(3)
    start(6)
    lax.fori_loop(blocks // 2, blocks, unit_block, 0)
    for block in (blocks - 2, blocks - 1):
        pre_store(block, block % 2).wait()
    for c in stores + keeps:
        c.wait()
    hidden_store = pltpu.make_async_copy(hidden, hidden_out, store_sem.at[0])
    hidden_store.start()
    for message in (2, 4, 5, 6):
        arrived(message)
    half = up_w.shape[0] // 2
    out_rows = out_hbm.shape[0]
    late = [load(down_all.at[pl.ds(0, half)], tok, 0), load(down_all.at[pl.ds(half, half)], attn, 1),
            load(out_hbm, up_w.at[pl.ds(0, out_rows)], 2)]
    for c in late:
        c.start()
    hops.forward(2)
    for c in late:
        c.wait()

    def part_store(r):
        at = pl.ds(pl.multiple_of(r * band, band), band)
        return pltpu.make_async_copy(mlp.at[at], part_out.at[at], part_sem.at[r])

    def out_band(r, carry):
        at = pl.ds(pl.multiple_of(r * band, band), band)

        def out_columns(c, carry):
            to = pl.ds(pl.multiple_of(c * band, band), band)
            total = jnp.dot(hidden[at, :half], tok[:, to], preferred_element_type=full)
            total = total + jnp.dot(hidden[at, half:], attn[:, to], preferred_element_type=full)
            total = total + jnp.dot(ctx_ref[at, :], up_w[:out_rows, to], preferred_element_type=full)
            mlp[at, to] = total.astype(low)
            return carry
        lax.fori_loop(0, wide // band, out_columns, 0)
        part_store(r).start()
        return carry
    lax.fori_loop(0, seq // band, out_band, 0)
    hops.forward(3)
    for r in range(seq // band):
        part_store(r).wait()
    hidden_store.wait()
    for message in range(7):
        copy(message, *sends[message]).wait_send()
    hops.finish()

def front(sp_size, tokens, qkv_own, up_own, out_own, down_weight, cotangent, gains, shifts, qkv_bias, unit_bias, cos_t, sin_t,
          lengths, dp_size):
    seq, wide = tokens.shape
    units = down_weight.shape[0]
    width = qkv_own.shape[1] // 3
    all_units = up_own.shape[0]
    full, low = jnp.float32, jnp.bfloat16
    hbm = pl.BlockSpec(memory_space=pltpu.HBM)
    vmem = pl.BlockSpec(memory_space=pltpu.VMEM)
    dma = pltpu.SemaphoreType.DMA
    shape = jax.ShapeDtypeStruct
    return pl.pallas_call(
        functools.partial(front_kernel, sp_size),
        out_shape=[shape((units * dp_size, wide), low), shape((seq, wide), low), shape((seq, wide), low), shape((seq, wide), low),
                   shape((seq, all_units), low), shape((seq, all_units), full), shape((seq, wide), low)]
        + [shape((seq, width), low)] * 4,
        in_specs=[pl.BlockSpec(memory_space=pltpu.SMEM), hbm, hbm, hbm, hbm] + [vmem] * 8,
        out_specs=[hbm] * 7 + [vmem] * 4,
        scratch_shapes=[pltpu.VMEM((seq, wide), low)] * 3 + [
            pltpu.VMEM(qkv_own.shape, low), pltpu.VMEM(up_own.shape, low),
            pltpu.VMEM((seq, all_units), low), pltpu.VMEM((2, seq, units), full),
            dma((7,)), dma((7,)), dma((seq // 256 + 2,)), dma((2,)), dma((2,)), dma((2,)), dma((seq // 256,)),
            dma((2, sp_size)), dma((2, sp_size))],
        compiler_params=pltpu.CompilerParams(collective_id=2, has_side_effects=True, vmem_limit_bytes=60 << 20),
        cost_estimate=pl.CostEstimate(flops=26 * 10 ** 9, bytes_accessed=80 * 1000 * 1000, transcendentals=0),
        name="front",
    )(lengths, tokens, qkv_own, up_own, out_own, down_weight, cotangent, gains, shifts, qkv_bias, unit_bias, cos_t, sin_t)

CHUNK = 512


def add_into(target, *others):
    step_rows = 32

    def step(i, carry):
        at = pl.ds(pl.multiple_of(i * step_rows, step_rows), step_rows)
        total = target[at, :].astype(jnp.float32)
        for other in others:
            total = total + other[at, :].astype(jnp.float32)
        target[at, :] = total.astype(jnp.bfloat16)
        return carry

    lax.fori_loop(0, target.shape[0] // step_rows, step, 0)


class Square:
    def __init__(self, sp_size, lent, sib_send, sib_recv, one_send, one_recv, two_send, two_recv):
        self.dp, self.sp, self.sp_size = lax.axis_index("dp"), lax.axis_index("sp"), sp_size
        self.core, self.chip = self.dp % 2, self.dp // 2
        self.x, self.y = self.chip % 2, self.chip // 2
        self.sibling = self.dp + 1 - 2 * self.core
        self.across_x, self.across_y = self.dp + 2 - 4 * self.x, self.dp + 4 - 8 * self.y
        self.first = self.across_y * (1 - self.core) + self.across_x * self.core
        self.second = self.across_x * (1 - self.core) + self.across_y * self.core
        self.second_mask = 1 + self.core
        self.lent = lent
        self.sib_send, self.sib_recv, self.one_send, self.one_recv, self.two_send, self.two_recv = (
            sib_send, sib_recv, one_send, one_recv, two_send, two_recv)

    def chip_of(self, mask):
        return lax.rem(self.x + lax.rem(mask, 2), 2) + 2 * lax.rem(self.y + mask // 2, 2)

    def greet(self, barrier):
        for other in (self.first, self.second, self.sibling):
            pl.semaphore_signal(barrier, inc=1, device_id=(other, self.sp), device_id_type=MESH)
        for step in range(1, self.sp_size):
            pl.semaphore_signal(
                barrier, inc=1, device_id=(self.dp, lax.rem(self.sp + step, self.sp_size)), device_id_type=MESH)


def remote(source, target, send, recv, device):
    return pltpu.make_async_remote_copy(
        src_ref=source, dst_ref=target, send_sem=send, recv_sem=recv, device_id=device, device_id_type=MESH)


class Wide:
    def __init__(self, place, index, left, right, width, sums, sib, one, two):
        self.place, self.index, self.left, self.right, self.width = place, index, left, right, width
        self.sums, self.sib, self.one, self.two = sums, sib, one, two
        self.units = sums.shape[1]

    def product(self, block, store):
        at = pl.ds(pl.multiple_of(block * self.units, self.units), self.units)

        def columns(part, carry):
            to = pl.ds(pl.multiple_of(part * CHUNK, CHUNK), CHUNK)
            store(to, lax.dot_general(
                self.left[:, at], self.right[:, to], (((0,), (0,)), ((), ())),
                preferred_element_type=jnp.float32))
            return carry
        lax.fori_loop(0, self.width // CHUNK, columns, 0)

    def sib_copy(self, slot):
        p = self.place
        return remote(p.lent.at[slot, :, :self.width], self.sib.at[p.chip_of(3 - slot)],
                      p.sib_send.at[self.index, slot], p.sib_recv.at[self.index, slot], (p.sibling, p.sp))

    def for_sibling(self, previous):
        p = self.place

        def step(slot, carry):
            if previous is not None:
                previous.sib_copy(slot).wait_send()

            def store(to, total):
                p.lent[slot, :, to] = total.astype(jnp.bfloat16)
            self.product(p.chip_of(3 - slot) * 2 + 1 - p.core, store)
            self.sib_copy(slot).start()
            return carry
        lax.fori_loop(0, 4, step, 0)

    def own(self, mask, slot):
        at = self.place.chip_of(mask)
        self.sib_copy(slot).wait_recv()

        def store(to, total):
            self.sums[mask, :, to] = (total + self.sib[at, :, to].astype(jnp.float32)).astype(jnp.bfloat16)
        self.product(at * 2 + self.place.core, store)

    def for_self(self):
        core = self.place.core

        def leave(slot, carry):
            mask = 3 - slot * (1 + core)
            self.own(mask, 3 - mask)
            self.first_copy(slot).start()
            return carry
        lax.fori_loop(0, 2, leave, 0)

        def stay(slot, carry):
            mask = self.place.second_mask * (1 - slot)
            self.own(mask, 3 - mask)
            return carry
        lax.fori_loop(0, 2, stay, 0)

    def block(self, mask):
        return self.sums.at[mask]

    def first_copy(self, slot):
        p = self.place
        return remote(self.block(3 - slot * (1 + p.core)), self.one.at[slot], p.one_send.at[self.index, slot],
                      p.one_recv.at[self.index, slot], (p.first, p.sp))

    def second_copy(self):
        p = self.place
        return remote(self.block(p.second_mask), self.two, p.two_send.at[self.index],
                      p.two_recv.at[self.index], (p.second, p.sp))

    def onward(self):
        self.first_copy(0).wait_recv()
        add_into(self.block(self.place.second_mask), self.one.at[0])
        self.second_copy().start()

    def finish(self):
        self.first_copy(1).wait_recv()
        self.second_copy().wait_recv()
        add_into(self.block(0), self.one.at[1], self.two)

    def drain(self):
        for slot in (0, 1):
            self.first_copy(slot).wait_send()
        self.second_copy().wait_send()


class Dense(Wide):
    def __init__(self, place, index, left, right, width, sums, sib, one, two, part):
        self.place, self.index, self.left, self.right, self.width = place, index, left, right, width
        self.sums, self.sib, self.one, self.two, self.part = sums, sib, one, two, part
        self.units, self.rows = sums.shape[0], one.shape[1]

    def sib_copy(self, slot):
        p = self.place
        return remote(self.part, self.sib, p.sib_send.at[self.index, 0], p.sib_recv.at[self.index, 0], (p.sibling, p.sp))

    def for_sibling(self, previous):
        def store(to, total):
            self.part[:, to] = total.astype(jnp.bfloat16)
        self.product(1 - self.place.core, store)
        self.sib_copy(0).start()

    def for_self(self):
        self.sib_copy(0).wait_recv()

        def store(to, total):
            self.sums[:, to] = (total + self.sib[:, to].astype(jnp.float32)).astype(jnp.bfloat16)
        self.product(self.place.core, store)
        for slot in (0, 1):
            self.first_copy(slot).start()

    def block(self, mask):
        return self.sums.at[pl.ds(pl.multiple_of(self.place.chip_of(mask) * self.rows, self.rows), self.rows)]


class Fold:
    def __init__(self, place, source, inbox, stage, stage_sem, send, recv):
        self.place, self.source, self.inbox, self.stage = place, source, inbox, stage
        self.stage_sem, self.send, self.recv = stage_sem, send, recv
        self.rows = stage.shape[0]

    def along(self, way):
        last = self.place.sp_size - 1
        return self.place.sp if way == 0 else last - self.place.sp

    def rows_of(self, way, step):
        count = self.place.sp_size
        owner = self.along(way) + count - step
        owner = owner if way == 0 else count - 1 - owner
        return self.source.at[pl.ds(pl.multiple_of(owner * self.rows, self.rows), self.rows)]

    def copy(self, way, step, own):
        p = self.place
        to = lax.rem(p.sp + (1 if way == 0 else p.sp_size - 1), p.sp_size)
        source = self.rows_of(way, step) if own else self.inbox.at[way, max(step - 2, 0)]
        return remote(source, self.inbox.at[way, step - 1], self.send.at[way, step - 1],
                      self.recv.at[way, step - 1], (p.dp, to))

    def take(self, rows):
        c = pltpu.make_async_copy(rows, self.stage, self.stage_sem)
        c.start()
        c.wait()

    def step(self, step):
        last = self.place.sp_size - 1
        for way in (0, 1):
            if step == 1:
                @pl.when(self.along(way) == 0)
                def _():
                    for early in range(1, last + 1):
                        self.copy(way, early, True).start()
            else:
                @pl.when((self.along(way) > 0) & (self.along(way) < step) & (self.along(way) < last))
                def _():
                    self.take(self.rows_of(way, step))
                    self.copy(way, step - 1, False).wait_recv()
                    add_into(self.inbox.at[way, step - 2], self.stage)
                    self.copy(way, step, False).start()

    def finish(self):
        last = self.place.sp_size - 1
        self.take(self.source.at[pl.ds(pl.multiple_of(self.place.sp * self.rows, self.rows), self.rows)])
        for way in (0, 1):
            @pl.when(self.along(way) > 0)
            def _():
                self.copy(way, last, False).wait_recv()
                add_into(self.stage, self.inbox.at[way, last - 1])

    def drain(self):
        last = self.place.sp_size - 1
        for way in (0, 1):
            for step in range(1, last + 1):
                @pl.when(self.along(way) == 0)
                def _():
                    self.copy(way, step, True).wait_send()

                if step > 1:
                    @pl.when((self.along(way) > 0) & (self.along(way) < step) & (self.along(way) < last))
                    def _():
                        self.copy(way, step, False).wait_send()


def middle_kernel(sp_size, len_ref, cot_hbm, out_hbm, q_hbm, k_hbm, v_hbm, pre_hbm, hidden_hbm, down_hbm, up_hbm, qkv_hbm,
                  tok_hbm, part_hbm, gain_ref, cos_ref, sin_ref,
                  down_out, hat_out, proj_out, gpre_out, gout_out, red_out, small_ref,
                  cot, left, gpre, up_w, qkv_w, pre, gctx, gproj, dq, dk, dv, mean_s, inv_s,
                  lent, down_sum, down_sib, down_one, down_two, inbox, stage,
                  load_sem, stream_sem, store_sem, stage_sem, sib_send, sib_recv, one_send, one_recv, two_send, two_recv,
                  fold_send, fold_recv):
    full, low = jnp.float32, jnp.bfloat16
    place = Square(sp_size, lent, sib_send, sib_recv, one_send, one_recv, two_send, two_recv)
    seq, wide = cot.shape
    width = gctx.shape[1]
    heads = width // HEAD
    units = down_sum.shape[1]
    blocks = up_w.shape[0] // units
    out_rows = out_hbm.shape[0]
    band = 256
    bands = seq // band
    scale = HEAD ** -0.5

    def load(source, target, which):
        c = pltpu.make_async_copy(source, target, load_sem.at[which])
        c.start()
        return c

    early = [load(cot_hbm, cot, 0), load(hidden_hbm, left, 1), load(out_hbm, up_w.at[pl.ds(0, out_rows)], 2)]
    for i, source in enumerate((q_hbm, k_hbm, v_hbm)):
        early.append(load(source, qkv_w.at[pl.ds(0, seq), pl.ds(i * width, width)], 3 + i))

    def down_load(block, slot):
        return pltpu.make_async_copy(
            down_hbm.at[pl.ds(pl.multiple_of(block * units, units), units)],
            up_w.at[pl.ds(pl.multiple_of(out_rows + slot * units, units), units)], stream_sem.at[0, slot])

    def pre_load(block, slot):
        return pltpu.make_async_copy(
            pre_hbm.at[:, pl.ds(pl.multiple_of(block * units, units), units)], pre.at[slot], stream_sem.at[1, slot])

    for slot in (0, 1):
        down_load(slot, slot).start()
        pre_load(slot, slot).start()

    barrier = pltpu.get_barrier_semaphore()
    place.greet(barrier)
    pl.semaphore_wait(barrier, 2 + sp_size)
    fold = Fold(place, part_hbm, inbox, stage, stage_sem, fold_send, fold_recv)
    fold.step(1)
    small_ref[...] = jnp.zeros_like(small_ref)
    gain_row, shift_row, bias_row, unit_row = 0, 2, 4, 7
    per_row = wide // (sp_size * units)
    last_row = unit_row + blocks // per_row

    early[0].wait()

    def mask_rows(i, carry):
        at = pl.ds(pl.multiple_of(i * 32, 32), 32)
        row = i * 32 + lax.broadcasted_iota(jnp.int32, (32, wide), 0)
        cot[at, :] = jnp.where(row < len_ref[0], cot[at, :].astype(full), 0.0).astype(low)
        return carry
    lax.fori_loop(0, seq // 32, mask_rows, 0)
    stores = [pltpu.make_async_copy(cot, gout_out, store_sem.at[0])]
    stores[0].start()

    def own_rows(i, carry):
        at = pl.ds(pl.multiple_of(place.sp * (seq // sp_size) + i * 32, 32), 32)
        return carry + jnp.sum(cot[at, :].astype(full), axis=0, keepdims=True)
    small_ref[last_row:last_row + 1, :] = lax.fori_loop(0, seq // sp_size // 32, own_rows, jnp.zeros((1, wide), full))

    down = Wide(place, 0, left, cot, wide, down_sum, down_sib, down_one, down_two)
    early[1].wait()
    down.for_sibling(None)
    early[2].wait()

    def context_band(r, carry):
        at = pl.ds(pl.multiple_of(r * band, band), band)
        gctx[at, :] = lax.dot_general(
            cot[at, :], up_w[:out_rows, :], (((1,), (1,)), ((), ())), preferred_element_type=full).astype(low)
        return carry
    lax.fori_loop(0, bands, context_band, 0)
    down.for_self()
    fold.step(2)
    for c in early[3:]:
        c.wait()

    def head(h, carry):
        lanes = pl.ds(pl.multiple_of(h * HEAD, HEAD), HEAD)
        k_lanes = pl.ds(pl.multiple_of(width + h * HEAD, HEAD), HEAD)
        v_lanes = pl.ds(pl.multiple_of(2 * width + h * HEAD, HEAD), HEAD)
        dk[...] = jnp.zeros_like(dk)
        dv[...] = jnp.zeros_like(dv)
        for begin in range(0, seq, band):
            end = begin + band
            q, g = qkv_w[begin:end, lanes], gctx[begin:end, lanes]
            k, v = qkv_w[:end, k_lanes], qkv_w[:end, v_lanes]
            p = weights_of(q, k, begin, len_ref[0], scale)
            gp = lax.dot_general(g, v, (((1,), (1,)), ((), ())), preferred_element_type=full)
            ds = (p * (gp - jnp.sum(p * gp, axis=-1, keepdims=True))).astype(low)
            dq[begin:end, :] = jnp.dot(ds, k, preferred_element_type=full) * scale
            dk[:end, :] += lax.dot_general(ds, q, (((0,), (0,)), ((), ())), preferred_element_type=full)
            dv[:end, :] += lax.dot_general(p.astype(low), g, (((0,), (0,)), ((), ())), preferred_element_type=full)

        def back(r, sums):
            at = pl.ds(pl.multiple_of(r * band, band), band)
            cos_t, sin_t = cos_ref[at, :], -sin_ref[at, :]
            pieces = (turn(dq[at, :].astype(low).astype(full), cos_t, sin_t).astype(low),
                      turn((dk[at, :] * scale).astype(low).astype(full), cos_t, sin_t).astype(low),
                      dv[at, :].astype(low))
            out = []
            for part, (piece, total) in enumerate(zip(pieces, sums)):
                gproj[at, pl.ds(pl.multiple_of(part * width + h * HEAD, HEAD), HEAD)] = piece
                out.append(total + jnp.sum(piece.astype(full), axis=0, keepdims=True))
            return tuple(out)
        sums = lax.fori_loop(0, bands, back, (jnp.zeros((1, HEAD), full),) * 3)
        for part, total in enumerate(sums):
            small_ref[bias_row + part:bias_row + part + 1,
                      pl.ds(pl.multiple_of(place.sp * width + h * HEAD, HEAD), HEAD)] = total
        return carry
    lax.fori_loop(0, heads, head, 0)
    stores.append(pltpu.make_async_copy(gproj, proj_out, store_sem.at[1]))
    stores[1].start()
    qkv_load = load(qkv_hbm, qkv_w, 3)

    def unit_block(block, carry):
        slot = lax.rem(block, 2)
        down_load(block, slot).wait()
        pre_load(block, slot).wait()
        of = pl.ds(pl.multiple_of(block * units, units), units)
        room = pl.ds(pl.multiple_of(out_rows + slot * units, units), units)

        def row_band(r, total):
            at = pl.ds(pl.multiple_of(r * band, band), band)
            value = lax.dot_general(cot[at, :], up_w[room, :], (((1,), (1,)), ((), ())), preferred_element_type=full)
            value = (value * gelu_slope(pre[slot, at, :])).astype(low)
            gpre[at, of] = value
            return total + jnp.sum(value.astype(full), axis=0, keepdims=True)
        total = lax.fori_loop(0, bands, row_band, jnp.zeros((1, units), full))
        small_ref[pl.ds(unit_row + block // per_row, 1),
                  pl.ds(pl.multiple_of((lax.rem(block, per_row) * sp_size + place.sp) * units, units), units)] = total

        @pl.when(block + 2 < blocks)
        def _():
            down_load(block + 2, slot).start()
            pre_load(block + 2, slot).start()
        return carry

    lax.fori_loop(0, blocks // 2, unit_block, 0)
    fold.step(3)
    down.onward()
    tok_load = load(tok_hbm, left, 1)
    lax.fori_loop(blocks // 2, blocks, unit_block, 0)
    up_load = load(up_hbm, up_w, 0)
    stores.append(pltpu.make_async_copy(gpre, gpre_out, store_sem.at[2]))
    stores[2].start()
    tok_load.wait()

    def statistics(i, carry):
        at = pl.ds(pl.multiple_of(i * 32, 32), 32)
        rows = left[at, :].astype(full)
        mean = jnp.mean(rows, axis=-1, keepdims=True)
        centered = rows - mean
        inverse = lax.rsqrt(jnp.mean(centered * centered, axis=-1, keepdims=True) + eps)
        mean_s[at, :] = jnp.broadcast_to(mean, (32, 128))
        inv_s[at, :] = jnp.broadcast_to(inverse, (32, 128))
        return carry
    lax.fori_loop(0, seq // 32, statistics, 0)
    stores[0].wait()
    qkv_load.wait()
    up_load.wait()

    def hat_store(r):
        at = pl.ds(pl.multiple_of(r * band, band), band)
        return pltpu.make_async_copy(cot.at[at], hat_out.at[at], store_sem.at[3 + r])

    def hat_band(r):
        at = pl.ds(r * band, band)

        def columns(c, carry):
            to = pl.ds(pl.multiple_of(c * band, band), band)
            from_mlp = jnp.dot(gpre[at, :], up_w[:, to], preferred_element_type=full)
            from_attn = lax.dot_general(gproj[at, :], qkv_w[to, :], (((1,), (1,)), ((), ())), preferred_element_type=full)
            normed = (left[at, to].astype(full) - mean_s[at, 0:1]) * inv_s[at, 0:1]
            small_ref[gain_row:gain_row + 1, to] += jnp.sum(from_attn * normed, axis=0, keepdims=True)
            small_ref[gain_row + 1:gain_row + 2, to] += jnp.sum(from_mlp * normed, axis=0, keepdims=True)
            small_ref[shift_row:shift_row + 1, to] += jnp.sum(from_attn, axis=0, keepdims=True)
            small_ref[shift_row + 1:shift_row + 2, to] += jnp.sum(from_mlp, axis=0, keepdims=True)
            cot[at, to] = (from_attn * gain_ref[0:1, to] + from_mlp * gain_ref[1:2, to]).astype(low)
            return carry
        lax.fori_loop(0, wide // band, columns, 0)
        hat_store(r).start()

    for r in range(bands):
        hat_band(r)
    fold.finish()
    stores.append(pltpu.make_async_copy(stage, red_out, store_sem.at[3 + bands]))
    stores[-1].start()
    down.finish()
    stores.append(pltpu.make_async_copy(down.block(0), down_out, store_sem.at[4 + bands]))
    stores[-1].start()
    for r in range(bands):
        hat_store(r).wait()
    for c in stores[1:]:
        c.wait()
    for slot in range(4):
        down.sib_copy(slot).wait_send()
    down.drain()
    fold.drain()


def middle(sp_size, dp_size, lengths, cotangent, out_own, queries, key_rows, values, pre_act, hidden, down_own, up_own, qkv_own,
           tokens, partial_out, gains, cos_t, sin_t):
    seq, wide = tokens.shape
    width = queries.shape[1]
    units = up_own.shape[0] // dp_size
    own = seq // sp_size
    full, low = jnp.float32, jnp.bfloat16
    hbm = pl.BlockSpec(memory_space=pltpu.HBM)
    vmem = pl.BlockSpec(memory_space=pltpu.VMEM)
    dma = pltpu.SemaphoreType.DMA
    shape = jax.ShapeDtypeStruct

    def v(*dims, kind=low):
        return pltpu.VMEM(dims, kind)
    bands = seq // 256
    return pl.pallas_call(
        functools.partial(middle_kernel, sp_size),
        out_shape=[shape((units, wide), low), shape((seq, wide), low), shape((seq, 3 * width), low), shape(hidden.shape, low),
                   shape((seq, wide), low), shape((own, wide), low), shape((16, wide), full)],
        in_specs=[pl.BlockSpec(memory_space=pltpu.SMEM)] + [hbm] * 12 + [vmem] * 3,
        out_specs=[hbm] * 6 + [vmem],
        scratch_shapes=[
            v(seq, wide), v(seq, wide), v(*hidden.shape), v(*up_own.shape), v(*qkv_own.shape), v(2, seq, units, kind=full),
            v(seq, width), v(seq, 3 * width), v(seq, HEAD, kind=full), v(seq, HEAD, kind=full), v(seq, HEAD, kind=full),
            v(seq, 128, kind=full), v(seq, 128, kind=full),
            v(4, units, wide), v(4, units, wide), v(4, units, wide), v(2, units, wide), v(units, wide),
            v(2, sp_size - 1, own, wide), v(own, wide),
            dma((6,)), dma((2, 2)), dma((5 + bands,)), dma, dma((1, 4)), dma((1, 4)), dma((1, 2)), dma((1, 2)), dma((1,)), dma((1,)),
            dma((2, sp_size - 1)), dma((2, sp_size - 1))],
        compiler_params=pltpu.CompilerParams(collective_id=3, has_side_effects=True, vmem_limit_bytes=67043328),
        cost_estimate=pl.CostEstimate(flops=40 * 10 ** 9, bytes_accessed=90 * 1000 * 1000, transcendentals=0),
        name="middle",
    )(lengths, cotangent, out_own, queries, key_rows, values, pre_act, hidden, down_own, up_own, qkv_own, tokens, partial_out,
      gains, cos_t, sin_t)


def back_kernel(sp_size, cot_hbm, pre_hbm, mlp_hbm, attn_hbm, proj_hbm, ctx_hbm, hat_hbm, small_ref,
                up_out, qkv_out, dense_out, red_out, small_out,
                left_a, right_a, left_b, right_b, ctx, lent,
                up_sum, qkv_sum, dense_sum, up_sib, qkv_sib, dense_sib, up_one, qkv_one, dense_one, up_two, qkv_two, dense_two,
                dense_part, small_acc, small_in, small_z, inbox, stage,
                load_sem, store_sem, stage_sem, sib_send, sib_recv, one_send, one_recv, two_send, two_recv,
                slab_send, slab_recv, turn_send, turn_recv, small_send, small_recv, z_send, z_recv, fold_send, fold_recv):
    place = Square(sp_size, lent, sib_send, sib_recv, one_send, one_recv, two_send, two_recv)
    dp, sp = place.dp, place.sp
    per = 2
    pair, lane = dp // per, dp % per
    turn_dp = sp * per + lane
    slab_width = qkv_sum.shape[2]
    head_width = slab_width // 3
    rows = dense_one.shape[1]
    wide = left_b.shape[1]

    def load(source, target, which):
        c = pltpu.make_async_copy(source, target, load_sem.at[which])
        c.start()
        return c

    loads = [load(attn_hbm, left_a, 0), load(proj_hbm, right_a, 1), load(cot_hbm, right_b, 2), load(ctx_hbm, ctx, 3),
             load(pre_hbm, left_b, 4)]

    barrier = pltpu.get_barrier_semaphore()
    place.greet(barrier)

    @pl.when(pair != sp)
    def _():
        pl.semaphore_signal(barrier, inc=1, device_id=(turn_dp, pair), device_id_type=MESH)

    pl.semaphore_wait(barrier, 2 + sp_size + jnp.where(pair != sp, 1, 0))
    fold = Fold(place, hat_hbm, inbox, stage, stage_sem, fold_send, fold_recv)
    fold.step(1)

    def small_copy(stage_of):
        partner = (place.sibling, place.across_x, place.across_y)[stage_of]
        return remote(small_ref if stage_of == 0 else small_acc.at[stage_of - 1], small_in.at[stage_of],
                      small_send.at[stage_of], small_recv.at[stage_of], (partner, sp))

    def small_step(stage_of):
        small_copy(stage_of).wait_recv()
        before = small_ref[...] if stage_of == 0 else small_acc[stage_of - 1]
        small_acc[stage_of] = before + small_in[stage_of]

    def z_copy(step):
        return remote(small_acc.at[2], small_z.at[sp], z_send.at[step - 1], z_recv.at[step - 1],
                      (dp, lax.rem(sp + step, sp_size)))

    def z_arrival(step):
        origin = lax.rem(sp + sp_size - step, sp_size)
        return remote(small_acc.at[2], small_z.at[origin], z_send.at[step - 1], z_recv.at[step - 1], (dp, origin))

    small_copy(0).start()
    qkv = Wide(place, 0, left_a, right_a, slab_width, qkv_sum, qkv_sib, qkv_one, qkv_two)
    dense = Dense(place, 1, ctx, right_b, wide, dense_sum, dense_sib, dense_one, dense_two, dense_part)
    up = Wide(place, 2, left_b, right_b, wide, up_sum, up_sib, up_one, up_two)

    def turn_copy():
        return remote(dense.block(0), dense_out, turn_send, turn_recv, (turn_dp, pair))

    def slab_rows(owner):
        return pl.ds(pl.multiple_of(owner * rows, rows), rows)

    def slab_columns(part, owner):
        return pl.ds(pl.multiple_of(part * wide + owner * head_width, head_width), head_width)

    def slab_copy(step, part, origin, there):
        return remote(qkv_sum.at[0, slab_rows(there), pl.ds(part * head_width, head_width)],
                      qkv_out.at[:, slab_columns(part, origin)],
                      slab_send.at[step - 1, part], slab_recv.at[step - 1, part], (dp, there))

    stores = []

    def store(source, target):
        c = pltpu.make_async_copy(source, target, store_sem.at[len(stores)])
        c.start()
        stores.append(c)

    loads[0].wait()
    loads[1].wait()
    qkv.for_sibling(None)
    small_step(0)
    small_copy(1).start()
    qkv.for_self()
    loads[2].wait()
    loads[3].wait()
    dense.for_sibling(None)
    small_step(1)
    small_copy(2).start()
    dense.for_self()
    late = load(mlp_hbm, right_b, 2)
    fold.step(2)
    loads[4].wait()
    late.wait()
    up.for_sibling(qkv)
    qkv.onward()
    small_step(2)
    for step in range(1, sp_size):
        z_copy(step).start()
    small_z[sp] = small_acc[2]
    up.for_self()
    dense.onward()
    qkv.finish()
    for step in range(1, sp_size):
        for part in range(3):
            slab_copy(step, part, sp, lax.rem(sp + step, sp_size)).start()
    for part in range(3):
        store(qkv_sum.at[0, slab_rows(sp), pl.ds(part * head_width, head_width)], qkv_out.at[:, slab_columns(part, sp)])
    fold.step(3)
    dense.finish()

    @pl.when(pair != sp)
    def _():
        turn_copy().start()

    @pl.when(pair == sp)
    def _():
        c = pltpu.make_async_copy(dense.block(0), dense_out, store_sem.at[5])
        c.start()
        c.wait()

    for step in range(1, sp_size):
        z_arrival(step).wait_recv()
    total = small_z[0]
    for origin in range(1, sp_size):
        total = total + small_z[origin]
    small_out[...] = total
    up.onward()
    for step in range(1, sp_size):
        for part in range(3):
            slab_copy(step, part, lax.rem(sp + sp_size - step, sp_size), sp).wait_recv()

    @pl.when(pair != sp)
    def _():
        turn_copy().wait_recv()
        turn_copy().wait_send()

    for slot in range(4):
        up.sib_copy(slot).wait_send()
    dense.sib_copy(0).wait_send()
    fold.finish()
    store(stage, red_out)
    for array in (qkv, dense, up):
        array.drain()
    for stage_of in range(3):
        small_copy(stage_of).wait_send()
    for step in range(1, sp_size):
        z_copy(step).wait_send()
        for part in range(3):
            slab_copy(step, part, sp, lax.rem(sp + step, sp_size)).wait_send()
    fold.drain()
    up.finish()
    store(up.block(0), up_out)
    for c in stores:
        c.wait()


def reduce_gradients(sp_size, rows, grad_out, grad_pre, mlp_in, attn_in, grad_proj, context, grad_hat, small):
    seq, wide = mlp_in.shape
    slab_width = grad_proj.shape[1]
    units = 4 * rows
    own = seq // sp_size
    full, low = jnp.float32, jnp.bfloat16
    hbm = pl.BlockSpec(memory_space=pltpu.HBM)
    vmem = pl.BlockSpec(memory_space=pltpu.VMEM)
    dma = pltpu.SemaphoreType.DMA
    shape = jax.ShapeDtypeStruct

    def v(*dims, kind=low):
        return pltpu.VMEM(dims, kind)
    scratch = [
        v(seq, wide), v(seq, slab_width), v(seq, wide), v(seq, wide), v(seq, context.shape[1]), v(4, units, wide),
        v(4, units, wide), v(4, units, slab_width), v(4 * rows, wide),
        v(4, units, wide), v(4, units, slab_width), v(4 * rows, wide),
        v(2, units, wide), v(2, units, slab_width), v(2, rows, wide),
        v(units, wide), v(units, slab_width), v(rows, wide),
        v(4 * rows, wide),
        v(3, *small.shape, kind=full), v(3, *small.shape, kind=full), v(sp_size, *small.shape, kind=full),
        v(2, sp_size - 1, own, wide), v(own, wide),
        dma((5,)), dma((6,)), dma, dma((3, 4)), dma((3, 4)), dma((3, 2)), dma((3, 2)), dma((3,)), dma((3,)),
        dma((sp_size - 1, 3)), dma((sp_size - 1, 3)), dma, dma, dma((3,)), dma((3,)), dma((sp_size - 1,)), dma((sp_size - 1,)),
        dma((2, sp_size - 1)), dma((2, sp_size - 1)),
    ]
    return pl.pallas_call(
        functools.partial(back_kernel, sp_size),
        out_shape=[shape((units, wide), low), shape((rows, 3 * wide), low), shape((rows, wide), low), shape((own, wide), low),
                   shape(small.shape, full)],
        in_specs=[hbm] * 7 + [vmem], out_specs=[hbm] * 4 + [vmem],
        scratch_shapes=scratch,
        compiler_params=pltpu.CompilerParams(collective_id=1, has_side_effects=True, vmem_limit_bytes=67043328),
        cost_estimate=pl.CostEstimate(flops=17 * 10 ** 9, bytes_accessed=200 * 1000 * 1000, transcendentals=0),
        name="reduce_gradients",
    )(grad_out, grad_pre, mlp_in, attn_in, grad_proj, context, grad_hat, small)

def gather_plain(dp_size, sp_size, qkv_weight, out_weight, up_weight, down_weight):
    head_width = D // sp_size
    qkv_rows = qkv_weight.shape[0]
    qkv_slab = lax.all_to_all(
        qkv_weight.reshape(qkv_rows, 3, sp_size, head_width),
        "sp",
        split_axis=2,
        concat_axis=0,
        tiled=True,
    )
    qkv_own = lax.all_gather(
        qkv_slab.reshape(qkv_rows * sp_size, 3 * head_width), "dp", axis=0, tiled=True
    )
    up_own = lax.all_gather(up_weight, "dp", axis=0, tiled=True)
    down_own = lax.all_gather(down_weight, "dp", axis=0, tiled=True)
    out_blocks = lax.all_gather(out_weight, "dp", axis=0, tiled=True)
    out_own = lax.all_to_all(
        out_blocks.reshape(sp_size, dp_size // sp_size, qkv_rows, D),
        "sp",
        split_axis=0,
        concat_axis=2,
        tiled=True,
    ).reshape(head_width, D)
    return qkv_own, out_own, up_own, down_own


def reduce_plain(
    dp_size, sp_size, rows, hidden, grad_out, grad_pre, mlp_in, attn_in, grad_proj, context
):
    def scatter(left, right):
        return lax.psum_scatter(
            contract_rows(left, right).astype(jnp.bfloat16), "dp", scatter_dimension=0, tiled=True
        )

    grad_dense = lax.all_to_all(
        contract_rows(context, grad_out)
        .astype(jnp.bfloat16)
        .reshape(dp_size // sp_size, sp_size, rows, D),
        "sp",
        split_axis=1,
        concat_axis=0,
        tiled=True,
    ).reshape(dp_size * rows, D)
    grad_dense = lax.psum_scatter(grad_dense, "dp", scatter_dimension=0, tiled=True)
    grad_qkv = lax.all_to_all(
        scatter(attn_in, grad_proj).reshape(sp_size, rows, 3, 1, D // sp_size),
        "sp",
        split_axis=0,
        concat_axis=3,
        tiled=True,
    ).reshape(rows, 3 * D)
    return scatter(hidden, grad_out), scatter(grad_pre, mlp_in), grad_qkv, grad_dense


def body(
    tokens,
    lengths,
    cotangent,
    ln_gains,
    ln_shifts,
    qkv_weight,
    qkv_bias,
    out_weight,
    up_weight,
    up_bias,
    down_weight,
    out_bias,
):
    dp_size = lax.axis_size("dp")
    sp_size = lax.axis_size("sp")
    shard = lax.axis_index("sp")
    own_rows = tokens.shape[0]
    seq_rows = own_rows * sp_size
    head_width = D // sp_size
    length = lengths[0]
    low = jnp.bfloat16
    full = jnp.float32

    qkv_rows = qkv_weight.shape[0]
    units = up_weight.shape[0]
    square = dp_size == 8 and sp_size == 4
    unit_bias = (
        lax.dynamic_index_in_dim(
            up_bias.reshape(dp_size, sp_size, units), shard, 1, keepdims=False
        )
        .reshape(dp_size * units)
        .astype(full)
    )
    bias_own = (
        lax.dynamic_index_in_dim(
            qkv_bias.reshape(3, sp_size, head_width), shard, 1, keepdims=False
        )
        .reshape(1, 3 * head_width)
        .astype(full)
    )
    positions = jnp.arange(seq_rows, dtype=jnp.int32)
    gains = ln_gains.astype(full)
    shifts = ln_shifts.astype(full)
    row_valid = positions < length
    if square:
        qkv_own, out_own, up_own, seq_tokens, cos_rows, sin_rows = gather_weights(
            dp_size, sp_size, qkv_weight, out_weight, up_weight, tokens
        )
    else:
        cos_rows, sin_rows = rotary_rows(seq_rows)
        seq_tokens = lax.all_gather(tokens, "sp", axis=0, tiled=True)
        qkv_own, out_own, up_own, down_own = gather_plain(
            dp_size, sp_size, qkv_weight, out_weight, up_weight, down_weight
        )
        seq_cotangent = lax.all_gather(cotangent, "sp", axis=0, tiled=True)
    own_valid = shard * own_rows + jnp.arange(own_rows, dtype=jnp.int32) < length
    own_cotangent = jnp.where(own_valid[:, None], cotangent.astype(full), 0.0)
    if square:
        (
            down_own,
            seq_cotangent,
            attn_in,
            mlp_in,
            hidden,
            pre_act,
            partial_out,
            queries,
            key_rows,
            values,
            context,
        ) = front(
            sp_size,
            seq_tokens,
            qkv_own,
            up_own,
            out_own,
            down_weight,
            cotangent,
            gains,
            shifts,
            bias_own,
            unit_bias[None],
            cos_rows,
            sin_rows,
            lengths,
            dp_size,
        )
        grad_down, grad_hat, grad_proj, grad_pre, grad_out, reduced_out, small = middle(
            sp_size,
            dp_size,
            lengths,
            seq_cotangent,
            out_own,
            queries,
            key_rows,
            values,
            pre_act,
            hidden,
            down_own,
            up_own,
            qkv_own,
            seq_tokens,
            partial_out,
            gains,
            cos_rows,
            sin_rows,
        )
        grad_up, grad_qkv, grad_dense, reduced_hat, small = reduce_gradients(
            sp_size,
            qkv_rows,
            grad_out,
            grad_pre,
            mlp_in,
            attn_in,
            grad_proj,
            context,
            grad_hat,
            small,
        )
        gain_total, shift_total, qkv_bias_total = small[:2], small[2:4], small[4:7]
        unit_rows = up_bias.shape[0] // D
        unit_total = small[7 : 7 + unit_rows].reshape(-1)
        out_bias_total = small[7 + unit_rows]
    else:
        inputs = seq_tokens.astype(full)
        centre = jnp.mean(inputs, axis=-1, keepdims=True)
        centered = inputs - centre
        inverse = lax.rsqrt(jnp.mean(centered * centered, axis=-1, keepdims=True) + eps)
        normed = centered * inverse
        attn_in = (normed * gains[0] + shifts[0]).astype(low)
        mlp_in = (normed * gains[1] + shifts[1]).astype(low)
        projected = jnp.dot(attn_in, qkv_own, preferred_element_type=full)
        queries, key_rows, values, context = attend_fwd(
            projected, bias_own, cos_rows, sin_rows, lengths
        )
        pre_act = contract_cols(mlp_in, up_own) + unit_bias
        hidden = gelu_value(pre_act).astype(low)
        partial_out = (
            jnp.dot(hidden, down_own, preferred_element_type=full)
            + jnp.dot(context, out_own, preferred_element_type=full)
        ).astype(low)
        reduced_out = lax.psum_scatter(
            partial_out, "sp", scatter_dimension=0, tiled=True
        )
        grad_out = jnp.where(row_valid[:, None], seq_cotangent, jnp.zeros_like(seq_cotangent))
        grad_hidden = contract_cols(grad_out, down_own)
        grad_pre = (grad_hidden * gelu_slope(pre_act)).astype(low)
        grad_mlp_in = jnp.dot(grad_pre, up_own, preferred_element_type=full)

        grad_context = contract_cols(grad_out, out_own).astype(low)
        grad_proj, grad_proj_sum = attend_bwd(
            queries, key_rows, values, grad_context, cos_rows, sin_rows, lengths
        )
        grad_attn_in = contract_cols(grad_proj, qkv_own)
        grad_hat = grad_attn_in * gains[0] + grad_mlp_in * gains[1]
        reduced_hat = lax.psum_scatter(
            grad_hat.astype(low), "sp", scatter_dimension=0, tiled=True
        )
        spread_units = lax.dynamic_update_index_in_dim(
            jnp.zeros((dp_size, sp_size, units), full),
            jnp.sum(grad_pre, axis=0, dtype=full).reshape(dp_size, units),
            shard,
            1,
        ).reshape(-1)
        spread_bias = lax.dynamic_update_index_in_dim(
            jnp.zeros((3, sp_size, head_width), full),
            grad_proj_sum.reshape(3, head_width),
            shard,
            1,
        ).reshape(3, D)
        gain_grad = jnp.stack(
            [jnp.sum(grad_attn_in * normed, axis=0), jnp.sum(grad_mlp_in * normed, axis=0)]
        )
        shift_grad = jnp.stack([jnp.sum(grad_attn_in, axis=0), jnp.sum(grad_mlp_in, axis=0)])
        out_bias_part = jnp.sum(own_cotangent, axis=0)
        grad_down, grad_up, grad_qkv, grad_dense = reduce_plain(
            dp_size,
            sp_size,
            qkv_rows,
            hidden,
            grad_out,
            grad_pre,
            mlp_in,
            attn_in,
            grad_proj,
            context,
        )
        gain_total, shift_total, qkv_bias_total, unit_total, out_bias_total = lax.psum(
            (gain_grad, shift_grad, spread_bias, spread_units, out_bias_part), ("dp", "sp")
        )


    output = (
        tokens.astype(full) + reduced_out.astype(full) + out_bias.astype(full)
    ).astype(low)

    reduced_hat = reduced_hat.astype(full)
    own_centered = tokens.astype(full) - jnp.mean(tokens.astype(full), axis=-1, keepdims=True)
    own_inverse = lax.rsqrt(jnp.mean(own_centered * own_centered, axis=-1, keepdims=True) + eps)
    own_normed = own_centered * own_inverse
    grad_input = own_inverse * (
        reduced_hat
        - jnp.mean(reduced_hat, axis=-1, keepdims=True)
        - own_normed * jnp.mean(reduced_hat * own_normed, axis=-1, keepdims=True)
    )
    input_grad = (own_cotangent + grad_input).astype(low)
    return (
        output,
        input_grad,
        gain_total,
        shift_total,
        grad_qkv.astype(full),
        qkv_bias_total,
        grad_dense.astype(full),
        grad_up.astype(full),
        unit_total,
        grad_down.astype(full),
        out_bias_total,
    )


def solution(mesh):
    return jax.shard_map(
        body,
        mesh=mesh,
        in_specs=(
            P(("dp", "sp"), None),
            P("dp"),
            P(("dp", "sp"), None),
            P(),
            P(),
            P(("dp", "sp"), None),
            P(),
            P(("dp", "sp"), None),
            P(("dp", "sp"), None),
            P(),
            P(("dp", "sp"), None),
            P(),
        ),
        out_specs=(
            P(("dp", "sp"), None),
            P(("dp", "sp"), None),
            P(),
            P(),
            P(("dp", "sp"), None),
            P(),
            P(("dp", "sp"), None),
            P(("dp", "sp"), None),
            P(),
            P(("dp", "sp"), None),
            P(),
        ),
        check_vma=False,
    )
```

profile of v0, /device:TPU:8, one launch (start us, length us, event | category | flops | bytes accessed | tf_op | source)
XLA Modules:
  0.0 407.3 jit_solution(11496751714888004877)
XLA Ops:
  0.6 0.0 copy-start.8
  0.7 0.0 copy-start.9
  0.7 0.7 reshape.88
  1.4 0.6 convert.2.unit_bias_ref
  2.0 0.7 convert_bitcast_fusion
  2.7 0.6 copy.25
  3.3 0.6 maximum_bitcast_fusion.freq_ref
  3.9 103.1 %gather_weights.1 = (bf16[2048,1536]{1,0:T(8,128)(2,1)}, bf16[512,2048]{1,0:T(8,128)(2,1)}, bf16[2048,2048]{1,0:T(8,128)(2,1)}, bf16[1024,2048]{1,0:T(8,128)(2,1...) custom-call(bf16[64,6144]{1,0:T(8,128)(2,1)} %qkv_ref.1, bf16[64,2048]{1,0:T(8,128)(2,1)} %out_ref.1, ...), custom_call_target="tpu_custom_call" | custom-call | bytes 250000000 | tf_op jit(solution)/shard_map/gather_weights/pallas_call | solution.py:380
  107.7 0.0 copy-done.8
  107.7 0.6 convert_element_type.60.gain_ref
  108.3 0.0 copy-done.9
  108.3 0.6 convert_element_type.61.shift_ref
  109.0 78.3 %front.1 = (bf16[2048,2048]{1,0:T(8,128)(2,1)}, bf16[1024,2048]{1,0:T(8,128)(2,1)}, bf16[1024,2048]{1,0:T(8,128)(2,1)}, bf16[1024,2048]{1,0:T(8,128)(2,1)}, bf16...) custom-call(s32[1]{0:T(128)} %copy.27.len_ref, ...), custom_call_target="tpu_custom_call" | custom-call | flops 25999998976 | bytes 80000000 | tf_op jit(solution)/shard_map/front/pallas_call | solution.py:580
  187.3 94.8 %middle.1 = (bf16[256,2048]{1,0:T(8,128)(2,1)}, bf16[1024,2048]{1,0:T(8,128)(2,1)}, bf16[1024,1536]{1,0:T(8,128)(2,1)}, bf16[1024,2048]{1,0:T(8,128)(2,1)}, bf16...) custom-call(s32[1]{0:T(128)} %copy.27.len_ref, ...), custom_call_target="tpu_custom_call" | custom-call | flops 40000000000 | bytes 90000000 | tf_op jit(solution)/shard_map/middle/pallas_call | solution.py:1051
  282.1 109.7 %reduce_gradients.1 = (bf16[256,2048]{1,0:T(8,128)(2,1)}, bf16[64,6144]{1,0:T(8,128)(2,1)}, bf16[64,2048]{1,0:T(8,128)(2,1)}, bf16[256,2048]{1,0:T(8,128)(2,1)}, f32[16,2048]{1,0:T(8,128)}) custom-call(bf16[1024,2048]{1,0:T(8,128)(2,1)} %get-tuple-element.55.cot_hbm, bf16[1024,2048]{1,0:T(8,128)(2,1)} %get-tuple-element.56.pre_hbm, ...), custom_call_target="tpu_custom_call" | custom-call | flops 16999999488 | bytes 200000000 | tf_op jit(solution)/shard_map/reduce_gradients/pallas_call | solution.py:1257
  391.8 0.0 copy-start
  391.8 0.0 copy-start.1
  391.8 0.0 copy-start.10
  391.8 0.0 copy-start.4
  391.9 1.6 convert_reduce_fusion.1
  393.5 1.6 fusion.7
  395.1 0.0 copy-done
  395.1 0.0 copy-done.1
  395.1 0.7 convert_reduce_fusion
  395.9 0.0 copy-done.10
  395.9 0.0 copy-done.4
  395.9 0.0 copy-start.3
  395.9 3.7 fusion.6
  399.6 0.0 copy-start.5
  399.6 0.0 copy-done.3
  399.6 0.0 copy-start.6
  399.6 1.6 convert_element_type.74
  401.2 0.0 copy-start.7
  401.2 0.0 copy-start.2
  401.2 0.0 copy-done.5
  401.2 1.2 convert_element_type.72
  402.4 0.0 copy-done.6
  402.4 0.8 convert_element_type.73
  403.3 0.0 copy-done.7
  403.3 0.6 copy.26
  403.9 0.6 fusion.11
  404.5 0.6 slice.17
  405.1 0.6 slice.19
  405.7 0.0 copy-done.2
  405.7 1.6 convert_element_type.75
  (9 shorter events, 0.1 us)
Async XLA Ops:
  0.6 107.1 %copy-start.8 = (bf16[2,2048]{1,0:T(2,128)(2,1)S(1)}, bf16[2,2048]{1,0:T(2,128)(2,1)}, u32[]{:S(2)}) copy-start(bf16[2,2048]{1,0:T(2,128)(2,1)} %param.15) | copy-start | bytes 24580
  0.7 107.7 %copy-start.9 = (bf16[2,2048]{1,0:T(2,128)(2,1)S(1)}, bf16[2,2048]{1,0:T(2,128)(2,1)}, u32[]{:S(2)}) copy-start(bf16[2,2048]{1,0:T(2,128)(2,1)} %param.16) | copy-start | bytes 24580
  391.8 3.3 copy-start
  391.8 3.3 copy-start.1
  391.8 4.0 copy-start.10
  391.8 4.0 copy-start.4
  395.9 3.7 copy-start.3
  399.6 1.6 copy-start.5
  399.6 2.8 copy-start.6
  401.2 2.1 copy-start.7
  401.2 4.6 %copy-start.2 = (bf16[256,2048]{1,0:T(8,128)(2,1)S(1)}, bf16[256,2048]{1,0:T(8,128)(2,1)}, u32[]{:S(2)}) copy-start(bf16[256,2048]{1,0:T(8,128)(2,1)} %get-tuple-element.68) | copy-start | bytes 3145732
where the time goes:
time: 414 us; the launch traced here: 407 us
  Pallas kernels  386 us (93%)
  other arithmetic  16 us (4%)
    pallas_call x1, Pallas kernels, reduce_gradients(): pl.pallas_call(functools.partial(back_kernel, sp_size), out_shape=[shape(...  110 us
    pallas_call x1, Pallas kernels, gather_weights(): pl.pallas_call(functools.partial(gather_kernel, sp_size), out_shape=[shap...  103 us
    pallas_call x1, Pallas kernels, middle(): pl.pallas_call(functools.partial(middle_kernel, sp_size), out_shape=[shap...  94.8 us
    pallas_call x1, Pallas kernels, front(): pl.pallas_call(functools.partial(front_kernel, sp_size), out_shape=[shape...  78.3 us

commit v1 on v0

--- a/solution.py
+++ b/solution.py
@@ -177,13 +177,18 @@
         for way in (0, 1):
             self.start(way, 0)
 
-    def forward(self, step):
+    def relay(self, step):
         for way in (0, 1):
-            @pl.when(self.receives(way, step - 1))
+            @pl.when(self.receives(way, step - 1) & self.sends(way, step))
             def _():
                 self.copy(way, step - 1, self.owner(way, step), False).wait_recv()
-            if step < self.count - 1:
-                self.start(way, step)
+                self.copy(way, step, self.owner(way, step), False).start()
+
+    def settle(self, step):
+        for way in (0, 1):
+            @pl.when(self.receives(way, step - 1) & jnp.logical_not(self.sends(way, step)))
+            def _():
+                self.copy(way, step - 1, self.owner(way, step), False).wait_recv()
 
     def finish(self):
         for step in range(self.count - 1):
@@ -193,51 +198,57 @@
                     self.copy(way, step, self.owner(way, step), step == 0).wait_send()
 
 
-def gather_kernel(sp_size, qkv_ref, out_ref, up_ref, tok_ref, freq_ref, qkv_all, out_all, up_all, tok_all,
-                  cos_ref, sin_ref,
-                  send_sem, recv_sem, slab_send, slab_recv, local_sem, turn_send, turn_recv, hop_send, hop_recv):
+def front_kernel(sp_size, len_ref, qkv_ref, out_ref, up_ref, down_ref, tok_ref, cot_ref, freq_ref, gain_ref, shift_ref,
+                 qkv_bias_ref, unit_bias_ref,
+                 qkv_all, out_all, up_all, down_all, tok_all, cot_all, attn_out, mlp_out, hidden_out, pre_out, part_out,
+                 cos_ref, sin_ref, mean_ref, inv_ref, q_ref, k_ref, v_ref, ctx_ref,
+                 tok, attn, mlp, qkv_w, up_w, hidden, pre,
+                 send_sem, recv_sem, slab_send, slab_recv, keep_sem, turn_send, turn_recv, tok_send, tok_recv, cot_send, cot_recv,
+                 load_sem, store_sem, pre_sem, part_sem):
+    full, low = jnp.float32, jnp.bfloat16
     dp, sp = lax.axis_index("dp"), lax.axis_index("sp")
     first, second, diagonal, flip = square_partners(dp)
     sibling = dp + flip
     per = 2
     pair, lane = dp // per, dp % per
     rows = qkv_ref.shape[0]
-    wide = up_ref.shape[1]
+    seq, wide = tok.shape
+    own_rows = tok_ref.shape[0]
     head_width = wide // sp_size
+    units = down_ref.shape[0]
+    slab = rows * sp_size
+    width = q_ref.shape[1]
     turn_dp = sp * per + lane
+    scale = HEAD ** -0.5
+    band = 256
 
     barrier = pltpu.get_barrier_semaphore()
     for other in (first, second, sibling):
         pl.semaphore_signal(barrier, inc=1, device_id=(other, sp), device_id_type=MESH)
     for step in range(1, sp_size):
         pl.semaphore_signal(barrier, inc=1, device_id=(dp, lax.rem(sp + step, sp_size)), device_id_type=MESH)
+
     @pl.when(pair != sp)
     def _():
         pl.semaphore_signal(barrier, inc=1, device_id=(turn_dp, pair), device_id_type=MESH)
 
     pl.semaphore_wait(barrier, 2 + sp_size + jnp.where(pair != sp, 1, 0))
 
-    def slab_at(owner_sp):
-        return pl.ds(pl.multiple_of((dp * sp_size + owner_sp) * rows, rows), rows)
-
-    def slab_copy(step, part):
-        there = lax.rem(sp + step, sp_size)
+    def remote_copy(source, target, send, recv, device):
         return pltpu.make_async_remote_copy(
-            src_ref=qkv_ref.at[:, pl.ds(pl.multiple_of(part * wide + there * head_width, head_width), head_width)],
-            dst_ref=qkv_all.at[slab_at(sp), pl.ds(part * head_width, head_width)],
-            send_sem=slab_send.at[step - 1, part], recv_sem=slab_recv.at[step - 1, part],
-            device_id=(dp, there), device_id_type=MESH)
-
-    def slab_arrival(step, part):
-        origin = lax.rem(sp + sp_size - step, sp_size)
-        return pltpu.make_async_remote_copy(
-            src_ref=qkv_ref.at[:, pl.ds(part * head_width, head_width)],
-            dst_ref=qkv_all.at[slab_at(origin), pl.ds(part * head_width, head_width)],
-            send_sem=slab_send.at[step - 1, part], recv_sem=slab_recv.at[step - 1, part],
-            device_id=(dp, origin), device_id_type=MESH)
-
-    units = up_ref.shape[0]
-    slab = rows * sp_size
+            src_ref=source, dst_ref=target, send_sem=send, recv_sem=recv, device_id=device, device_id_type=MESH)
+
+    def slab_at(owner):
+        return pl.ds(pl.multiple_of((dp * sp_size + owner) * rows, rows), rows)
+
+    def slab_columns(part, there):
+        return pl.ds(pl.multiple_of(part * wide + there * head_width, head_width), head_width)
+
+    def slab_copy(step, part, there, origin):
+        return remote_copy(
+            qkv_ref.at[:, slab_columns(part, there)],
+            qkv_all.at[slab_at(origin), pl.ds(part * head_width, head_width)],
+            slab_send.at[step - 1, part], slab_recv.at[step - 1, part], (dp, there))
 
     def plain(height):
         return lambda owner: pl.ds(pl.multiple_of(owner * height, height), height)
@@ -245,18 +256,17 @@
     def turned(owner):
         return pl.ds(pl.multiple_of((owner % per) * slab + (owner // per) * rows, rows), rows)
 
-    arrays = ((up_ref, up_all, plain(units)), (None, qkv_all, plain(slab)), (None, out_all, turned))
-    hops = Hops(sp_size, dp, sp, tok_ref, tok_all, hop_send, hop_recv)
+    def turn_copy(landing):
+        return remote_copy(out_ref, out_all.at[turned(landing)], turn_send, turn_recv, (turn_dp, pair))
+
+    arrays = ((up_ref, up_all, plain(units)), (None, qkv_all, plain(slab)), (None, out_all, turned), (down_ref, down_all, plain(units)))
+    UP, QKV, OUT, DOWN = 0, 1, 2, 3
 
     def copy(index, message, block, target):
         source, result, place = arrays[index]
         at = result.at[place(block)]
-        src = at
-        if source is not None and message < 3:
-            src = source
-        return pltpu.make_async_remote_copy(
-            src_ref=src, dst_ref=at, send_sem=send_sem.at[index, message], recv_sem=recv_sem.at[index, message],
-            device_id=(target, sp), device_id_type=MESH)
+        return remote_copy(at if source is None or message > 2 else source, at,
+                           send_sem.at[index, message], recv_sem.at[index, message], (target, sp))
 
     sends = ((dp, first), (dp, second), (dp, sibling), (first, second), (first, sibling), (second, sibling), (diagonal, sibling))
     arrivals = (first, second, sibling, diagonal, second + flip, first + flip, diagonal + flip)
@@ -265,41 +275,11 @@
         copy(index, message, *sends[message]).start()
 
     def arrived(index, message):
-        copy(index, message, arrivals[message], dp).wait_recv()
+        copy(index, message, arrivals[message], sibling).wait_recv()
 
     def own(index):
         for message in (0, 1, 2):
             start(index, message)
-
-    def keep(source, target, which):
-        return pltpu.make_async_copy(source, target, local_sem.at[which])
-
-    hops.begin()
-    own(0)
-    for step in range(1, sp_size):
-        for part in range(3):
-            slab_copy(step, part).start()
-
-    out_place = out_all.at[turned(turn_dp)]
-    my_out_place = out_all.at[turned(dp)]
-    turn = pltpu.make_async_remote_copy(
-        src_ref=out_ref, dst_ref=out_place, send_sem=turn_send, recv_sem=turn_recv,
-        device_id=(turn_dp, pair), device_id_type=MESH)
-    turn_arrival = pltpu.make_async_remote_copy(
-        src_ref=out_ref, dst_ref=my_out_place, send_sem=turn_send, recv_sem=turn_recv,
-        device_id=(turn_dp, pair), device_id_type=MESH)
-
-    @pl.when(pair != sp)
-    def _():
-        turn.start()
-
-    local = [keep(tok_ref, tok_all.at[hops.place(sp)], 0), keep(up_ref, up_all.at[plain(units)(dp)], 1)]
-    for part in range(3):
-        local.append(keep(
-            qkv_ref.at[:, pl.ds(pl.multiple_of(part * wide + sp * head_width, head_width), head_width)],
-            qkv_all.at[slab_at(sp), pl.ds(part * head_width, head_width)], 2 + part))
-    for c in local:
-        c.start()
 
     def onward(index):
         arrived(index, 0)
@@ -308,161 +288,128 @@
         arrived(index, 1)
         start(index, 5)
 
+    def corner(index):
+        arrived(index, 3)
+        start(index, 6)
+
+    def complete(index):
+        for message in (2, 4, 5, 6):
+            arrived(index, message)
+
+    def load(source, target, which):
+        c = pltpu.make_async_copy(source, target, load_sem.at[which])
+        c.start()
+        return c
+
+    for step in range(1, sp_size):
+        for part in range(3):
+            slab_copy(step, part, lax.rem(sp + step, sp_size), sp).start()
+
+    @pl.when(pair != sp)
+    def _():
+        turn_copy(turn_dp).start()
+
+    own(UP)
+    tokens = Hops(sp_size, dp, sp, tok_ref, tok_all, tok_send, tok_recv)
+    cotangents = Hops(sp_size, dp, sp, cot_ref, cot_all, cot_send, cot_recv)
+    tokens.begin()
+    keeps = []
+
+    def keep(source, target):
+        c = pltpu.make_async_copy(source, target, keep_sem.at[len(keeps)])
+        c.start()
+        keeps.append(c)
+
+    for part in range(3):
+        keep(qkv_ref.at[:, slab_columns(part, sp)], qkv_all.at[slab_at(sp), pl.ds(part * head_width, head_width)])
+    keep(up_ref, up_all.at[plain(units)(dp)])
+    keep(down_ref, down_all.at[plain(units)(dp)])
+    keep(tok_ref, tok_all.at[tokens.place(sp)])
+    keep(cot_ref, cot_all.at[cotangents.place(sp)])
+
+    def normalize(source, source_start, target_start):
+        def chunk(i, carry):
+            at = pl.ds(pl.multiple_of(target_start + i * 32, 32), 32)
+            values = source[pl.ds(pl.multiple_of(source_start + i * 32, 32), 32), :].astype(full)
+            mean = jnp.mean(values, axis=-1, keepdims=True)
+            centered = values - mean
+            inverse = lax.rsqrt(jnp.mean(centered * centered, axis=-1, keepdims=True) + eps)
+            normed = centered * inverse
+            mean_ref[at, :] = jnp.broadcast_to(mean, (32, 128))
+            inv_ref[at, :] = jnp.broadcast_to(inverse, (32, 128))
+            attn[at, :] = (normed * gain_ref[0:1, :].astype(full) + shift_ref[0:1, :].astype(full)).astype(low)
+            mlp[at, :] = (normed * gain_ref[1:2, :].astype(full) + shift_ref[1:2, :].astype(full)).astype(low)
+            return carry
+        lax.fori_loop(0, own_rows // 32, chunk, 0)
+
+    def absorb(step):
+        for way in (0, 1):
+            @pl.when(tokens.receives(way, step - 1))
+            def _():
+                at = tokens.place(tokens.owner(way, step))
+                c = load(tok_all.at[at], tok.at[at], way)
+                c.wait()
+                begin = tokens.owner(way, step) * own_rows
+                normalize(tok, begin, begin)
+
     def table(i, carry):
         at = pl.ds(pl.multiple_of(i * 64, 64), 64)
-        lane = lax.broadcasted_iota(jnp.int32, (64, 128), 1)
+        lanes = lax.broadcasted_iota(jnp.int32, (64, 128), 1)
         position = i * 64 + lax.broadcasted_iota(jnp.int32, (64, 128), 0)
-        angle = position.astype(jnp.float32) * freq_ref[...]
-        turned_lane = lane < ROT
-        cos_ref[at, :] = jnp.where(turned_lane, jnp.cos(angle), 1.0)
+        angle = position.astype(full) * freq_ref[...]
+        cos_ref[at, :] = jnp.where(lanes < ROT, jnp.cos(angle), 1.0)
         sine = jnp.sin(angle)
-        sin_ref[at, :] = jnp.where(turned_lane, jnp.where(lane < ROT // 2, -sine, sine), 0.0)
+        sin_ref[at, :] = jnp.where(lanes < ROT, jnp.where(lanes < ROT // 2, -sine, sine), 0.0)
         return carry
 
-    onward(0)
-    hops.forward(1)
-    lax.fori_loop(0, cos_ref.shape[0] // 64, table, 0)
+    normalize(tok_ref, 0, sp * own_rows)
+    lax.fori_loop(0, seq // 64, table, 0)
+    for step in range(1, sp_size):
+        for part in range(3):
+            slab_copy(step, part, sp, lax.rem(sp + sp_size - step, sp_size)).wait_recv()
+    for c in keeps[:3]:
+        c.wait()
+    own(QKV)
 
     @pl.when(pair == sp)
     def _():
-        c = keep(out_ref, my_out_place, 5)
+        c = pltpu.make_async_copy(out_ref, out_all.at[turned(dp)], keep_sem.at[7])
         c.start()
         c.wait()
 
     @pl.when(pair != sp)
     def _():
-        turn_arrival.wait_recv()
-
-    own(2)
-    for step in range(1, sp_size):
-        for part in range(3):
-            slab_arrival(step, part).wait_recv()
-    for c in local:
+        turn_copy(dp).wait_recv()
+
+    own(OUT)
+    onward(UP)
+    tokens.relay(1)
+    onward(QKV)
+    onward(OUT)
+    own(DOWN)
+    tokens.settle(1)
+    absorb(1)
+    tokens.relay(2)
+    cotangents.begin()
+    corner(UP)
+    complete(UP)
+    for c in keeps[3:]:
         c.wait()
-    own(1)
-    arrived(0, 3)
-    start(0, 6)
-    onward(2)
-    hops.forward(2)
-    onward(1)
-    for index in (2, 1):
-        arrived(index, 3)
-        start(index, 6)
-    hops.forward(3)
-    for index in range(3):
-        for message in (2, 4, 5, 6):
-            arrived(index, message)
-    for index in range(3):
-        for message in range(7):
-            copy(index, message, *sends[message]).wait_send()
-    for step in range(1, sp_size):
-        for part in range(3):
-            slab_copy(step, part).wait_send()
-
-    @pl.when(pair != sp)
-    def _():
-        turn.wait_send()
-
-    hops.finish()
-
-def gather_weights(dp_size, sp_size, qkv_weight, out_weight, up_weight, tokens):
-    rows, wide = out_weight.shape
-    units = up_weight.shape[0]
-    seq = tokens.shape[0] * sp_size
-    low = jnp.bfloat16
-    half = ROT // 2
-    freq = base_freq ** (-jnp.arange(half, dtype=jnp.float32) * (2.0 / ROT))
-    freq = jnp.concatenate([freq, freq, jnp.zeros((128 - ROT,), jnp.float32)])[None]
-    hbm = pl.BlockSpec(memory_space=pltpu.HBM)
-    vmem = pl.BlockSpec(memory_space=pltpu.VMEM)
-    dma = pltpu.SemaphoreType.DMA
-    shape = jax.ShapeDtypeStruct
-    return pl.pallas_call(
-        functools.partial(gather_kernel, sp_size),
-        out_shape=[shape((rows * sp_size * dp_size, 3 * wide // sp_size), low),
-                   shape((rows * dp_size, wide), low),
-                   shape((units * dp_size, wide), low),
-                   shape((seq, wide), low),
-                   shape((seq, 128), jnp.float32), shape((seq, 128), jnp.float32)],
-        in_specs=[vmem] * 5, out_specs=[hbm] * 4 + [vmem] * 2,
-        scratch_shapes=[dma((3, 7)), dma((3, 7)), dma((sp_size - 1, 3)), dma((sp_size - 1, 3)), dma((6,)), dma, dma,
-                        dma((2, sp_size)), dma((2, sp_size))],
-        compiler_params=pltpu.CompilerParams(collective_id=0, has_side_effects=True),
-        cost_estimate=pl.CostEstimate(flops=0, bytes_accessed=250 * 1000 * 1000, transcendentals=0),
-        name="gather_weights",
-    )(qkv_weight, out_weight, up_weight, tokens, freq)
-
-def front_kernel(sp_size, len_ref, tok_hbm, qkv_hbm, up_hbm, out_hbm, down_ref, cot_ref, gain_ref, shift_ref, qkv_bias_ref, unit_bias_ref,
-                 cos_ref, sin_ref,
-                 down_all, cot_all, attn_out, mlp_out, hidden_out, pre_out, part_out, q_ref, k_ref, v_ref, ctx_ref,
-                 tok, attn, mlp, qkv_w, up_w, hidden, pre,
-                 send_sem, recv_sem, load_sem, store_sem, pre_sem, keep_sem, part_sem, hop_send, hop_recv):
-    full, low = jnp.float32, jnp.bfloat16
-    dp, sp = lax.axis_index("dp"), lax.axis_index("sp")
-    first, second, diagonal, flip = square_partners(dp)
-    sibling = dp + flip
-    seq, wide = tok.shape
-    units = down_ref.shape[0]
-    width = q_ref.shape[1]
-    scale = HEAD ** -0.5
-    band = 256
-
-    def load(source, target, which):
-        return pltpu.make_async_copy(source, target, load_sem.at[which])
-
-    token_loads = [load(tok_hbm.at[pl.ds(r, band)], tok.at[pl.ds(r, band)], r // band) for r in range(0, seq, band)]
-    loads = token_loads + [load(qkv_hbm, qkv_w, seq // band), load(up_hbm, up_w, seq // band + 1)]
-    for c in loads:
-        c.start()
-
-    barrier = pltpu.get_barrier_semaphore()
-    for other in (first, second, sibling):
-        pl.semaphore_signal(barrier, inc=1, device_id=(other, sp), device_id_type=MESH)
-    for step in range(1, sp_size):
-        pl.semaphore_signal(barrier, inc=1, device_id=(dp, lax.rem(sp + step, sp_size)), device_id_type=MESH)
-    pl.semaphore_wait(barrier, 2 + sp_size)
-
-    sends = ((dp, first), (dp, second), (dp, sibling), (first, second), (first, sibling), (second, sibling), (diagonal, sibling))
-    arrivals = (first, second, sibling, diagonal, second + flip, first + flip, diagonal + flip)
-
-    def copy(message, block, target):
-        at = down_all.at[pl.ds(pl.multiple_of(block * units, units), units)]
-        return pltpu.make_async_remote_copy(
-            src_ref=down_ref if message < 3 else at, dst_ref=at,
-            send_sem=send_sem.at[message], recv_sem=recv_sem.at[message],
-            device_id=(target, sp), device_id_type=MESH)
-
-    def start(message):
-        copy(message, *sends[message]).start()
-
-    def arrived(message):
-        copy(message, arrivals[message], sibling).wait_recv()
-
-    hops = Hops(sp_size, dp, sp, cot_ref, cot_all, hop_send, hop_recv)
-    hops.begin()
-    for message in (0, 1, 2):
-        start(message)
-    keeps = [pltpu.make_async_copy(down_ref, down_all.at[pl.ds(pl.multiple_of(dp * units, units), units)], keep_sem.at[0]),
-             pltpu.make_async_copy(cot_ref, cot_all.at[hops.place(sp)], keep_sem.at[1])]
-    for c in keeps:
-        c.start()
-
-    def normalize(i, carry):
-        at = pl.ds(pl.multiple_of(i * 32, 32), 32)
-        rows = tok[at, :].astype(full)
-        centered = rows - jnp.mean(rows, axis=-1, keepdims=True)
-        normed = centered * lax.rsqrt(jnp.mean(centered * centered, axis=-1, keepdims=True) + eps)
-        attn[at, :] = (normed * gain_ref[0:1, :] + shift_ref[0:1, :]).astype(low)
-        mlp[at, :] = (normed * gain_ref[1:2, :] + shift_ref[1:2, :]).astype(low)
-        return carry
-
-    for part, c in enumerate(token_loads):
-        c.wait()
-        lax.fori_loop(part * band // 32, (part + 1) * band // 32, normalize, 0)
+    up_load = load(up_all, up_w, 2)
+    tokens.settle(2)
+    absorb(2)
+    corner(QKV)
+    corner(OUT)
+    complete(QKV)
+    qkv_load = load(qkv_all, qkv_w, 3)
+    complete(OUT)
+    onward(DOWN)
+    tokens.settle(3)
+    absorb(3)
     stores = [pltpu.make_async_copy(attn, attn_out, store_sem.at[0]), pltpu.make_async_copy(mlp, mlp_out, store_sem.at[1])]
     for c in stores:
         c.start()
-    loads[-2].wait()
+    qkv_load.wait()
 
     def head(h, carry):
         lanes = pl.ds(pl.multiple_of(h * HEAD, HEAD), HEAD)
@@ -485,13 +432,9 @@
         return carry
 
     lax.fori_loop(0, width // HEAD, head, 0)
-    arrived(0)
-    start(3)
-    start(4)
-    arrived(1)
-    start(5)
-    hops.forward(1)
-    loads[-1].wait()
+    corner(DOWN)
+    cotangents.relay(1)
+    up_load.wait()
 
     def pre_store(block, slot):
         return pltpu.make_async_copy(pre.at[slot], pre_out.at[:, pl.ds(pl.multiple_of(block * units, units), units)],
@@ -519,24 +462,19 @@
 
     blocks = up_w.shape[0] // units
     lax.fori_loop(0, blocks // 2, unit_block, 0)
-    arrived(3)
-    start(6)
+    complete(DOWN)
+    half = up_w.shape[0] // 2
+    stores[0].wait()
+    late = [load(down_all.at[pl.ds(0, half)], tok, 0), load(down_all.at[pl.ds(half, half)], attn, 1)]
     lax.fori_loop(blocks // 2, blocks, unit_block, 0)
+    out_rows = out_all.shape[0]
+    late.append(load(out_all, up_w.at[pl.ds(0, out_rows)], 2))
+    cotangents.relay(2)
     for block in (blocks - 2, blocks - 1):
         pre_store(block, block % 2).wait()
-    for c in stores + keeps:
-        c.wait()
+    stores[1].wait()
     hidden_store = pltpu.make_async_copy(hidden, hidden_out, store_sem.at[0])
     hidden_store.start()
-    for message in (2, 4, 5, 6):
-        arrived(message)
-    half = up_w.shape[0] // 2
-    out_rows = out_hbm.shape[0]
-    late = [load(down_all.at[pl.ds(0, half)], tok, 0), load(down_all.at[pl.ds(half, half)], attn, 1),
-            load(out_hbm, up_w.at[pl.ds(0, out_rows)], 2)]
-    for c in late:
-        c.start()
-    hops.forward(2)
     for c in late:
         c.wait()
 
@@ -558,41 +496,61 @@
         part_store(r).start()
         return carry
     lax.fori_loop(0, seq // band, out_band, 0)
-    hops.forward(3)
     for r in range(seq // band):
         part_store(r).wait()
     hidden_store.wait()
-    for message in range(7):
-        copy(message, *sends[message]).wait_send()
-    hops.finish()
-
-def front(sp_size, tokens, qkv_own, up_own, out_own, down_weight, cotangent, gains, shifts, qkv_bias, unit_bias, cos_t, sin_t,
-          lengths, dp_size):
-    seq, wide = tokens.shape
-    units = down_weight.shape[0]
-    width = qkv_own.shape[1] // 3
-    all_units = up_own.shape[0]
+    for index in range(4):
+        for message in range(7):
+            copy(index, message, *sends[message]).wait_send()
+    for step in range(1, sp_size):
+        for part in range(3):
+            slab_copy(step, part, lax.rem(sp + step, sp_size), sp).wait_send()
+
+    @pl.when(pair != sp)
+    def _():
+        turn_copy(turn_dp).wait_send()
+
+    tokens.finish()
+    for step in (1, 2, 3):
+        cotangents.settle(step)
+    cotangents.finish()
+
+
+def front(sp_size, dp_size, lengths, qkv_weight, out_weight, up_weight, down_weight, tokens, cotangent, gains, shifts, qkv_bias,
+          unit_bias):
+    rows, wide = out_weight.shape
+    units = up_weight.shape[0]
+    seq = tokens.shape[0] * sp_size
+    width = wide // sp_size
+    all_units = units * dp_size
     full, low = jnp.float32, jnp.bfloat16
+    half = ROT // 2
+    freq = base_freq ** (-jnp.arange(half, dtype=full) * (2.0 / ROT))
+    freq = jnp.concatenate([freq, freq, jnp.zeros((128 - ROT,), full)])[None]
     hbm = pl.BlockSpec(memory_space=pltpu.HBM)
     vmem = pl.BlockSpec(memory_space=pltpu.VMEM)
     dma = pltpu.SemaphoreType.DMA
     shape = jax.ShapeDtypeStruct
+    qkv_shape = (rows * sp_size * dp_size, 3 * width)
     return pl.pallas_call(
         functools.partial(front_kernel, sp_size),
-        out_shape=[shape((units * dp_size, wide), low), shape((seq, wide), low), shape((seq, wide), low), shape((seq, wide), low),
-                   shape((seq, all_units), low), shape((seq, all_units), full), shape((seq, wide), low)]
-        + [shape((seq, width), low)] * 4,
-        in_specs=[pl.BlockSpec(memory_space=pltpu.SMEM), hbm, hbm, hbm, hbm] + [vmem] * 8,
-        out_specs=[hbm] * 7 + [vmem] * 4,
+        out_shape=[shape(qkv_shape, low), shape((rows * dp_size, wide), low), shape((all_units, wide), low),
+                   shape((all_units, wide), low), shape((seq, wide), low), shape((seq, wide), low),
+                   shape((seq, wide), low), shape((seq, wide), low), shape((seq, all_units), low), shape((seq, all_units), full),
+                   shape((seq, wide), low)]
+        + [shape((seq, 128), full)] * 4 + [shape((seq, width), low)] * 4,
+        in_specs=[pl.BlockSpec(memory_space=pltpu.SMEM)] + [vmem] * 11,
+        out_specs=[hbm] * 11 + [vmem] * 8,
         scratch_shapes=[pltpu.VMEM((seq, wide), low)] * 3 + [
-            pltpu.VMEM(qkv_own.shape, low), pltpu.VMEM(up_own.shape, low),
+            pltpu.VMEM(qkv_shape, low), pltpu.VMEM((all_units, wide), low),
             pltpu.VMEM((seq, all_units), low), pltpu.VMEM((2, seq, units), full),
-            dma((7,)), dma((7,)), dma((seq // 256 + 2,)), dma((2,)), dma((2,)), dma((2,)), dma((seq // 256,)),
-            dma((2, sp_size)), dma((2, sp_size))],
-        compiler_params=pltpu.CompilerParams(collective_id=2, has_side_effects=True, vmem_limit_bytes=60 << 20),
-        cost_estimate=pl.CostEstimate(flops=26 * 10 ** 9, bytes_accessed=80 * 1000 * 1000, transcendentals=0),
+            dma((4, 7)), dma((4, 7)), dma((sp_size - 1, 3)), dma((sp_size - 1, 3)), dma((8,)), dma, dma,
+            dma((2, sp_size)), dma((2, sp_size)), dma((2, sp_size)), dma((2, sp_size)),
+            dma((4,)), dma((2,)), dma((2,)), dma((seq // 256,))],
+        compiler_params=pltpu.CompilerParams(collective_id=0, has_side_effects=True, vmem_limit_bytes=62 << 20),
+        cost_estimate=pl.CostEstimate(flops=26 * 10 ** 9, bytes_accessed=300 * 1000 * 1000, transcendentals=0),
         name="front",
-    )(lengths, tokens, qkv_own, up_own, out_own, down_weight, cotangent, gains, shifts, qkv_bias, unit_bias, cos_t, sin_t)
+    )(lengths, qkv_weight, out_weight, up_weight, down_weight, tokens, cotangent, freq, gains, shifts, qkv_bias, unit_bias)
 
 CHUNK = 512
 
@@ -760,7 +718,8 @@
 
 
 class Fold:
-    def __init__(self, place, source, inbox, stage, stage_sem, send, recv):
+    def __init__(self, place, source, inbox, stage, stage_sem, send, recv, begun=1):
+        self.begun = begun
         self.place, self.source, self.inbox, self.stage = place, source, inbox, stage
         self.stage_sem, self.send, self.recv = stage_sem, send, recv
         self.rows = stage.shape[0]
@@ -790,16 +749,17 @@
     def step(self, step):
         last = self.place.sp_size - 1
         for way in (0, 1):
-            if step == 1:
+            if step >= self.begun:
                 @pl.when(self.along(way) == 0)
                 def _():
-                    for early in range(1, last + 1):
-                        self.copy(way, early, True).start()
-            else:
+                    self.copy(way, step, True).start()
+
+            if step > 1:
                 @pl.when((self.along(way) > 0) & (self.along(way) < step) & (self.along(way) < last))
                 def _():
                     self.take(self.rows_of(way, step))
-                    self.copy(way, step - 1, False).wait_recv()
+                    if step > self.begun:
+                        self.copy(way, step - 1, False).wait_recv()
                     add_into(self.inbox.at[way, step - 2], self.stage)
                     self.copy(way, step, False).start()
 
@@ -816,9 +776,10 @@
         last = self.place.sp_size - 1
         for way in (0, 1):
             for step in range(1, last + 1):
-                @pl.when(self.along(way) == 0)
-                def _():
-                    self.copy(way, step, True).wait_send()
+                if step >= self.begun:
+                    @pl.when(self.along(way) == 0)
+                    def _():
+                        self.copy(way, step, True).wait_send()
 
                 if step > 1:
                     @pl.when((self.along(way) > 0) & (self.along(way) < step) & (self.along(way) < last))
@@ -827,12 +788,12 @@
 
 
 def middle_kernel(sp_size, len_ref, cot_hbm, out_hbm, q_hbm, k_hbm, v_hbm, pre_hbm, hidden_hbm, down_hbm, up_hbm, qkv_hbm,
-                  tok_hbm, part_hbm, gain_ref, cos_ref, sin_ref,
-                  down_out, hat_out, proj_out, gpre_out, gout_out, red_out, small_ref,
-                  cot, left, gpre, up_w, qkv_w, pre, gctx, gproj, dq, dk, dv, mean_s, inv_s,
+                  tok_hbm, part_hbm, mlp_hbm, gain_ref, cos_ref, sin_ref, mean_s, inv_s,
+                  down_out, up_out, hat_out, hat_in, proj_out, gout_out, red_out, small_ref,
+                  cot, left, gpre, up_w, qkv_w, pre, gctx, gproj, dq, dk, dv,
                   lent, down_sum, down_sib, down_one, down_two, inbox, stage,
                   load_sem, stream_sem, store_sem, stage_sem, sib_send, sib_recv, one_send, one_recv, two_send, two_recv,
-                  fold_send, fold_recv):
+                  fold_send, fold_recv, hat_send, hat_recv, sib_free, one_free):
     full, low = jnp.float32, jnp.bfloat16
     place = Square(sp_size, lent, sib_send, sib_recv, one_send, one_recv, two_send, two_recv)
     seq, wide = cot.shape
@@ -905,6 +866,8 @@
         return carry
     lax.fori_loop(0, bands, context_band, 0)
     down.for_self()
+    mlp_load = load(mlp_hbm, left, 1)
+    pl.semaphore_signal(sib_free, inc=1, device_id=(place.sibling, place.sp), device_id_type=MESH)
     fold.step(2)
     for c in early[3:]:
         c.wait()
@@ -970,36 +933,43 @@
             pre_load(block + 2, slot).start()
         return carry
 
-    lax.fori_loop(0, blocks // 2, unit_block, 0)
+    down.onward()
+    lax.fori_loop(0, 3 * blocks // 4, unit_block, 0)
     fold.step(3)
-    down.onward()
+    lax.fori_loop(3 * blocks // 4, blocks, unit_block, 0)
+    up_load = load(up_hbm, up_w, 0)
+    down.finish()
+    stores.append(pltpu.make_async_copy(down.block(0), down_out, store_sem.at[3 + bands]))
+    stores[2].start()
+    pl.semaphore_signal(one_free, inc=1, device_id=(place.first, place.sp), device_id_type=MESH)
+    up = Wide(place, 1, gpre, left, wide, down_sum, down_sib, down_one, down_two)
+    mlp_load.wait()
+    pl.semaphore_wait(sib_free, 1)
+    up.for_sibling(down)
+    down.drain()
+    stores[2].wait()
+    pl.semaphore_wait(one_free, 1)
+    up.for_self()
     tok_load = load(tok_hbm, left, 1)
-    lax.fori_loop(blocks // 2, blocks, unit_block, 0)
-    up_load = load(up_hbm, up_w, 0)
-    stores.append(pltpu.make_async_copy(gpre, gpre_out, store_sem.at[2]))
-    stores[2].start()
     tok_load.wait()
-
-    def statistics(i, carry):
-        at = pl.ds(pl.multiple_of(i * 32, 32), 32)
-        rows = left[at, :].astype(full)
-        mean = jnp.mean(rows, axis=-1, keepdims=True)
-        centered = rows - mean
-        inverse = lax.rsqrt(jnp.mean(centered * centered, axis=-1, keepdims=True) + eps)
-        mean_s[at, :] = jnp.broadcast_to(mean, (32, 128))
-        inv_s[at, :] = jnp.broadcast_to(inverse, (32, 128))
-        return carry
-    lax.fori_loop(0, seq // 32, statistics, 0)
     stores[0].wait()
     qkv_load.wait()
     up_load.wait()
 
+    upper = 2 * place.sp // sp_size
+
+    def hat_rows(r):
+        return pl.ds(pl.multiple_of(((1 - upper) * (bands - 1 - r) + upper * r) * band, band), band)
+
     def hat_store(r):
-        at = pl.ds(pl.multiple_of(r * band, band), band)
-        return pltpu.make_async_copy(cot.at[at], hat_out.at[at], store_sem.at[3 + r])
-
-    def hat_band(r):
-        at = pl.ds(r * band, band)
+        return pltpu.make_async_copy(cot.at[hat_rows(r)], hat_out.at[hat_rows(r)], store_sem.at[3 + r])
+
+    def hat_hop(way):
+        to = lax.rem(place.sp + (1 if way == 0 else sp_size - 1), sp_size)
+        return remote(cot.at[hat_rows(0)], hat_in.at[way], hat_send.at[way], hat_recv.at[way], (place.dp, to))
+
+    def hat_band(r, carry):
+        at = hat_rows(r)
 
         def columns(c, carry):
             to = pl.ds(pl.multiple_of(c * band, band), band)
@@ -1010,31 +980,47 @@
             small_ref[gain_row + 1:gain_row + 2, to] += jnp.sum(from_mlp * normed, axis=0, keepdims=True)
             small_ref[shift_row:shift_row + 1, to] += jnp.sum(from_attn, axis=0, keepdims=True)
             small_ref[shift_row + 1:shift_row + 2, to] += jnp.sum(from_mlp, axis=0, keepdims=True)
-            cot[at, to] = (from_attn * gain_ref[0:1, to] + from_mlp * gain_ref[1:2, to]).astype(low)
+            cot[at, to] = (from_attn * gain_ref[0:1, to].astype(full) + from_mlp * gain_ref[1:2, to].astype(full)).astype(low)
             return carry
         lax.fori_loop(0, wide // band, columns, 0)
         hat_store(r).start()
-
-    for r in range(bands):
-        hat_band(r)
+        return carry
+
+    hat_band(0, 0)
+    for way in (0, 1):
+        @pl.when(fold.along(way) == 0)
+        def _():
+            hat_hop(way).start()
+    lax.fori_loop(1, bands, hat_band, 0)
     fold.finish()
-    stores.append(pltpu.make_async_copy(stage, red_out, store_sem.at[3 + bands]))
+    stores.append(pltpu.make_async_copy(stage, red_out, store_sem.at[4 + bands]))
     stores[-1].start()
-    down.finish()
-    stores.append(pltpu.make_async_copy(down.block(0), down_out, store_sem.at[4 + bands]))
-    stores[-1].start()
+    for slot, mask in enumerate((place.second_mask, 0)):
+        up.first_copy(slot).wait_recv()
+        add_into(up.block(mask), up.one.at[slot])
+        stores.append(pltpu.make_async_copy(up.block(mask), up_out.at[slot], store_sem.at[5 + bands + slot]))
+        stores[-1].start()
     for r in range(bands):
         hat_store(r).wait()
-    for c in stores[1:]:
-        c.wait()
+    for which in (1, 3, 4, 5):
+        stores[which].wait()
     for slot in range(4):
-        down.sib_copy(slot).wait_send()
-    down.drain()
+        up.sib_copy(slot).wait_send()
+    for slot in (0, 1):
+        up.first_copy(slot).wait_send()
     fold.drain()
+    for way in (0, 1):
+        @pl.when(fold.along(way) == 0)
+        def _():
+            hat_hop(way).wait_send()
+
+        @pl.when(fold.along(way) == 1)
+        def _():
+            hat_hop(way).wait_recv()
 
 
 def middle(sp_size, dp_size, lengths, cotangent, out_own, queries, key_rows, values, pre_act, hidden, down_own, up_own, qkv_own,
-           tokens, partial_out, gains, cos_t, sin_t):
+           tokens, partial_out, mlp_in, gains, cos_t, sin_t, means, inverses):
     seq, wide = tokens.shape
     width = queries.shape[1]
     units = up_own.shape[0] // dp_size
@@ -1050,32 +1036,34 @@
     bands = seq // 256
     return pl.pallas_call(
         functools.partial(middle_kernel, sp_size),
-        out_shape=[shape((units, wide), low), shape((seq, wide), low), shape((seq, 3 * width), low), shape(hidden.shape, low),
+        out_shape=[shape((units, wide), low), shape((2, units, wide), low), shape((seq, wide), low), shape((2, own, wide), low),
+                   shape((seq, 3 * width), low),
                    shape((seq, wide), low), shape((own, wide), low), shape((16, wide), full)],
-        in_specs=[pl.BlockSpec(memory_space=pltpu.SMEM)] + [hbm] * 12 + [vmem] * 3,
-        out_specs=[hbm] * 6 + [vmem],
+        in_specs=[pl.BlockSpec(memory_space=pltpu.SMEM)] + [hbm] * 13 + [vmem] * 5,
+        out_specs=[hbm] * 7 + [vmem],
         scratch_shapes=[
             v(seq, wide), v(seq, wide), v(*hidden.shape), v(*up_own.shape), v(*qkv_own.shape), v(2, seq, units, kind=full),
             v(seq, width), v(seq, 3 * width), v(seq, HEAD, kind=full), v(seq, HEAD, kind=full), v(seq, HEAD, kind=full),
-            v(seq, 128, kind=full), v(seq, 128, kind=full),
             v(4, units, wide), v(4, units, wide), v(4, units, wide), v(2, units, wide), v(units, wide),
             v(2, sp_size - 1, own, wide), v(own, wide),
-            dma((6,)), dma((2, 2)), dma((5 + bands,)), dma, dma((1, 4)), dma((1, 4)), dma((1, 2)), dma((1, 2)), dma((1,)), dma((1,)),
-            dma((2, sp_size - 1)), dma((2, sp_size - 1))],
+            dma((6,)), dma((2, 2)), dma((7 + bands,)), dma, dma((2, 4)), dma((2, 4)), dma((2, 2)), dma((2, 2)), dma((2,)), dma((2,)),
+            dma((2, sp_size - 1)), dma((2, sp_size - 1)), dma((2,)), dma((2,)),
+            pltpu.SemaphoreType.REGULAR, pltpu.SemaphoreType.REGULAR],
         compiler_params=pltpu.CompilerParams(collective_id=3, has_side_effects=True, vmem_limit_bytes=67043328),
         cost_estimate=pl.CostEstimate(flops=40 * 10 ** 9, bytes_accessed=90 * 1000 * 1000, transcendentals=0),
         name="middle",
     )(lengths, cotangent, out_own, queries, key_rows, values, pre_act, hidden, down_own, up_own, qkv_own, tokens, partial_out,
-      gains, cos_t, sin_t)
-
-
-def back_kernel(sp_size, cot_hbm, pre_hbm, mlp_hbm, attn_hbm, proj_hbm, ctx_hbm, hat_hbm, small_ref,
+      mlp_in, gains, cos_t, sin_t, means, inverses)
+
+
+def back_kernel(sp_size, cot_hbm, attn_hbm, proj_hbm, ctx_hbm, hat_hbm, hop_hbm, up_hbm, small_ref,
                 up_out, qkv_out, dense_out, red_out, small_out,
-                left_a, right_a, left_b, right_b, ctx, lent,
-                up_sum, qkv_sum, dense_sum, up_sib, qkv_sib, dense_sib, up_one, qkv_one, dense_one, up_two, qkv_two, dense_two,
-                dense_part, small_acc, small_in, small_z, inbox, stage,
+                left, right, cot, ctx, lent,
+                qkv_sum, dense_sum, qkv_sib, dense_sib, qkv_one, dense_one, qkv_two, dense_two,
+                dense_part, up_room, up_two, small_acc, small_in, small_z, inbox, stage,
                 load_sem, store_sem, stage_sem, sib_send, sib_recv, one_send, one_recv, two_send, two_recv,
-                slab_send, slab_recv, turn_send, turn_recv, small_send, small_recv, z_send, z_recv, fold_send, fold_recv):
+                slab_send, slab_recv, turn_send, turn_recv, up_send, up_recv, small_send, small_recv, z_send, z_recv,
+                fold_send, fold_recv):
     place = Square(sp_size, lent, sib_send, sib_recv, one_send, one_recv, two_send, two_recv)
     dp, sp = place.dp, place.sp
     per = 2
@@ -1084,15 +1072,16 @@
     slab_width = qkv_sum.shape[2]
     head_width = slab_width // 3
     rows = dense_one.shape[1]
-    wide = left_b.shape[1]
+    wide = left.shape[1]
 
     def load(source, target, which):
         c = pltpu.make_async_copy(source, target, load_sem.at[which])
         c.start()
         return c
 
-    loads = [load(attn_hbm, left_a, 0), load(proj_hbm, right_a, 1), load(cot_hbm, right_b, 2), load(ctx_hbm, ctx, 3),
-             load(pre_hbm, left_b, 4)]
+    up_load = load(up_hbm, up_room, 0)
+    hops = [load(hop_hbm.at[way], inbox.at[way, 0], 1 + way) for way in (0, 1)]
+    loads = [load(ctx_hbm, ctx, 3), load(cot_hbm, cot, 4), load(attn_hbm, left, 5), load(proj_hbm, right, 6)]
 
     barrier = pltpu.get_barrier_semaphore()
     place.greet(barrier)
@@ -1102,8 +1091,7 @@
         pl.semaphore_signal(barrier, inc=1, device_id=(turn_dp, pair), device_id_type=MESH)
 
     pl.semaphore_wait(barrier, 2 + sp_size + jnp.where(pair != sp, 1, 0))
-    fold = Fold(place, hat_hbm, inbox, stage, stage_sem, fold_send, fold_recv)
-    fold.step(1)
+    fold = Fold(place, hat_hbm, inbox, stage, stage_sem, fold_send, fold_recv, begun=2)
 
     def small_copy(stage_of):
         partner = (place.sibling, place.across_x, place.across_y)[stage_of]
@@ -1123,10 +1111,8 @@
         origin = lax.rem(sp + sp_size - step, sp_size)
         return remote(small_acc.at[2], small_z.at[origin], z_send.at[step - 1], z_recv.at[step - 1], (dp, origin))
 
-    small_copy(0).start()
-    qkv = Wide(place, 0, left_a, right_a, slab_width, qkv_sum, qkv_sib, qkv_one, qkv_two)
-    dense = Dense(place, 1, ctx, right_b, wide, dense_sum, dense_sib, dense_one, dense_two, dense_part)
-    up = Wide(place, 2, left_b, right_b, wide, up_sum, up_sib, up_one, up_two)
+    def up_copy():
+        return remote(up_room.at[0], up_two, up_send, up_recv, (place.second, sp))
 
     def turn_copy():
         return remote(dense.block(0), dense_out, turn_send, turn_recv, (turn_dp, pair))
@@ -1149,89 +1135,91 @@
         c.start()
         stores.append(c)
 
+    small_copy(0).start()
+    up_load.wait()
+    up_copy().start()
+    dense = Dense(place, 0, ctx, cot, wide, dense_sum, dense_sib, dense_one, dense_two, dense_part)
+    qkv = Wide(place, 1, left, right, slab_width, qkv_sum, qkv_sib, qkv_one, qkv_two)
+    for way in (0, 1):
+        hops[way].wait()
+    fold.step(2)
+    small_step(0)
+    small_copy(1).start()
     loads[0].wait()
     loads[1].wait()
-    qkv.for_sibling(None)
-    small_step(0)
-    small_copy(1).start()
-    qkv.for_self()
+    dense.for_sibling(None)
     loads[2].wait()
     loads[3].wait()
-    dense.for_sibling(None)
+    qkv.for_sibling(None)
     small_step(1)
     small_copy(2).start()
     dense.for_self()
-    late = load(mlp_hbm, right_b, 2)
-    fold.step(2)
-    loads[4].wait()
-    late.wait()
-    up.for_sibling(qkv)
-    qkv.onward()
+    qkv.for_self()
     small_step(2)
     for step in range(1, sp_size):
         z_copy(step).start()
     small_z[sp] = small_acc[2]
-    up.for_self()
+    fold.step(3)
     dense.onward()
+    qkv.onward()
+    dense.finish()
+
+    @pl.when(pair != sp)
+    def _():
+        turn_copy().start()
+
+    @pl.when(pair == sp)
+    def _():
+        c = pltpu.make_async_copy(dense.block(0), dense_out, store_sem.at[5])
+        c.start()
+        c.wait()
+
     qkv.finish()
     for step in range(1, sp_size):
         for part in range(3):
             slab_copy(step, part, sp, lax.rem(sp + step, sp_size)).start()
     for part in range(3):
         store(qkv_sum.at[0, slab_rows(sp), pl.ds(part * head_width, head_width)], qkv_out.at[:, slab_columns(part, sp)])
-    fold.step(3)
-    dense.finish()
-
-    @pl.when(pair != sp)
-    def _():
-        turn_copy().start()
-
-    @pl.when(pair == sp)
-    def _():
-        c = pltpu.make_async_copy(dense.block(0), dense_out, store_sem.at[5])
-        c.start()
-        c.wait()
-
+    up_copy().wait_recv()
+    add_into(up_room.at[1], up_two)
+    store(up_room.at[1], up_out)
     for step in range(1, sp_size):
         z_arrival(step).wait_recv()
     total = small_z[0]
     for origin in range(1, sp_size):
         total = total + small_z[origin]
     small_out[...] = total
-    up.onward()
+    fold.finish()
+    store(stage, red_out)
+    for slot in range(4):
+        qkv.sib_copy(slot).wait_send()
+    dense.sib_copy(0).wait_send()
+    for array in (dense, qkv):
+        array.drain()
+    up_copy().wait_send()
+    for stage_of in range(3):
+        small_copy(stage_of).wait_send()
+    fold.drain()
     for step in range(1, sp_size):
+        z_copy(step).wait_send()
         for part in range(3):
             slab_copy(step, part, lax.rem(sp + sp_size - step, sp_size), sp).wait_recv()
+            slab_copy(step, part, sp, lax.rem(sp + step, sp_size)).wait_send()
 
     @pl.when(pair != sp)
     def _():
         turn_copy().wait_recv()
         turn_copy().wait_send()
 
-    for slot in range(4):
-        up.sib_copy(slot).wait_send()
-    dense.sib_copy(0).wait_send()
-    fold.finish()
-    store(stage, red_out)
-    for array in (qkv, dense, up):
-        array.drain()
-    for stage_of in range(3):
-        small_copy(stage_of).wait_send()
-    for step in range(1, sp_size):
-        z_copy(step).wait_send()
-        for part in range(3):
-            slab_copy(step, part, sp, lax.rem(sp + step, sp_size)).wait_send()
-    fold.drain()
-    up.finish()
-    store(up.block(0), up_out)
     for c in stores:
         c.wait()
 
 
-def reduce_gradients(sp_size, rows, grad_out, grad_pre, mlp_in, attn_in, grad_proj, context, grad_hat, small):
-    seq, wide = mlp_in.shape
+def reduce_gradients(sp_size, rows, grad_out, attn_in, grad_proj, context, grad_hat, hat_hop, up_sums, small):
+    seq, wide = attn_in.shape
     slab_width = grad_proj.shape[1]
-    units = 4 * rows
+    units = up_sums.shape[1]
+    slab = 4 * rows
     own = seq // sp_size
     full, low = jnp.float32, jnp.bfloat16
     hbm = pl.BlockSpec(memory_space=pltpu.HBM)
@@ -1242,17 +1230,15 @@
     def v(*dims, kind=low):
         return pltpu.VMEM(dims, kind)
     scratch = [
-        v(seq, wide), v(seq, slab_width), v(seq, wide), v(seq, wide), v(seq, context.shape[1]), v(4, units, wide),
-        v(4, units, wide), v(4, units, slab_width), v(4 * rows, wide),
-        v(4, units, wide), v(4, units, slab_width), v(4 * rows, wide),
-        v(2, units, wide), v(2, units, slab_width), v(2, rows, wide),
-        v(units, wide), v(units, slab_width), v(rows, wide),
-        v(4 * rows, wide),
+        v(seq, wide), v(seq, slab_width), v(seq, wide), v(seq, context.shape[1]), v(4, slab, slab_width),
+        v(4, slab, slab_width), v(slab, wide), v(4, slab, slab_width), v(slab, wide),
+        v(2, slab, slab_width), v(2, rows, wide), v(slab, slab_width), v(rows, wide),
+        v(slab, wide), v(2, units, wide), v(units, wide),
         v(3, *small.shape, kind=full), v(3, *small.shape, kind=full), v(sp_size, *small.shape, kind=full),
         v(2, sp_size - 1, own, wide), v(own, wide),
-        dma((5,)), dma((6,)), dma, dma((3, 4)), dma((3, 4)), dma((3, 2)), dma((3, 2)), dma((3,)), dma((3,)),
-        dma((sp_size - 1, 3)), dma((sp_size - 1, 3)), dma, dma, dma((3,)), dma((3,)), dma((sp_size - 1,)), dma((sp_size - 1,)),
-        dma((2, sp_size - 1)), dma((2, sp_size - 1)),
+        dma((7,)), dma((6,)), dma, dma((2, 4)), dma((2, 4)), dma((2, 2)), dma((2, 2)), dma((2,)), dma((2,)),
+        dma((sp_size - 1, 3)), dma((sp_size - 1, 3)), dma, dma, dma, dma, dma((3,)), dma((3,)),
+        dma((sp_size - 1,)), dma((sp_size - 1,)), dma((2, sp_size - 1)), dma((2, sp_size - 1)),
     ]
     return pl.pallas_call(
         functools.partial(back_kernel, sp_size),
@@ -1260,10 +1246,10 @@
                    shape(small.shape, full)],
         in_specs=[hbm] * 7 + [vmem], out_specs=[hbm] * 4 + [vmem],
         scratch_shapes=scratch,
-        compiler_params=pltpu.CompilerParams(collective_id=1, has_side_effects=True, vmem_limit_bytes=67043328),
-        cost_estimate=pl.CostEstimate(flops=17 * 10 ** 9, bytes_accessed=200 * 1000 * 1000, transcendentals=0),
+        compiler_params=pltpu.CompilerParams(collective_id=1, has_side_effects=True, vmem_limit_bytes=62 << 20),
+        cost_estimate=pl.CostEstimate(flops=9 * 10 ** 9, bytes_accessed=200 * 1000 * 1000, transcendentals=0),
         name="reduce_gradients",
-    )(grad_out, grad_pre, mlp_in, attn_in, grad_proj, context, grad_hat, small)
+    )(grad_out, attn_in, grad_proj, context, grad_hat, hat_hop, up_sums, small)
 
 def gather_plain(dp_size, sp_size, qkv_weight, out_weight, up_weight, down_weight):
     head_width = D // sp_size
@@ -1364,11 +1350,7 @@
     gains = ln_gains.astype(full)
     shifts = ln_shifts.astype(full)
     row_valid = positions < length
-    if square:
-        qkv_own, out_own, up_own, seq_tokens, cos_rows, sin_rows = gather_weights(
-            dp_size, sp_size, qkv_weight, out_weight, up_weight, tokens
-        )
-    else:
+    if not square:
         cos_rows, sin_rows = rotary_rows(seq_rows)
         seq_tokens = lax.all_gather(tokens, "sp", axis=0, tiled=True)
         qkv_own, out_own, up_own, down_own = gather_plain(
@@ -1379,35 +1361,41 @@
     own_cotangent = jnp.where(own_valid[:, None], cotangent.astype(full), 0.0)
     if square:
         (
+            qkv_own,
+            out_own,
+            up_own,
             down_own,
+            seq_tokens,
             seq_cotangent,
             attn_in,
             mlp_in,
             hidden,
             pre_act,
             partial_out,
+            cos_rows,
+            sin_rows,
+            means,
+            inverses,
             queries,
             key_rows,
             values,
             context,
         ) = front(
             sp_size,
-            seq_tokens,
-            qkv_own,
-            up_own,
-            out_own,
+            dp_size,
+            lengths,
+            qkv_weight,
+            out_weight,
+            up_weight,
             down_weight,
+            tokens,
             cotangent,
-            gains,
-            shifts,
+            ln_gains,
+            ln_shifts,
             bias_own,
             unit_bias[None],
-            cos_rows,
-            sin_rows,
-            lengths,
-            dp_size,
         )
-        grad_down, grad_hat, grad_proj, grad_pre, grad_out, reduced_out, small = middle(
+        grad_down, up_sums, grad_hat, hat_hop, grad_proj, grad_out, reduced_out, small = middle(
             sp_size,
             dp_size,
             lengths,
@@ -1423,20 +1411,23 @@
             qkv_own,
             seq_tokens,
             partial_out,
-            gains,
+            mlp_in,
+            ln_gains,
             cos_rows,
             sin_rows,
+            means,
+            inverses,
         )
         grad_up, grad_qkv, grad_dense, reduced_hat, small = reduce_gradients(
             sp_size,
             qkv_rows,
             grad_out,
-            grad_pre,
-            mlp_in,
             attn_in,
             grad_proj,
             context,
             grad_hat,
+            hat_hop,
+            up_sums,
             small,
         )
         gain_total, shift_total, qkv_bias_total = small[:2], small[2:4], small[4:7]

time: 414 us -> 392 us (0.947); the launches traced: 407 us -> 391 us
  Pallas kernels: 386 us -> 373 us
    pallas_call x1 -> x0, Pallas kernels: 103 us -> none  [gather_weights(): pl.pallas_call(functools.partial(gather_kernel, sp_size), out_shape=[shap...]
    pallas_call x1, Pallas kernels: 78.3 us -> 173 us  [front(): pl.pallas_call(functools.partial(front_kernel, sp_size), out_shape=[shape...]
    pallas_call x1, Pallas kernels: 110 us -> 95.2 us  [reduce_gradients(): pl.pallas_call(functools.partial(back_kernel, sp_size), out_shape=[shape(...]
    pallas_call x1, Pallas kernels: 94.8 us -> 105 us  [middle(): pl.pallas_call(functools.partial(middle_kernel, sp_size), out_shape=[shap...]
where the time goes in v1:
time: 392 us; the launch traced here: 391 us
  Pallas kernels  373 us (95%)
  other arithmetic  12.5 us (3%)
  local copies, waits for them, and re-layouts  4.4 us (1%)
    pallas_call x1, Pallas kernels, front(): pl.pallas_call(functools.partial(front_kernel, sp_size), out_shape=[shape...  173 us
    pallas_call x1, Pallas kernels, middle(): pl.pallas_call(functools.partial(middle_kernel, sp_size), out_shape=[shap...  105 us
    pallas_call x1, Pallas kernels, reduce_gradients(): pl.pallas_call(functools.partial(back_kernel, sp_size), out_shape=[shape(...  95.2 us

profile of v1, /device:TPU:8, one launch (start us, length us, event | category | flops | bytes accessed | tf_op | source)
XLA Modules:
  0.0 391.4 jit_solution(900649835973465057)
XLA Ops:
  0.6 0.7 reshape.88
  1.4 0.6 convert.2.unit_bias_ref
  2.0 0.7 convert_bitcast_fusion
  2.7 0.6 copy.25
  4.0 0.6 maximum_bitcast_fusion.freq_ref
  4.6 173.4 %front.1 = (bf16[2048,1536]{1,0:T(8,128)(2,1)}, bf16[512,2048]{1,0:T(8,128)(2,1)}, bf16[2048,2048]{1,0:T(8,128)(2,1)}, bf16[2048,2048]{1,0:T(8,128)(2,1)}, bf16[...) custom-call(s32[1]{0:T(128)} %copy.27.len_ref, ...), custom_call_target="tpu_custom_call" | custom-call | flops 25999998976 | bytes 300000000 | tf_op jit(solution)/shard_map/front/pallas_call | solution.py:535
  177.9 104.5 %middle.1 = (bf16[256,2048]{1,0:T(8,128)(2,1)}, bf16[2,256,2048]{2,1,0:T(8,128)(2,1)}, bf16[1024,2048]{1,0:T(8,128)(2,1)}, bf16[2,256,2048]{2,1,0:T(8,128)(2,1)}...) custom-call(s32[1]{0:T(128)} %copy.27.len_ref, ...), custom_call_target="tpu_custom_call" | custom-call | flops 40000000000 | bytes 90000000 | tf_op jit(solution)/shard_map/middle/pallas_call | solution.py:1037
  282.5 0.0 copy-start
  282.5 95.2 %reduce_gradients.1 = (bf16[256,2048]{1,0:T(8,128)(2,1)}, bf16[64,6144]{1,0:T(8,128)(2,1)}, bf16[64,2048]{1,0:T(8,128)(2,1)}, bf16[256,2048]{1,0:T(8,128)(2,1)}, f32[16,2048]{1,0:T(8,128)}) custom-call(bf16[1024,2048]{1,0:T(8,128)(2,1)} %get-tuple-element.61.cot_hbm, bf16[1024,2048]{1,0:T(8,128)(2,1)} %get-tuple-element.62.attn_hbm, ...), custom_call_target="tpu_custom_call" | custom-call | flops 8999999488 | bytes 200000000 | tf_op jit(solution)/shard_map/reduce_gradients/pallas_call | solution.py:1243
  377.7 0.0 copy-start.1
  377.7 0.0 copy-done
  377.7 0.0 copy-start.7
  377.7 0.2 convert_reduce_fusion.1
  377.9 0.4 fusion.7
  378.4 0.5 copy-done.1
  378.9 0.7 convert_reduce_fusion
  379.6 0.0 copy-done.7
  379.6 0.0 copy-start.3
  379.7 4.0 %fusion.6 = (bf16[256,2048]{1,0:T(8,128)(2,1)}, bf16[256,2048]{1,0:T(8,128)(2,1)}) fusion(bf16[256,2048]{1,0:T(8,128)(2,1)S(1)} %copy-done, bf16[256,2048]{1,0:T(8,128)(2,1)S(1)} %copy-done.1, bf16[256,2048]{1,0:T(8,128)(2,1)} %cot_ref.1, f32[256]{0:T(256)S(1)} %get-tuple-element.81, f32[256]{0:T(256)S(1)} %get-tuple-element.82, f32[256]{0:T(256)S(1)} %add_rsqrt_fusion, ...), kind=kLoop, calls=%fused_computation.12 | loop fusion | flops 8388608 | bytes 6304000 | tf_op jit(solution)/shard_map/convert_element_type | solution.py:1519
  383.6 0.0 copy-start.4
  383.6 0.0 copy-done.3
  383.6 0.0 copy-start.5
  383.6 1.6 convert_element_type.66
  385.2 0.0 copy-start.6
  385.2 0.0 copy-start.2
  385.2 0.0 copy-done.4
  385.2 1.2 convert_element_type.64
  386.5 0.0 copy-done.5
  386.5 0.8 convert_element_type.65
  387.3 0.0 copy-done.6
  387.3 0.6 copy.26
  387.9 0.6 fusion.11
  388.6 0.6 slice.17
  389.2 0.6 slice.19
  389.8 0.0 copy-done.2
  389.8 1.6 convert_element_type.67
  (9 shorter events, 0.1 us)
Async XLA Ops:
  282.5 95.2 %copy-start = (bf16[256,2048]{1,0:T(8,128)(2,1)S(1)}, bf16[256,2048]{1,0:T(8,128)(2,1)}, u32[]{:S(2)}) copy-start(bf16[256,2048]{1,0:T(8,128)(2,1)} %tok_ref.1) | copy-start | bytes 3145732
  377.7 1.2 copy-start.1
  377.7 1.9 copy-start.7
  379.6 4.0 %copy-start.3 = (bf16[256,2048]{1,0:T(8,128)(2,1)S(1)}, bf16[256,2048]{1,0:T(8,128)(2,1)}, u32[]{:S(2)}) copy-start(bf16[256,2048]{1,0:T(8,128)(2,1)} %get-tuple-element.73) | copy-start | bytes 3145732
  383.6 1.6 copy-start.4
  383.6 2.8 copy-start.5
  385.2 2.1 copy-start.6
  385.2 4.6 %copy-start.2 = (bf16[256,2048]{1,0:T(8,128)(2,1)S(1)}, bf16[256,2048]{1,0:T(8,128)(2,1)}, u32[]{:S(2)}) copy-start(bf16[256,2048]{1,0:T(8,128)(2,1)} %get-tuple-element.74) | copy-start | bytes 3145732

commit v2 on v1

--- a/solution.py
+++ b/solution.py
@@ -198,13 +198,16 @@
                     self.copy(way, step, self.owner(way, step), step == 0).wait_send()
 
 
+NEAR = 2
+
+
 def front_kernel(sp_size, len_ref, qkv_ref, out_ref, up_ref, down_ref, tok_ref, cot_ref, freq_ref, gain_ref, shift_ref,
                  qkv_bias_ref, unit_bias_ref,
-                 qkv_all, out_all, up_all, down_all, tok_all, cot_all, attn_out, mlp_out, hidden_out, pre_out, part_out,
-                 cos_ref, sin_ref, mean_ref, inv_ref, q_ref, k_ref, v_ref, ctx_ref,
-                 tok, attn, mlp, qkv_w, up_w, hidden, pre,
+                 qkv_all, out_all, up_all, down_all, tok_all, cot_all, attn_out, mlp_out, hidden_out, pre_out, part_out, part_in, gpre_out,
+                 cos_ref, sin_ref, mean_ref, inv_ref, unit_ref, q_ref, k_ref, v_ref, ctx_ref,
+                 tok, attn, mlp, qkv_w, up_w, hidden, pre, cot, gpre,
                  send_sem, recv_sem, slab_send, slab_recv, keep_sem, turn_send, turn_recv, tok_send, tok_recv, cot_send, cot_recv,
-                 load_sem, store_sem, pre_sem, part_sem):
+                 load_sem, store_sem, pre_sem, part_sem, hop_send, hop_recv, slope_sem, gpre_sem):
     full, low = jnp.float32, jnp.bfloat16
     dp, sp = lax.axis_index("dp"), lax.axis_index("sp")
     first, second, diagonal, flip = square_partners(dp)
@@ -478,12 +481,24 @@
     for c in late:
         c.wait()
 
+    bands = seq // band
+    upper = 2 * sp // sp_size
+
+    def band_rows(r):
+        return pl.ds(pl.multiple_of(((1 - upper) * (bands - 1 - r) + upper * r) * band, band), band)
+
     def part_store(r):
-        at = pl.ds(pl.multiple_of(r * band, band), band)
-        return pltpu.make_async_copy(mlp.at[at], part_out.at[at], part_sem.at[r])
+        return pltpu.make_async_copy(mlp.at[band_rows(r)], part_out.at[band_rows(r)], part_sem.at[r])
+
+    def part_hop(way):
+        to = lax.rem(sp + (1 if way == 0 else sp_size - 1), sp_size)
+        return remote_copy(mlp.at[band_rows(0)], part_in.at[way], hop_send.at[way], hop_recv.at[way], (dp, to))
+
+    def along(way):
+        return sp if way == 0 else sp_size - 1 - sp
 
     def out_band(r, carry):
-        at = pl.ds(pl.multiple_of(r * band, band), band)
+        at = band_rows(r)
 
         def out_columns(c, carry):
             to = pl.ds(pl.multiple_of(c * band, band), band)
@@ -495,7 +510,80 @@
         lax.fori_loop(0, wide // band, out_columns, 0)
         part_store(r).start()
         return carry
-    lax.fori_loop(0, seq // band, out_band, 0)
+    out_band(0, 0)
+    for way in (0, 1):
+        @pl.when(along(way) == 0)
+        def _():
+            part_hop(way).start()
+    lax.fori_loop(1, bands, out_band, 0)
+
+    for step in (1, 2):
+        cotangents.settle(step)
+    unit_ref[...] = jnp.zeros_like(unit_ref)
+    early = NEAR
+
+    def near_rows(n):
+        return pl.ds(pl.multiple_of((upper * (bands - NEAR) + n) * band, band), band)
+
+    def slope_room(block):
+        return pre.at[block // 4, pl.ds(pl.multiple_of(lax.rem(block, 4) * band, band), band)]
+
+    def slope_load(n, block):
+        return pltpu.make_async_copy(
+            pre_out.at[near_rows(n), pl.ds(pl.multiple_of(block * units, units), units)], slope_room(block), slope_sem.at[block])
+
+    def cot_load(n):
+        return pltpu.make_async_copy(cot_all.at[near_rows(n)], cot.at[lax.rem(n, 2)], gpre_sem.at[2 + lax.rem(n, 2)])
+
+    def gpre_store(n):
+        return pltpu.make_async_copy(gpre.at[lax.rem(n, 2)], gpre_out.at[near_rows(n)], gpre_sem.at[lax.rem(n, 2)])
+
+    def first_loads(block, carry):
+        slope_load(0, block).start()
+        return carry
+    lax.fori_loop(0, blocks, first_loads, 0)
+    cot_load(0).start()
+
+    def near_band(n, carry):
+        slot = lax.rem(n, 2)
+        cot_load(n).wait()
+
+        @pl.when(n + 1 < early)
+        def _():
+            cot_load(n + 1).start()
+
+        def mask(i, carry):
+            at = pl.ds(pl.multiple_of(i * 32, 32), 32)
+            row = (upper * (bands - NEAR) + n) * band + i * 32 + lax.broadcasted_iota(jnp.int32, (32, wide), 0)
+            cot[slot, at, :] = jnp.where(row < len_ref[0], cot[slot, at, :].astype(full), 0.0).astype(low)
+            return carry
+        lax.fori_loop(0, band // 32, mask, 0)
+
+        @pl.when(n >= 2)
+        def _():
+            gpre_store(n - 2).wait()
+
+        for side, room in enumerate((tok, attn)):
+            def unit_part(k, carry):
+                block = side * (blocks // 2) + k
+                slope_load(n, block).wait()
+                of = pl.ds(pl.multiple_of(block * units, units), units)
+                value = lax.dot_general(cot[slot], room[pl.ds(pl.multiple_of(k * units, units), units), :],
+                                        (((1,), (1,)), ((), ())), preferred_element_type=full)
+                value = (value * gelu_slope(slope_room(block)[...])).astype(low)
+                gpre[slot, :, of] = value
+                unit_ref[:, of] += jnp.sum(value.astype(full), axis=0, keepdims=True)
+
+                @pl.when(n + 1 < early)
+                def _():
+                    slope_load(n + 1, block).start()
+                return carry
+            lax.fori_loop(0, blocks // 2, unit_part, 0)
+        gpre_store(n).start()
+        return carry
+    lax.fori_loop(0, early, near_band, 0)
+    for n in range(max(early - 2, 0), early):
+        gpre_store(n).wait()
     for r in range(seq // band):
         part_store(r).wait()
     hidden_store.wait()
@@ -511,9 +599,16 @@
         turn_copy(turn_dp).wait_send()
 
     tokens.finish()
-    for step in (1, 2, 3):
-        cotangents.settle(step)
+    cotangents.settle(3)
     cotangents.finish()
+    for way in (0, 1):
+        @pl.when(along(way) == 0)
+        def _():
+            part_hop(way).wait_send()
+
+        @pl.when(along(way) == 1)
+        def _():
+            part_hop(way).wait_recv()
 
 
 def front(sp_size, dp_size, lengths, qkv_weight, out_weight, up_weight, down_weight, tokens, cotangent, gains, shifts, qkv_bias,
@@ -537,16 +632,17 @@
         out_shape=[shape(qkv_shape, low), shape((rows * dp_size, wide), low), shape((all_units, wide), low),
                    shape((all_units, wide), low), shape((seq, wide), low), shape((seq, wide), low),
                    shape((seq, wide), low), shape((seq, wide), low), shape((seq, all_units), low), shape((seq, all_units), full),
-                   shape((seq, wide), low)]
-        + [shape((seq, 128), full)] * 4 + [shape((seq, width), low)] * 4,
+                   shape((seq, wide), low), shape((2, seq // sp_size, wide), low), shape((seq, all_units), low)]
+        + [shape((seq, 128), full)] * 4 + [shape((1, all_units), full)] + [shape((seq, width), low)] * 4,
         in_specs=[pl.BlockSpec(memory_space=pltpu.SMEM)] + [vmem] * 11,
-        out_specs=[hbm] * 11 + [vmem] * 8,
+        out_specs=[hbm] * 13 + [vmem] * 9,
         scratch_shapes=[pltpu.VMEM((seq, wide), low)] * 3 + [
             pltpu.VMEM(qkv_shape, low), pltpu.VMEM((all_units, wide), low),
             pltpu.VMEM((seq, all_units), low), pltpu.VMEM((2, seq, units), full),
+            pltpu.VMEM((2, 256, wide), low), pltpu.VMEM((2, 256, all_units), low),
             dma((4, 7)), dma((4, 7)), dma((sp_size - 1, 3)), dma((sp_size - 1, 3)), dma((8,)), dma, dma,
             dma((2, sp_size)), dma((2, sp_size)), dma((2, sp_size)), dma((2, sp_size)),
-            dma((4,)), dma((2,)), dma((2,)), dma((seq // 256,))],
+            dma((4,)), dma((2,)), dma((2,)), dma((seq // 256,)), dma((2,)), dma((2,)), dma((all_units // units,)), dma((4,))],
         compiler_params=pltpu.CompilerParams(collective_id=0, has_side_effects=True, vmem_limit_bytes=62 << 20),
         cost_estimate=pl.CostEstimate(flops=26 * 10 ** 9, bytes_accessed=300 * 1000 * 1000, transcendentals=0),
         name="front",
@@ -618,7 +714,7 @@
 
     def sib_copy(self, slot):
         p = self.place
-        return remote(p.lent.at[slot, :, :self.width], self.sib.at[p.chip_of(3 - slot)],
+        return remote(p.lent.at[slot, :, :self.width], self.sib.at[p.chip_of(3 - slot), :, :self.width],
                       p.sib_send.at[self.index, slot], p.sib_recv.at[self.index, slot], (p.sibling, p.sp))
 
     def for_sibling(self, previous):
@@ -660,27 +756,33 @@
         lax.fori_loop(0, 2, stay, 0)
 
     def block(self, mask):
-        return self.sums.at[mask]
+        return self.sums.at[mask, :, :self.width]
+
+    def from_first(self, slot):
+        return self.one.at[slot, :, :self.width]
+
+    def from_second(self):
+        return self.two.at[:, :self.width]
 
     def first_copy(self, slot):
         p = self.place
-        return remote(self.block(3 - slot * (1 + p.core)), self.one.at[slot], p.one_send.at[self.index, slot],
+        return remote(self.block(3 - slot * (1 + p.core)), self.from_first(slot), p.one_send.at[self.index, slot],
                       p.one_recv.at[self.index, slot], (p.first, p.sp))
 
     def second_copy(self):
         p = self.place
-        return remote(self.block(p.second_mask), self.two, p.two_send.at[self.index],
+        return remote(self.block(p.second_mask), self.from_second(), p.two_send.at[self.index],
                       p.two_recv.at[self.index], (p.second, p.sp))
 
     def onward(self):
         self.first_copy(0).wait_recv()
-        add_into(self.block(self.place.second_mask), self.one.at[0])
+        add_into(self.block(self.place.second_mask), self.from_first(0))
         self.second_copy().start()
 
     def finish(self):
         self.first_copy(1).wait_recv()
         self.second_copy().wait_recv()
-        add_into(self.block(0), self.one.at[1], self.two)
+        add_into(self.block(0), self.from_first(1), self.from_second())
 
     def drain(self):
         for slot in (0, 1):
@@ -788,12 +890,12 @@
 
 
 def middle_kernel(sp_size, len_ref, cot_hbm, out_hbm, q_hbm, k_hbm, v_hbm, pre_hbm, hidden_hbm, down_hbm, up_hbm, qkv_hbm,
-                  tok_hbm, part_hbm, mlp_hbm, gain_ref, cos_ref, sin_ref, mean_s, inv_s,
-                  down_out, up_out, hat_out, hat_in, proj_out, gout_out, red_out, small_ref,
-                  cot, left, gpre, up_w, qkv_w, pre, gctx, gproj, dq, dk, dv,
+                  tok_hbm, part_hbm, hop_hbm, near_hbm, attn_hbm, unit_ref, gain_ref, cos_ref, sin_ref, mean_s, inv_s,
+                  down_out, slab_out, gpre_out, hat_out, hat_in, proj_out, gout_out, red_out, small_ref,
+                  cot, left, tok, gpre, up_w, qkv_w, pre, gctx, gproj, dq, dk, dv,
                   lent, down_sum, down_sib, down_one, down_two, inbox, stage,
                   load_sem, stream_sem, store_sem, stage_sem, sib_send, sib_recv, one_send, one_recv, two_send, two_recv,
-                  fold_send, fold_recv, hat_send, hat_recv, sib_free, one_free):
+                  fold_send, fold_recv, hat_send, hat_recv, sib_free, one_free, two_free, near_sem, tok_sem):
     full, low = jnp.float32, jnp.bfloat16
     place = Square(sp_size, lent, sib_send, sib_recv, one_send, one_recv, two_send, two_recv)
     seq, wide = cot.shape
@@ -811,28 +913,44 @@
         c.start()
         return c
 
-    early = [load(cot_hbm, cot, 0), load(hidden_hbm, left, 1), load(out_hbm, up_w.at[pl.ds(0, out_rows)], 2)]
-    for i, source in enumerate((q_hbm, k_hbm, v_hbm)):
-        early.append(load(source, qkv_w.at[pl.ds(0, seq), pl.ds(i * width, width)], 3 + i))
+    early = [load(cot_hbm, cot, 0), load(hidden_hbm, left, 1)]
 
     def down_load(block, slot):
         return pltpu.make_async_copy(
             down_hbm.at[pl.ds(pl.multiple_of(block * units, units), units)],
             up_w.at[pl.ds(pl.multiple_of(out_rows + slot * units, units), units)], stream_sem.at[0, slot])
 
+    upper = 2 * place.sp // sp_size
+
+    def hat_rows(r):
+        return pl.ds(pl.multiple_of(((1 - upper) * (bands - 1 - r) + upper * r) * band, band), band)
+
+    far = bands - NEAR
+    near = pl.ds(pl.multiple_of(upper * far * band, band), NEAR * band)
+    far_rows = pl.ds(pl.multiple_of((1 - upper) * NEAR * band, band), far * band)
+    near_load = pltpu.make_async_copy(near_hbm.at[near], gpre.at[near], near_sem)
+
     def pre_load(block, slot):
         return pltpu.make_async_copy(
-            pre_hbm.at[:, pl.ds(pl.multiple_of(block * units, units), units)], pre.at[slot], stream_sem.at[1, slot])
-
+            pre_hbm.at[far_rows, pl.ds(pl.multiple_of(block * units, units), units)], pre.at[slot], stream_sem.at[1, slot])
+
+    hops = []
+    for way in (0, 1):
+        hops.append(load(hop_hbm.at[way], inbox.at[way, 0], 6 + way))
+
+    barrier = pltpu.get_barrier_semaphore()
+    place.greet(barrier)
+    pl.semaphore_wait(barrier, 2 + sp_size)
+    fold = Fold(place, part_hbm, inbox, stage, stage_sem, fold_send, fold_recv, begun=2)
+    for way in (0, 1):
+        hops[way].wait()
+    fold.step(2)
+    early.append(load(out_hbm, up_w.at[pl.ds(0, out_rows)], 2))
+    for i, source in enumerate((q_hbm, k_hbm, v_hbm)):
+        early.append(load(source, qkv_w.at[pl.ds(0, seq), pl.ds(i * width, width)], 3 + i))
     for slot in (0, 1):
         down_load(slot, slot).start()
         pre_load(slot, slot).start()
-
-    barrier = pltpu.get_barrier_semaphore()
-    place.greet(barrier)
-    pl.semaphore_wait(barrier, 2 + sp_size)
-    fold = Fold(place, part_hbm, inbox, stage, stage_sem, fold_send, fold_recv)
-    fold.step(1)
     small_ref[...] = jnp.zeros_like(small_ref)
     gain_row, shift_row, bias_row, unit_row = 0, 2, 4, 7
     per_row = wide // (sp_size * units)
@@ -857,6 +975,7 @@
     down = Wide(place, 0, left, cot, wide, down_sum, down_sib, down_one, down_two)
     early[1].wait()
     down.for_sibling(None)
+    down.for_self()
     early[2].wait()
 
     def context_band(r, carry):
@@ -865,10 +984,11 @@
             cot[at, :], up_w[:out_rows, :], (((1,), (1,)), ((), ())), preferred_element_type=full).astype(low)
         return carry
     lax.fori_loop(0, bands, context_band, 0)
-    down.for_self()
-    mlp_load = load(mlp_hbm, left, 1)
+    attn_load = load(attn_hbm, left, 1)
+    near_load.start()
+    late_rows = pl.ds(out_rows + 2 * units, up_w.shape[0] - out_rows - 2 * units)
+    up_load = load(up_hbm.at[late_rows], up_w.at[late_rows], 8)
     pl.semaphore_signal(sib_free, inc=1, device_id=(place.sibling, place.sp), device_id_type=MESH)
-    fold.step(2)
     for c in early[3:]:
         c.wait()
 
@@ -917,15 +1037,15 @@
         of = pl.ds(pl.multiple_of(block * units, units), units)
         room = pl.ds(pl.multiple_of(out_rows + slot * units, units), units)
 
-        def row_band(r, total):
-            at = pl.ds(pl.multiple_of(r * band, band), band)
+        def far_band(r, total):
+            at = pl.ds(pl.multiple_of(((1 - upper) * NEAR + r) * band, band), band)
             value = lax.dot_general(cot[at, :], up_w[room, :], (((1,), (1,)), ((), ())), preferred_element_type=full)
-            value = (value * gelu_slope(pre[slot, at, :])).astype(low)
+            value = (value * gelu_slope(pre[slot, pl.ds(pl.multiple_of(r * band, band), band), :])).astype(low)
             gpre[at, of] = value
             return total + jnp.sum(value.astype(full), axis=0, keepdims=True)
-        total = lax.fori_loop(0, bands, row_band, jnp.zeros((1, units), full))
         small_ref[pl.ds(unit_row + block // per_row, 1),
-                  pl.ds(pl.multiple_of((lax.rem(block, per_row) * sp_size + place.sp) * units, units), units)] = total
+                  pl.ds(pl.multiple_of((lax.rem(block, per_row) * sp_size + place.sp) * units, units), units)] = (
+            lax.fori_loop(0, far, far_band, unit_ref[:, of]))
 
         @pl.when(block + 2 < blocks)
         def _():
@@ -934,33 +1054,19 @@
         return carry
 
     down.onward()
-    lax.fori_loop(0, 3 * blocks // 4, unit_block, 0)
     fold.step(3)
-    lax.fori_loop(3 * blocks // 4, blocks, unit_block, 0)
-    up_load = load(up_hbm, up_w, 0)
-    down.finish()
-    stores.append(pltpu.make_async_copy(down.block(0), down_out, store_sem.at[3 + bands]))
-    stores[2].start()
-    pl.semaphore_signal(one_free, inc=1, device_id=(place.first, place.sp), device_id_type=MESH)
-    up = Wide(place, 1, gpre, left, wide, down_sum, down_sib, down_one, down_two)
-    mlp_load.wait()
-    pl.semaphore_wait(sib_free, 1)
-    up.for_sibling(down)
-    down.drain()
-    stores[2].wait()
-    pl.semaphore_wait(one_free, 1)
-    up.for_self()
-    tok_load = load(tok_hbm, left, 1)
-    tok_load.wait()
+    lax.fori_loop(0, blocks, unit_block, 0)
+    used = out_rows + 2 * units
+    up_loads = [load(up_hbm.at[pl.ds(0, used)], up_w.at[pl.ds(0, used)], 0), up_load]
+
+    def tok_load(r):
+        return pltpu.make_async_copy(tok_hbm.at[hat_rows(r)], tok.at[r % 2], tok_sem.at[r % 2])
+    tok_load(0).start()
+    tok_load(1).start()
+    near_load.wait()
+    gpre_store = pltpu.make_async_copy(gpre, gpre_out, store_sem.at[2])
+    gpre_store.start()
     stores[0].wait()
-    qkv_load.wait()
-    up_load.wait()
-
-    upper = 2 * place.sp // sp_size
-
-    def hat_rows(r):
-        return pl.ds(pl.multiple_of(((1 - upper) * (bands - 1 - r) + upper * r) * band, band), band)
-
     def hat_store(r):
         return pltpu.make_async_copy(cot.at[hat_rows(r)], hat_out.at[hat_rows(r)], store_sem.at[3 + r])
 
@@ -968,14 +1074,15 @@
         to = lax.rem(place.sp + (1 if way == 0 else sp_size - 1), sp_size)
         return remote(cot.at[hat_rows(0)], hat_in.at[way], hat_send.at[way], hat_recv.at[way], (place.dp, to))
 
-    def hat_band(r, carry):
+    def hat_band(r):
         at = hat_rows(r)
+        tok_load(r).wait()
 
         def columns(c, carry):
             to = pl.ds(pl.multiple_of(c * band, band), band)
             from_mlp = jnp.dot(gpre[at, :], up_w[:, to], preferred_element_type=full)
             from_attn = lax.dot_general(gproj[at, :], qkv_w[to, :], (((1,), (1,)), ((), ())), preferred_element_type=full)
-            normed = (left[at, to].astype(full) - mean_s[at, 0:1]) * inv_s[at, 0:1]
+            normed = (tok[r % 2, :, to].astype(full) - mean_s[at, 0:1]) * inv_s[at, 0:1]
             small_ref[gain_row:gain_row + 1, to] += jnp.sum(from_attn * normed, axis=0, keepdims=True)
             small_ref[gain_row + 1:gain_row + 2, to] += jnp.sum(from_mlp * normed, axis=0, keepdims=True)
             small_ref[shift_row:shift_row + 1, to] += jnp.sum(from_attn, axis=0, keepdims=True)
@@ -984,30 +1091,49 @@
             return carry
         lax.fori_loop(0, wide // band, columns, 0)
         hat_store(r).start()
-        return carry
-
-    hat_band(0, 0)
+        if r + 2 < bands:
+            tok_load(r + 2).start()
+
+    qkv = Wide(place, 1, left, gproj, 3 * width, down_sum, down_sib, down_one, down_two)
+    attn_load.wait()
+    pl.semaphore_wait(sib_free, 1)
+    qkv.for_sibling(down)
+    qkv_load.wait()
+    for c in up_loads:
+        c.wait()
+    hat_band(0)
     for way in (0, 1):
         @pl.when(fold.along(way) == 0)
         def _():
             hat_hop(way).start()
-    lax.fori_loop(1, bands, hat_band, 0)
+    down.finish()
+    stores.append(pltpu.make_async_copy(down.block(0), down_out, store_sem.at[3 + bands]))
+    stores[2].start()
+    pl.semaphore_signal(one_free, inc=1, device_id=(place.first, place.sp), device_id_type=MESH)
+    pl.semaphore_signal(two_free, inc=1, device_id=(place.second, place.sp), device_id_type=MESH)
+    down.drain()
+    stores[2].wait()
+    pl.semaphore_wait(one_free, 1)
+    qkv.for_self()
+    for r in range(1, bands - 1):
+        hat_band(r)
+    pl.semaphore_wait(two_free, 1)
+    qkv.onward()
+    hat_band(bands - 1)
     fold.finish()
     stores.append(pltpu.make_async_copy(stage, red_out, store_sem.at[4 + bands]))
     stores[-1].start()
-    for slot, mask in enumerate((place.second_mask, 0)):
-        up.first_copy(slot).wait_recv()
-        add_into(up.block(mask), up.one.at[slot])
-        stores.append(pltpu.make_async_copy(up.block(mask), up_out.at[slot], store_sem.at[5 + bands + slot]))
-        stores[-1].start()
+    qkv.finish()
+    stores.append(pltpu.make_async_copy(qkv.block(0), slab_out, store_sem.at[5 + bands]))
+    stores[-1].start()
     for r in range(bands):
         hat_store(r).wait()
-    for which in (1, 3, 4, 5):
+    for which in (1, 3, 4):
         stores[which].wait()
+    gpre_store.wait()
     for slot in range(4):
-        up.sib_copy(slot).wait_send()
-    for slot in (0, 1):
-        up.first_copy(slot).wait_send()
+        qkv.sib_copy(slot).wait_send()
+    qkv.drain()
     fold.drain()
     for way in (0, 1):
         @pl.when(fold.along(way) == 0)
@@ -1020,7 +1146,7 @@
 
 
 def middle(sp_size, dp_size, lengths, cotangent, out_own, queries, key_rows, values, pre_act, hidden, down_own, up_own, qkv_own,
-           tokens, partial_out, mlp_in, gains, cos_t, sin_t, means, inverses):
+           tokens, partial_out, part_hop, near_pre, attn_in, unit_sums, gains, cos_t, sin_t, means, inverses):
     seq, wide = tokens.shape
     width = queries.shape[1]
     units = up_own.shape[0] // dp_size
@@ -1036,40 +1162,42 @@
     bands = seq // 256
     return pl.pallas_call(
         functools.partial(middle_kernel, sp_size),
-        out_shape=[shape((units, wide), low), shape((2, units, wide), low), shape((seq, wide), low), shape((2, own, wide), low),
+        out_shape=[shape((units, wide), low), shape((units, 3 * width), low), shape(hidden.shape, low), shape((seq, wide), low),
+                   shape((2, own, wide), low),
                    shape((seq, 3 * width), low),
                    shape((seq, wide), low), shape((own, wide), low), shape((16, wide), full)],
-        in_specs=[pl.BlockSpec(memory_space=pltpu.SMEM)] + [hbm] * 13 + [vmem] * 5,
-        out_specs=[hbm] * 7 + [vmem],
+        in_specs=[pl.BlockSpec(memory_space=pltpu.SMEM)] + [hbm] * 15 + [vmem] * 6,
+        out_specs=[hbm] * 8 + [vmem],
         scratch_shapes=[
-            v(seq, wide), v(seq, wide), v(*hidden.shape), v(*up_own.shape), v(*qkv_own.shape), v(2, seq, units, kind=full),
+            v(seq, wide), v(seq, wide), v(2, 256, wide), v(*hidden.shape), v(*up_own.shape), v(*qkv_own.shape),
+            v(2, (seq // 256 - NEAR) * 256, units, kind=full),
             v(seq, width), v(seq, 3 * width), v(seq, HEAD, kind=full), v(seq, HEAD, kind=full), v(seq, HEAD, kind=full),
             v(4, units, wide), v(4, units, wide), v(4, units, wide), v(2, units, wide), v(units, wide),
             v(2, sp_size - 1, own, wide), v(own, wide),
-            dma((6,)), dma((2, 2)), dma((7 + bands,)), dma, dma((2, 4)), dma((2, 4)), dma((2, 2)), dma((2, 2)), dma((2,)), dma((2,)),
+            dma((9,)), dma((2, 2)), dma((7 + bands,)), dma, dma((2, 4)), dma((2, 4)), dma((2, 2)), dma((2, 2)), dma((2,)), dma((2,)),
             dma((2, sp_size - 1)), dma((2, sp_size - 1)), dma((2,)), dma((2,)),
-            pltpu.SemaphoreType.REGULAR, pltpu.SemaphoreType.REGULAR],
+            pltpu.SemaphoreType.REGULAR, pltpu.SemaphoreType.REGULAR, pltpu.SemaphoreType.REGULAR, dma, dma((2,))],
         compiler_params=pltpu.CompilerParams(collective_id=3, has_side_effects=True, vmem_limit_bytes=67043328),
         cost_estimate=pl.CostEstimate(flops=40 * 10 ** 9, bytes_accessed=90 * 1000 * 1000, transcendentals=0),
         name="middle",
     )(lengths, cotangent, out_own, queries, key_rows, values, pre_act, hidden, down_own, up_own, qkv_own, tokens, partial_out,
-      mlp_in, gains, cos_t, sin_t, means, inverses)
-
-
-def back_kernel(sp_size, cot_hbm, attn_hbm, proj_hbm, ctx_hbm, hat_hbm, hop_hbm, up_hbm, small_ref,
+      part_hop, near_pre, attn_in, unit_sums, gains, cos_t, sin_t, means, inverses)
+
+
+def back_kernel(sp_size, cot_hbm, pre_hbm, mlp_hbm, ctx_hbm, hat_hbm, hop_hbm, slab_hbm, small_ref,
                 up_out, qkv_out, dense_out, red_out, small_out,
                 left, right, cot, ctx, lent,
-                qkv_sum, dense_sum, qkv_sib, dense_sib, qkv_one, dense_one, qkv_two, dense_two,
-                dense_part, up_room, up_two, small_acc, small_in, small_z, inbox, stage,
+                up_sum, dense_sum, up_sib, dense_sib, up_one, dense_one, up_two, dense_two,
+                dense_part, slab, small_acc, small_in, small_z, small_fin, inbox, stage,
                 load_sem, store_sem, stage_sem, sib_send, sib_recv, one_send, one_recv, two_send, two_recv,
-                slab_send, slab_recv, turn_send, turn_recv, up_send, up_recv, small_send, small_recv, z_send, z_recv,
-                fold_send, fold_recv):
+                slab_send, slab_recv, turn_send, turn_recv, small_send, small_recv, z_send, z_recv,
+                fold_send, fold_recv, plane_send, plane_recv):
     place = Square(sp_size, lent, sib_send, sib_recv, one_send, one_recv, two_send, two_recv)
     dp, sp = place.dp, place.sp
     per = 2
     pair, lane = dp // per, dp % per
     turn_dp = sp * per + lane
-    slab_width = qkv_sum.shape[2]
+    slab_width = slab.shape[1]
     head_width = slab_width // 3
     rows = dense_one.shape[1]
     wide = left.shape[1]
@@ -1079,18 +1207,21 @@
         c.start()
         return c
 
-    up_load = load(up_hbm, up_room, 0)
+    slab_load = load(slab_hbm, slab, 0)
     hops = [load(hop_hbm.at[way], inbox.at[way, 0], 1 + way) for way in (0, 1)]
-    loads = [load(ctx_hbm, ctx, 3), load(cot_hbm, cot, 4), load(attn_hbm, left, 5), load(proj_hbm, right, 6)]
+    loads = [load(ctx_hbm, ctx, 3), load(cot_hbm, cot, 4)]
 
     barrier = pltpu.get_barrier_semaphore()
-    place.greet(barrier)
+    for step in range(1, 8):
+        pl.semaphore_signal(barrier, inc=1, device_id=(lax.rem(dp + step, 8), sp), device_id_type=MESH)
+    for step in range(1, sp_size):
+        pl.semaphore_signal(barrier, inc=1, device_id=(dp, lax.rem(sp + step, sp_size)), device_id_type=MESH)
 
     @pl.when(pair != sp)
     def _():
         pl.semaphore_signal(barrier, inc=1, device_id=(turn_dp, pair), device_id_type=MESH)
 
-    pl.semaphore_wait(barrier, 2 + sp_size + jnp.where(pair != sp, 1, 0))
+    pl.semaphore_wait(barrier, 6 + sp_size + jnp.where(pair != sp, 1, 0))
     fold = Fold(place, hat_hbm, inbox, stage, stage_sem, fold_send, fold_recv, begun=2)
 
     def small_copy(stage_of):
@@ -1103,16 +1234,23 @@
         before = small_ref[...] if stage_of == 0 else small_acc[stage_of - 1]
         small_acc[stage_of] = before + small_in[stage_of]
 
+    share = small_ref.shape[1] // 8
+
+    def columns_of(owner):
+        return pl.ds(pl.multiple_of(owner * share, share), share)
+
     def z_copy(step):
-        return remote(small_acc.at[2], small_z.at[sp], z_send.at[step - 1], z_recv.at[step - 1],
+        return remote(small_acc.at[2, :, columns_of(dp)], small_z.at[sp], z_send.at[step - 1], z_recv.at[step - 1],
                       (dp, lax.rem(sp + step, sp_size)))
 
     def z_arrival(step):
         origin = lax.rem(sp + sp_size - step, sp_size)
-        return remote(small_acc.at[2], small_z.at[origin], z_send.at[step - 1], z_recv.at[step - 1], (dp, origin))
-
-    def up_copy():
-        return remote(up_room.at[0], up_two, up_send, up_recv, (place.second, sp))
+        return remote(small_acc.at[2, :, columns_of(dp)], small_z.at[origin], z_send.at[step - 1], z_recv.at[step - 1],
+                      (dp, origin))
+
+    def plane_copy(step, owner, target):
+        at = small_fin.at[:, columns_of(owner)]
+        return remote(at, at, plane_send.at[step - 1], plane_recv.at[step - 1], (target, sp))
 
     def turn_copy():
         return remote(dense.block(0), dense_out, turn_send, turn_recv, (turn_dp, pair))
@@ -1124,7 +1262,7 @@
         return pl.ds(pl.multiple_of(part * wide + owner * head_width, head_width), head_width)
 
     def slab_copy(step, part, origin, there):
-        return remote(qkv_sum.at[0, slab_rows(there), pl.ds(part * head_width, head_width)],
+        return remote(slab.at[slab_rows(there), pl.ds(part * head_width, head_width)],
                       qkv_out.at[:, slab_columns(part, origin)],
                       slab_send.at[step - 1, part], slab_recv.at[step - 1, part], (dp, there))
 
@@ -1136,13 +1274,18 @@
         stores.append(c)
 
     small_copy(0).start()
-    up_load.wait()
-    up_copy().start()
     dense = Dense(place, 0, ctx, cot, wide, dense_sum, dense_sib, dense_one, dense_two, dense_part)
-    qkv = Wide(place, 1, left, right, slab_width, qkv_sum, qkv_sib, qkv_one, qkv_two)
+    up = Wide(place, 1, left, right, wide, up_sum, up_sib, up_one, up_two)
     for way in (0, 1):
         hops[way].wait()
     fold.step(2)
+    slab_load.wait()
+    for step in range(1, sp_size):
+        for part in range(3):
+            slab_copy(step, part, sp, lax.rem(sp + step, sp_size)).start()
+    for part in range(3):
+        store(slab.at[slab_rows(sp), pl.ds(part * head_width, head_width)], qkv_out.at[:, slab_columns(part, sp)])
+    loads += [load(pre_hbm, left, 5), load(mlp_hbm, right, 6)]
     small_step(0)
     small_copy(1).start()
     loads[0].wait()
@@ -1150,18 +1293,18 @@
     dense.for_sibling(None)
     loads[2].wait()
     loads[3].wait()
-    qkv.for_sibling(None)
+    up.for_sibling(None)
     small_step(1)
     small_copy(2).start()
     dense.for_self()
-    qkv.for_self()
+    up.for_self()
     small_step(2)
     for step in range(1, sp_size):
         z_copy(step).start()
-    small_z[sp] = small_acc[2]
+    small_z[sp] = small_acc[2, :, columns_of(dp)]
+    dense.onward()
     fold.step(3)
-    dense.onward()
-    qkv.onward()
+    up.onward()
     dense.finish()
 
     @pl.when(pair != sp)
@@ -1174,29 +1317,23 @@
         c.start()
         c.wait()
 
-    qkv.finish()
-    for step in range(1, sp_size):
-        for part in range(3):
-            slab_copy(step, part, sp, lax.rem(sp + step, sp_size)).start()
-    for part in range(3):
-        store(qkv_sum.at[0, slab_rows(sp), pl.ds(part * head_width, head_width)], qkv_out.at[:, slab_columns(part, sp)])
-    up_copy().wait_recv()
-    add_into(up_room.at[1], up_two)
-    store(up_room.at[1], up_out)
     for step in range(1, sp_size):
         z_arrival(step).wait_recv()
     total = small_z[0]
     for origin in range(1, sp_size):
         total = total + small_z[origin]
-    small_out[...] = total
+    small_fin[:, columns_of(dp)] = total
+    for step in range(1, 8):
+        plane_copy(step, dp, lax.rem(dp + step, 8)).start()
+    up.finish()
+    store(up.block(0), up_out)
     fold.finish()
     store(stage, red_out)
     for slot in range(4):
-        qkv.sib_copy(slot).wait_send()
+        up.sib_copy(slot).wait_send()
     dense.sib_copy(0).wait_send()
-    for array in (dense, qkv):
+    for array in (dense, up):
         array.drain()
-    up_copy().wait_send()
     for stage_of in range(3):
         small_copy(stage_of).wait_send()
     fold.drain()
@@ -1211,15 +1348,19 @@
         turn_copy().wait_recv()
         turn_copy().wait_send()
 
+    for step in range(1, 8):
+        origin = lax.rem(dp + 8 - step, 8)
+        plane_copy(step, origin, origin).wait_recv()
+        plane_copy(step, dp, origin).wait_send()
+    small_out[...] = small_fin[...]
     for c in stores:
         c.wait()
 
 
-def reduce_gradients(sp_size, rows, grad_out, attn_in, grad_proj, context, grad_hat, hat_hop, up_sums, small):
-    seq, wide = attn_in.shape
-    slab_width = grad_proj.shape[1]
-    units = up_sums.shape[1]
-    slab = 4 * rows
+def reduce_gradients(sp_size, rows, grad_out, grad_pre, mlp_in, context, grad_hat, hat_hop, slab_sum, small):
+    seq, wide = mlp_in.shape
+    slab, slab_width = slab_sum.shape
+    units = slab
     own = seq // sp_size
     full, low = jnp.float32, jnp.bfloat16
     hbm = pl.BlockSpec(memory_space=pltpu.HBM)
@@ -1230,15 +1371,15 @@
     def v(*dims, kind=low):
         return pltpu.VMEM(dims, kind)
     scratch = [
-        v(seq, wide), v(seq, slab_width), v(seq, wide), v(seq, context.shape[1]), v(4, slab, slab_width),
-        v(4, slab, slab_width), v(slab, wide), v(4, slab, slab_width), v(slab, wide),
-        v(2, slab, slab_width), v(2, rows, wide), v(slab, slab_width), v(rows, wide),
-        v(slab, wide), v(2, units, wide), v(units, wide),
-        v(3, *small.shape, kind=full), v(3, *small.shape, kind=full), v(sp_size, *small.shape, kind=full),
+        v(seq, wide), v(seq, wide), v(seq, wide), v(seq, context.shape[1]), v(4, units, wide),
+        v(4, units, wide), v(slab, wide), v(4, units, wide), v(slab, wide),
+        v(2, units, wide), v(2, rows, wide), v(units, wide), v(rows, wide),
+        v(slab, wide), v(slab, slab_width),
+        v(3, *small.shape, kind=full), v(3, *small.shape, kind=full), v(sp_size, small.shape[0], small.shape[1] // 8, kind=full), v(*small.shape, kind=full),
         v(2, sp_size - 1, own, wide), v(own, wide),
         dma((7,)), dma((6,)), dma, dma((2, 4)), dma((2, 4)), dma((2, 2)), dma((2, 2)), dma((2,)), dma((2,)),
-        dma((sp_size - 1, 3)), dma((sp_size - 1, 3)), dma, dma, dma, dma, dma((3,)), dma((3,)),
-        dma((sp_size - 1,)), dma((sp_size - 1,)), dma((2, sp_size - 1)), dma((2, sp_size - 1)),
+        dma((sp_size - 1, 3)), dma((sp_size - 1, 3)), dma, dma, dma((3,)), dma((3,)),
+        dma((sp_size - 1,)), dma((sp_size - 1,)), dma((2, sp_size - 1)), dma((2, sp_size - 1)), dma((7,)), dma((7,)),
     ]
     return pl.pallas_call(
         functools.partial(back_kernel, sp_size),
@@ -1249,7 +1390,65 @@
         compiler_params=pltpu.CompilerParams(collective_id=1, has_side_effects=True, vmem_limit_bytes=62 << 20),
         cost_estimate=pl.CostEstimate(flops=9 * 10 ** 9, bytes_accessed=200 * 1000 * 1000, transcendentals=0),
         name="reduce_gradients",
-    )(grad_out, attn_in, grad_proj, context, grad_hat, hat_hop, up_sums, small)
+    )(grad_out, grad_pre, mlp_in, context, grad_hat, hat_hop, slab_sum, small)
+
+def finish_kernel(len_ref, tok_ref, cot_ref, sum_ref, hat_ref, down_ref, up_ref, qkv_ref, dense_ref, bias_ref, small_ref,
+                  out_ref, input_ref, gain_out, shift_out, qkv_out, qkv_bias_out, dense_out, up_out, unit_out, down_out, bias_out):
+    full = jnp.float32
+    part = pl.program_id(0)
+    rows, wide = tok_ref.shape
+    tokens = tok_ref[...].astype(full)
+    out_ref[...] = (tokens + sum_ref[...].astype(full) + bias_ref[...].astype(full)).astype(out_ref.dtype)
+    centered = tokens - jnp.mean(tokens, axis=-1, keepdims=True)
+    inverse = lax.rsqrt(jnp.mean(centered * centered, axis=-1, keepdims=True) + eps)
+    normed = centered * inverse
+    hat = hat_ref[...].astype(full)
+    grad = inverse * (
+        hat - jnp.mean(hat, axis=-1, keepdims=True) - normed * jnp.mean(hat * normed, axis=-1, keepdims=True))
+    position = (lax.axis_index("sp") * pl.num_programs(0) + part) * rows + lax.broadcasted_iota(jnp.int32, (rows, wide), 0)
+    own = jnp.where(position < len_ref[0], cot_ref[...].astype(full), 0.0)
+    input_ref[...] = (own + grad).astype(input_ref.dtype)
+    down_out[...] = down_ref[...].astype(full)
+    up_out[...] = up_ref[...].astype(full)
+    qkv_out[...] = qkv_ref[...].astype(full)
+    dense_out[...] = dense_ref[...].astype(full)
+
+    @pl.when(part == 0)
+    def _():
+        gain_out[...] = small_ref[0:2, :]
+        shift_out[...] = small_ref[2:4, :]
+        qkv_bias_out[...] = small_ref[4:7, :]
+        unit_rows = unit_out.shape[1] // wide
+        for row in range(unit_rows):
+            unit_out[:, row * wide:(row + 1) * wide] = small_ref[7 + row:8 + row, :]
+        bias_out[...] = small_ref[7 + unit_rows:8 + unit_rows, :]
+
+
+def finish(lengths, tokens, cotangent, reduced_out, reduced_hat, grad_down, grad_up, grad_qkv, grad_dense, out_bias, small, all_units):
+    own, wide = tokens.shape
+    steps = 4
+    full = jnp.float32
+    shape = jax.ShapeDtypeStruct
+
+    def rows(x):
+        return pl.BlockSpec((x.shape[0] // steps, x.shape[1]), lambda i: (i, 0))
+
+    def whole(*dims):
+        return pl.BlockSpec(dims, lambda i: (0, 0))
+    out_row = out_bias[None]
+    return pl.pallas_call(
+        finish_kernel,
+        grid=(steps,),
+        out_shape=[shape(tokens.shape, tokens.dtype), shape(tokens.shape, tokens.dtype), shape((2, wide), full),
+                   shape((2, wide), full), shape(grad_qkv.shape, full), shape((3, wide), full), shape(grad_dense.shape, full),
+                   shape(grad_up.shape, full), shape((1, all_units), full), shape(grad_down.shape, full), shape((1, wide), full)],
+        in_specs=[pl.BlockSpec(memory_space=pltpu.SMEM)]
+        + [rows(x) for x in (tokens, cotangent, reduced_out, reduced_hat, grad_down, grad_up, grad_qkv, grad_dense)]
+        + [whole(1, wide), whole(*small.shape)],
+        out_specs=[rows(tokens), rows(tokens), whole(2, wide), whole(2, wide), rows(grad_qkv), whole(3, wide), rows(grad_dense),
+                   rows(grad_up), whole(1, all_units), rows(grad_down), whole(1, wide)],
+        name="finish",
+    )(lengths, tokens, cotangent, reduced_out, reduced_hat, grad_down, grad_up, grad_qkv, grad_dense, out_row, small)
 
 def gather_plain(dp_size, sp_size, qkv_weight, out_weight, up_weight, down_weight):
     head_width = D // sp_size
@@ -1357,8 +1556,6 @@
             dp_size, sp_size, qkv_weight, out_weight, up_weight, down_weight
         )
         seq_cotangent = lax.all_gather(cotangent, "sp", axis=0, tiled=True)
-    own_valid = shard * own_rows + jnp.arange(own_rows, dtype=jnp.int32) < length
-    own_cotangent = jnp.where(own_valid[:, None], cotangent.astype(full), 0.0)
     if square:
         (
             qkv_own,
@@ -1372,10 +1569,13 @@
             hidden,
             pre_act,
             partial_out,
+            part_hop,
+            near_pre,
             cos_rows,
             sin_rows,
             means,
             inverses,
+            unit_sums,
             queries,
             key_rows,
             values,
@@ -1395,7 +1595,7 @@
             bias_own,
             unit_bias[None],
         )
-        grad_down, up_sums, grad_hat, hat_hop, grad_proj, grad_out, reduced_out, small = middle(
+        grad_down, slab_sum, grad_pre, grad_hat, hat_hop, _, grad_out, reduced_out, small = middle(
             sp_size,
             dp_size,
             lengths,
@@ -1411,7 +1611,10 @@
             qkv_own,
             seq_tokens,
             partial_out,
-            mlp_in,
+            part_hop,
+            near_pre,
+            attn_in,
+            unit_sums,
             ln_gains,
             cos_rows,
             sin_rows,
@@ -1422,18 +1625,42 @@
             sp_size,
             qkv_rows,
             grad_out,
-            attn_in,
-            grad_proj,
+            grad_pre,
+            mlp_in,
             context,
             grad_hat,
             hat_hop,
-            up_sums,
+            slab_sum,
             small,
         )
-        gain_total, shift_total, qkv_bias_total = small[:2], small[2:4], small[4:7]
-        unit_rows = up_bias.shape[0] // D
-        unit_total = small[7 : 7 + unit_rows].reshape(-1)
-        out_bias_total = small[7 + unit_rows]
+        (
+            output,
+            input_grad,
+            gain_total,
+            shift_total,
+            grad_qkv,
+            qkv_bias_total,
+            grad_dense,
+            grad_up,
+            unit_total,
+            grad_down,
+            out_bias_total,
+        ) = finish(
+            lengths,
+            tokens,
+            cotangent,
+            reduced_out,
+            reduced_hat,
+            grad_down,
+            grad_up,
+            grad_qkv,
+            grad_dense,
+            out_bias,
+            small,
+            up_bias.shape[0],
+        )
+        unit_total = unit_total.reshape(-1)
+        out_bias_total = out_bias_total.reshape(-1)
     else:
         inputs = seq_tokens.astype(full)
         centre = jnp.mean(inputs, axis=-1, keepdims=True)
@@ -1485,6 +1712,8 @@
             [jnp.sum(grad_attn_in * normed, axis=0), jnp.sum(grad_mlp_in * normed, axis=0)]
         )
         shift_grad = jnp.stack([jnp.sum(grad_attn_in, axis=0), jnp.sum(grad_mlp_in, axis=0)])
+        own_valid = shard * own_rows + jnp.arange(own_rows, dtype=jnp.int32) < length
+        own_cotangent = jnp.where(own_valid[:, None], cotangent.astype(full), 0.0)
         out_bias_part = jnp.sum(own_cotangent, axis=0)
         grad_down, grad_up, grad_qkv, grad_dense = reduce_plain(
             dp_size,
@@ -1503,31 +1732,34 @@
         )
 
 
-    output = (
-        tokens.astype(full) + reduced_out.astype(full) + out_bias.astype(full)
-    ).astype(low)
-
-    reduced_hat = reduced_hat.astype(full)
-    own_centered = tokens.astype(full) - jnp.mean(tokens.astype(full), axis=-1, keepdims=True)
-    own_inverse = lax.rsqrt(jnp.mean(own_centered * own_centered, axis=-1, keepdims=True) + eps)
-    own_normed = own_centered * own_inverse
-    grad_input = own_inverse * (
-        reduced_hat
-        - jnp.mean(reduced_hat, axis=-1, keepdims=True)
-        - own_normed * jnp.mean(reduced_hat * own_normed, axis=-1, keepdims=True)
-    )
-    input_grad = (own_cotangent + grad_input).astype(low)
+        output = (
+            tokens.astype(full) + reduced_out.astype(full) + out_bias.astype(full)
+        ).astype(low)
+
+        reduced_hat = reduced_hat.astype(full)
+        own_centered = tokens.astype(full) - jnp.mean(tokens.astype(full), axis=-1, keepdims=True)
+        own_inverse = lax.rsqrt(jnp.mean(own_centered * own_centered, axis=-1, keepdims=True) + eps)
+        own_normed = own_centered * own_inverse
+        grad_input = own_inverse * (
+            reduced_hat
+            - jnp.mean(reduced_hat, axis=-1, keepdims=True)
+            - own_normed * jnp.mean(reduced_hat * own_normed, axis=-1, keepdims=True)
+        )
+        input_grad = (own_cotangent + grad_input).astype(low)
+        grad_qkv, grad_dense = grad_qkv.astype(full), grad_dense.astype(full)
+        grad_up, grad_down = grad_up.astype(full), grad_down.astype(full)
+
     return (
         output,
         input_grad,
         gain_total,
         shift_total,
-        grad_qkv.astype(full),
+        grad_qkv,
         qkv_bias_total,
-        grad_dense.astype(full),
-        grad_up.astype(full),
+        grad_dense,
+        grad_up,
         unit_total,
-        grad_down.astype(full),
+        grad_down,
         out_bias_total,
     )
 

time: 392 us -> 369 us (0.941)
  Pallas kernels: 373 us -> 360 us
  other arithmetic: 12.5 us -> 1.9 us
    pallas_call x1, Pallas kernels: 95.2 us -> 83.7 us  [reduce_gradients(): pl.pallas_call(functools.partial(back_kernel, sp_size), out_shape=[shape(...]
    pallas_call x1, Pallas kernels: 105 us -> 95.1 us  [middle(): pl.pallas_call(functools.partial(middle_kernel, sp_size), out_shape=[shap...]
    convert_element_type x6 -> x0, other arithmetic: 9.19 us -> none  [the longest x1 3.99 us: body(): input_grad = (own_cotangent + grad_input).astype(low)]
    pallas_call x0 -> x1, Pallas kernels: none -> 8.07 us  [finish(): pl.pallas_call(finish_kernel, grid=(steps,), out_shape=[shape(tokens.shap...]
where the time goes in v2:
time: 369 us; the launch traced here: 366 us
  Pallas kernels  360 us (98%)
    pallas_call x1, Pallas kernels, front(): pl.pallas_call(functools.partial(front_kernel, sp_size), out_shape=[shape...  173 us
    pallas_call x1, Pallas kernels, middle(): pl.pallas_call(functools.partial(middle_kernel, sp_size), out_shape=[shap...  95.1 us
    pallas_call x1, Pallas kernels, reduce_gradients(): pl.pallas_call(functools.partial(back_kernel, sp_size), out_shape=[shape(...  83.7 us
    pallas_call x1, Pallas kernels, finish(): pl.pallas_call(finish_kernel, grid=(steps,), out_shape=[shape(tokens.shap...  8.07 us

profile of v2, /device:TPU:8, one launch (start us, length us, event | category | flops | bytes accessed | tf_op | source)
XLA Modules:
  0.0 365.7 jit_solution(12090020604191469183)
XLA Ops:
  0.6 0.7 reshape.65
  1.4 0.6 convert.2.unit_bias_ref
  2.0 0.7 convert_bitcast_fusion
  2.7 0.6 copy.25
  4.0 0.6 maximum_bitcast_fusion.freq_ref
  4.6 173.5 %front.1 = (bf16[2048,1536]{1,0:T(8,128)(2,1)}, bf16[512,2048]{1,0:T(8,128)(2,1)}, bf16[2048,2048]{1,0:T(8,128)(2,1)}, bf16[2048,2048]{1,0:T(8,128)(2,1)}, bf16[...) custom-call(s32[1]{0:T(128)S(6)} %copy.26.len_ref, ...), custom_call_target="tpu_custom_call" | custom-call | flops 25999998976 | bytes 300000000 | tf_op jit(solution)/shard_map/front/pallas_call | solution.py:630
  178.0 95.1 %middle.1 = (bf16[256,2048]{1,0:T(8,128)(2,1)}, bf16[256,1536]{1,0:T(8,128)(2,1)}, bf16[1024,2048]{1,0:T(8,128)(2,1)}, bf16[1024,2048]{1,0:T(8,128)(2,1)}, bf16[...) custom-call(s32[1]{0:T(128)S(6)} %copy.26.len_ref, ...), custom_call_target="tpu_custom_call" | custom-call | flops 40000000000 | bytes 90000000 | tf_op jit(solution)/shard_map/middle/pallas_call | solution.py:1163
  273.1 0.0 copy-start
  273.1 83.7 %reduce_gradients.1 = (bf16[256,2048]{1,0:T(8,128)(2,1)}, bf16[64,6144]{1,0:T(8,128)(2,1)}, bf16[64,2048]{1,0:T(8,128)(2,1)}, bf16[256,2048]{1,0:T(8,128)(2,1)}, f32[16,2048]{1,0:T(8,128)}) custom-call(bf16[1024,2048]{1,0:T(8,128)(2,1)} %get-tuple-element.78.cot_hbm, bf16[1024,2048]{1,0:T(8,128)(2,1)} %get-tuple-element.79.pre_hbm, ...), custom_call_target="tpu_custom_call" | custom-call | flops 8999999488 | bytes 200000000 | tf_op jit(solution)/shard_map/reduce_gradients/pallas_call | solution.py:1384
  356.8 0.0 copy-done
  356.8 0.6 broadcast_in_dim.12.bias_ref
  357.4 8.1 %finish.1 = (bf16[256,2048]{1,0:T(8,128)(2,1)}, bf16[256,2048]{1,0:T(8,128)(2,1)}, f32[2,2048]{1,0:T(2,128)}, f32[2,2048]{1,0:T(2,128)}, f32[64,6144]{1,0:T(8,12...) custom-call(s32[1]{0:T(128)S(6)} %copy.26.len_ref, ...), custom_call_target="tpu_custom_call" | custom-call | tf_op jit(solution)/shard_map/finish/pallas_call | solution.py:1439
  (3 shorter events, 0.0 us)
Async XLA Ops:
  273.1 83.7 %copy-start = (bf16[2048]{0:T(1024)(128)(2,1)S(1)}, bf16[2048]{0:T(1024)(128)(2,1)}, u32[]{:S(2)}) copy-start(bf16[2048]{0:T(1024)(128)(2,1)} %param.23) | copy-start | bytes 12292

commit v3 on v2

--- a/solution.py
+++ b/solution.py
@@ -422,7 +422,9 @@
             cos_t, sin_t = cos_ref[at, :], sin_ref[at, :]
             for part, target in enumerate((q_ref, k_ref, v_ref)):
                 cols = pl.ds(pl.multiple_of(part * width + h * HEAD, HEAD), HEAD)
-                value = jnp.dot(attn[at, :], qkv_w[:, cols], preferred_element_type=full) + qkv_bias_ref[:, cols]
+                bias_cols = pl.ds(pl.multiple_of(sp * width + h * HEAD, HEAD), HEAD)
+                value = jnp.dot(attn[at, :], qkv_w[:, cols], preferred_element_type=full)
+                value = value + qkv_bias_ref[part:part + 1, bias_cols].astype(full)
                 if part < 2:
                     value = turn(value, cos_t, sin_t)
                 target[at, lanes] = value.astype(low)
@@ -451,11 +453,12 @@
             pre_store(block - 2, slot).wait()
 
         of = pl.ds(pl.multiple_of(block * units, units), units)
+        bias_of = pl.ds(pl.multiple_of((block * sp_size + sp) * units, units), units)
 
         def row_band(r, carry):
             at = pl.ds(pl.multiple_of(r * band, band), band)
             value = lax.dot_general(mlp[at, :], up_w[of, :], (((1,), (1,)), ((), ())), preferred_element_type=full)
-            value = value + unit_bias_ref[:, of]
+            value = value + unit_bias_ref[:, bias_of].astype(full)
             pre[slot, at, :] = value
             hidden[at, of] = gelu_value(value).astype(low)
             return carry
@@ -1115,11 +1118,11 @@
     stores[2].wait()
     pl.semaphore_wait(one_free, 1)
     qkv.for_self()
-    for r in range(1, bands - 1):
-        hat_band(r)
+    hat_band(1)
     pl.semaphore_wait(two_free, 1)
     qkv.onward()
-    hat_band(bands - 1)
+    for r in range(2, bands):
+        hat_band(r)
     fold.finish()
     stores.append(pltpu.make_async_copy(stage, red_out, store_sem.at[4 + bands]))
     stores[-1].start()
@@ -1291,20 +1294,18 @@
     loads[0].wait()
     loads[1].wait()
     dense.for_sibling(None)
+    dense.for_self()
     loads[2].wait()
     loads[3].wait()
     up.for_sibling(None)
     small_step(1)
     small_copy(2).start()
-    dense.for_self()
+    dense.onward()
     up.for_self()
     small_step(2)
     for step in range(1, sp_size):
         z_copy(step).start()
     small_z[sp] = small_acc[2, :, columns_of(dp)]
-    dense.onward()
-    fold.step(3)
-    up.onward()
     dense.finish()
 
     @pl.when(pair != sp)
@@ -1317,6 +1318,8 @@
         c.start()
         c.wait()
 
+    fold.step(3)
+    up.onward()
     for step in range(1, sp_size):
         z_arrival(step).wait_recv()
     total = small_z[0]
@@ -1431,7 +1434,8 @@
     shape = jax.ShapeDtypeStruct
 
     def rows(x):
-        return pl.BlockSpec((x.shape[0] // steps, x.shape[1]), lambda i: (i, 0))
+        shared = 1 if x.shape[0] // steps >= 16 else 2
+        return pl.BlockSpec((x.shape[0] * shared // steps, x.shape[1]), lambda i: (i // shared, 0))
 
     def whole(*dims):
         return pl.BlockSpec(dims, lambda i: (0, 0))
@@ -1531,25 +1535,25 @@
     qkv_rows = qkv_weight.shape[0]
     units = up_weight.shape[0]
     square = dp_size == 8 and sp_size == 4
-    unit_bias = (
-        lax.dynamic_index_in_dim(
-            up_bias.reshape(dp_size, sp_size, units), shard, 1, keepdims=False
-        )
-        .reshape(dp_size * units)
-        .astype(full)
-    )
-    bias_own = (
-        lax.dynamic_index_in_dim(
-            qkv_bias.reshape(3, sp_size, head_width), shard, 1, keepdims=False
-        )
-        .reshape(1, 3 * head_width)
-        .astype(full)
-    )
     positions = jnp.arange(seq_rows, dtype=jnp.int32)
     gains = ln_gains.astype(full)
     shifts = ln_shifts.astype(full)
     row_valid = positions < length
     if not square:
+        unit_bias = (
+            lax.dynamic_index_in_dim(
+                up_bias.reshape(dp_size, sp_size, units), shard, 1, keepdims=False
+            )
+            .reshape(dp_size * units)
+            .astype(full)
+        )
+        bias_own = (
+            lax.dynamic_index_in_dim(
+                qkv_bias.reshape(3, sp_size, head_width), shard, 1, keepdims=False
+            )
+            .reshape(1, 3 * head_width)
+            .astype(full)
+        )
         cos_rows, sin_rows = rotary_rows(seq_rows)
         seq_tokens = lax.all_gather(tokens, "sp", axis=0, tiled=True)
         qkv_own, out_own, up_own, down_own = gather_plain(
@@ -1592,8 +1596,8 @@
             cotangent,
             ln_gains,
             ln_shifts,
-            bias_own,
-            unit_bias[None],
+            qkv_bias,
+            up_bias[None],
         )
         grad_down, slab_sum, grad_pre, grad_hat, hat_hop, _, grad_out, reduced_out, small = middle(
             sp_size,

time: 369 us -> 367 us (level)
  no operation moved by 1% of the time
where the time goes in v3:
time: 367 us; the launch traced here: 366 us
  Pallas kernels  362 us (99%)
    pallas_call x1, Pallas kernels, front(): pl.pallas_call(functools.partial(front_kernel, sp_size), out_shape=[shape...  173 us
    pallas_call x1, Pallas kernels, middle(): pl.pallas_call(functools.partial(middle_kernel, sp_size), out_shape=[shap...  95.6 us
    pallas_call x1, Pallas kernels, reduce_gradients(): pl.pallas_call(functools.partial(back_kernel, sp_size), out_shape=[shape(...  85.1 us
    pallas_call x1, Pallas kernels, finish(): pl.pallas_call(finish_kernel, grid=(steps,), out_shape=[shape(tokens.shap...  8.07 us

profile of v3, /device:TPU:8, one launch (start us, length us, event | category | flops | bytes accessed | tf_op | source)
XLA Modules:
  0.0 366.3 jit_solution(11932668680818674278)
XLA Ops:
  1.3 1.4 broadcast_in_dim.14.unit_bias_ref
  2.7 0.6 maximum_bitcast_fusion.freq_ref
  3.2 173.5 %front.1 = (bf16[2048,1536]{1,0:T(8,128)(2,1)}, bf16[512,2048]{1,0:T(8,128)(2,1)}, bf16[2048,2048]{1,0:T(8,128)(2,1)}, bf16[2048,2048]{1,0:T(8,128)(2,1)}, bf16[...) custom-call(s32[1]{0:T(128)S(6)} %copy.23.len_ref, ...), custom_call_target="tpu_custom_call" | custom-call | flops 25999998976 | bytes 300000000 | tf_op jit(solution)/shard_map/front/pallas_call | solution.py:633
  176.7 95.6 %middle.1 = (bf16[256,2048]{1,0:T(8,128)(2,1)}, bf16[256,1536]{1,0:T(8,128)(2,1)}, bf16[1024,2048]{1,0:T(8,128)(2,1)}, bf16[1024,2048]{1,0:T(8,128)(2,1)}, bf16[...) custom-call(s32[1]{0:T(128)S(6)} %copy.23.len_ref, ...), custom_call_target="tpu_custom_call" | custom-call | flops 40000000000 | bytes 90000000 | tf_op jit(solution)/shard_map/middle/pallas_call | solution.py:1166
  272.3 0.0 copy-start
  272.3 85.1 %reduce_gradients.1 = (bf16[256,2048]{1,0:T(8,128)(2,1)}, bf16[64,6144]{1,0:T(8,128)(2,1)}, bf16[64,2048]{1,0:T(8,128)(2,1)}, bf16[256,2048]{1,0:T(8,128)(2,1)}, f32[16,2048]{1,0:T(8,128)}) custom-call(bf16[1024,2048]{1,0:T(8,128)(2,1)} %get-tuple-element.78.cot_hbm, bf16[1024,2048]{1,0:T(8,128)(2,1)} %get-tuple-element.79.pre_hbm, ...), custom_call_target="tpu_custom_call" | custom-call | flops 8999999488 | bytes 200000000 | tf_op jit(solution)/shard_map/reduce_gradients/pallas_call | solution.py:1387
  357.5 0.0 copy-done
  357.5 0.6 broadcast_in_dim.15.bias_ref
  358.1 8.1 %finish.1 = (bf16[256,2048]{1,0:T(8,128)(2,1)}, bf16[256,2048]{1,0:T(8,128)(2,1)}, f32[2,2048]{1,0:T(2,128)}, f32[2,2048]{1,0:T(2,128)}, f32[64,6144]{1,0:T(8,12...) custom-call(s32[1]{0:T(128)S(6)} %copy.23.len_ref, ...), custom_call_target="tpu_custom_call" | custom-call | tf_op jit(solution)/shard_map/finish/pallas_call | solution.py:1443
  (2 shorter events, 0.0 us)
Async XLA Ops:
  272.3 85.2 %copy-start = (bf16[2048]{0:T(1024)(128)(2,1)S(1)}, bf16[2048]{0:T(1024)(128)(2,1)}, u32[]{:S(2)}) copy-start(bf16[2048]{0:T(1024)(128)(2,1)} %param.23) | copy-start | bytes 12292

commit v4 on v3

--- a/solution.py
+++ b/solution.py
@@ -1429,7 +1429,7 @@
 
 def finish(lengths, tokens, cotangent, reduced_out, reduced_hat, grad_down, grad_up, grad_qkv, grad_dense, out_bias, small, all_units):
     own, wide = tokens.shape
-    steps = 4
+    steps = 2
     full = jnp.float32
     shape = jax.ShapeDtypeStruct
 

time: 367 us -> 366 us (level)
  no operation moved by 1% of the time
where the time goes in v4:
time: 366 us
  Pallas kernels  362 us (99%)
    pallas_call x1, Pallas kernels, front(): pl.pallas_call(functools.partial(front_kernel, sp_size), out_shape=[shape...  173 us
    pallas_call x1, Pallas kernels, middle(): pl.pallas_call(functools.partial(middle_kernel, sp_size), out_shape=[shap...  95.6 us
    pallas_call x1, Pallas kernels, reduce_gradients(): pl.pallas_call(functools.partial(back_kernel, sp_size), out_shape=[shape(...  85.1 us
    pallas_call x1, Pallas kernels, finish(): pl.pallas_call(finish_kernel, grid=(steps,), out_shape=[shape(tokens.shap...  7.45 us

profile of v4, /device:TPU:8, one launch (start us, length us, event | category | flops | bytes accessed | tf_op | source)
XLA Modules:
  0.0 365.7 jit_solution(12663924116513066784)
XLA Ops:
  1.3 1.4 broadcast_in_dim.14.unit_bias_ref
  2.7 0.6 maximum_bitcast_fusion.freq_ref
  3.2 173.5 %front.1 = (bf16[2048,1536]{1,0:T(8,128)(2,1)}, bf16[512,2048]{1,0:T(8,128)(2,1)}, bf16[2048,2048]{1,0:T(8,128)(2,1)}, bf16[2048,2048]{1,0:T(8,128)(2,1)}, bf16[...) custom-call(s32[1]{0:T(128)S(6)} %copy.23.len_ref, ...), custom_call_target="tpu_custom_call" | custom-call | flops 25999998976 | bytes 300000000 | tf_op jit(solution)/shard_map/front/pallas_call | solution.py:633
  176.7 95.6 %middle.1 = (bf16[256,2048]{1,0:T(8,128)(2,1)}, bf16[256,1536]{1,0:T(8,128)(2,1)}, bf16[1024,2048]{1,0:T(8,128)(2,1)}, bf16[1024,2048]{1,0:T(8,128)(2,1)}, bf16[...) custom-call(s32[1]{0:T(128)S(6)} %copy.23.len_ref, ...), custom_call_target="tpu_custom_call" | custom-call | flops 40000000000 | bytes 90000000 | tf_op jit(solution)/shard_map/middle/pallas_call | solution.py:1166
  272.3 0.0 copy-start
  272.3 85.1 %reduce_gradients.1 = (bf16[256,2048]{1,0:T(8,128)(2,1)}, bf16[64,6144]{1,0:T(8,128)(2,1)}, bf16[64,2048]{1,0:T(8,128)(2,1)}, bf16[256,2048]{1,0:T(8,128)(2,1)}, f32[16,2048]{1,0:T(8,128)}) custom-call(bf16[1024,2048]{1,0:T(8,128)(2,1)} %get-tuple-element.78.cot_hbm, bf16[1024,2048]{1,0:T(8,128)(2,1)} %get-tuple-element.79.pre_hbm, ...), custom_call_target="tpu_custom_call" | custom-call | flops 8999999488 | bytes 200000000 | tf_op jit(solution)/shard_map/reduce_gradients/pallas_call | solution.py:1387
  357.5 0.0 copy-done
  357.5 0.6 broadcast_in_dim.15.bias_ref
  358.1 7.4 %finish.1 = (bf16[256,2048]{1,0:T(8,128)(2,1)}, bf16[256,2048]{1,0:T(8,128)(2,1)}, f32[2,2048]{1,0:T(2,128)}, f32[2,2048]{1,0:T(2,128)}, f32[64,6144]{1,0:T(8,12...) custom-call(s32[1]{0:T(128)S(6)} %copy.23.len_ref, ...), custom_call_target="tpu_custom_call" | custom-call | tf_op jit(solution)/shard_map/finish/pallas_call | solution.py:1443
  (2 shorter events, 0.0 us)
Async XLA Ops:
  272.3 85.2 %copy-start = (bf16[2048]{0:T(1024)(128)(2,1)S(1)}, bf16[2048]{0:T(1024)(128)(2,1)}, u32[]{:S(2)}) copy-start(bf16[2048]{0:T(1024)(128)(2,1)} %param.23) | copy-start | bytes 12292
